TPU v7x, 32 devices: a whole 2x2x4 slice. The times are simulated.
32 devices in a mesh: rows: 8 (over y, x, core), cols: 4 (over z).
Axes of the slice: x: 2, y: 2, z: 4, core: 2. Of those that a mesh axis runs over, the one named last changes fastest.
Arguments:
- feats: bfloat16 [32768, 512], P('rows', 'cols'), may hold values from -6 to 6
- adj_vals: bfloat16 [256, 16, 128, 128], P('rows'), may hold values from -0.125 to 0.125
- colref: int32 [256, 16], P('rows'), may hold values from 0 to 47, as said below
- fetch_ids: int32 [8, 8, 2], P('rows'), may hold values from -1 to 31, as said below
- w_self: bfloat16 [512, 512], replicated, may hold values from -0.25 to 0.25
- w_neigh: bfloat16 [512, 512], replicated, may hold values from -0.25 to 0.25
- grad_out: bfloat16 [32768, 512], P(('rows', 'cols')), may hold values from -6 to 6
Outputs:
- act_out: bfloat16 [32768, 512], P(('rows', 'cols'))
- grad_self_w: float32 [512, 512], replicated
- grad_neigh_w: float32 [512, 512], replicated
- grad_feats: float32 [32768, 512], P('rows', 'cols')
Inputs may be any that keep to these rules, and one draw needn't show every extreme that they name: `fetch_ids`: entry [r, o, s] is a row tile index within partition o (0 to 31) that partition r reads, or -1 for an empty slot. The entries of one r and o are distinct, all slots with o = r are empty, and every r fills all 2 slots of at least one o. `colref`: entry [b, k], with r = b // 32, is below 32 for partition r's own row tile of that index, or 32 + o * 2 + s for the slot s of fetch_ids[r, o], never an empty slot; so it lies in 0 to 32 + 8 * 2 - 1. The 16 entries of a row tile are distinct and the first is b - r * 32, the row tile itself.
All inputs are finite; a program needn't handle non-finite values.
Results may differ from a plain program's by a relative error of at most 0.0057.
Values may be sent and summed in bfloat16 or wider, within the bound.
No kernel may reach another device: no remote copies, remote signals or barrier semaphores. Data moves between devices by JAX's collectives and lax.ppermute only.
A program may use at most 192 MiB of HBM per device.

v0:
```python
import math

import jax
import jax.numpy as jnp
from jax import lax
from jax.sharding import PartitionSpec as P


def body(feats, adj_vals, colref, fetch_ids, w_self, w_neigh, grad_out):
    node_rows, feat_cols = feats.shape
    blocks = adj_vals.shape[0]
    per_block = adj_vals.shape[1]
    tile_rows = adj_vals.shape[2]
    partitions = lax.axis_size("rows")
    capacity = fetch_ids.shape[2]
    total_nodes = node_rows * partitions
    own_tiles = feats.reshape(blocks, tile_rows * feat_cols)
    wanted = lax.all_to_all(fetch_ids, "rows", split_axis=1, concat_axis=0, tiled=True).reshape(
        partitions * capacity
    )
    choose = (wanted[:, None] == jnp.arange(blocks, dtype=jnp.int32)[None, :]).astype(jnp.bfloat16)
    outgoing = jnp.dot(choose, own_tiles, preferred_element_type=jnp.float32).astype(jnp.bfloat16)
    outgoing = outgoing.reshape(partitions, capacity, tile_rows, feat_cols)
    arrived = lax.all_to_all(outgoing, "rows", split_axis=0, concat_axis=0, tiled=True)
    tile_pool = jnp.concatenate(
        [
            feats.reshape(blocks, tile_rows, feat_cols),
            arrived.reshape(partitions * capacity, tile_rows, feat_cols),
        ],
        axis=0,
    )
    picked = jnp.take(tile_pool, colref, axis=0)
    aggregated = jnp.einsum("bkij,bkjf->bif", adj_vals, picked, preferred_element_type=jnp.float32)
    aggregated = aggregated.astype(jnp.bfloat16).reshape(node_rows, feat_cols)
    feat_rows, agg_rows = (
        lax.all_to_all(feats, "cols", split_axis=0, concat_axis=1, tiled=True),
        lax.all_to_all(aggregated, "cols", split_axis=0, concat_axis=1, tiled=True),
    )
    preact = jnp.dot(feat_rows, w_self, preferred_element_type=jnp.float32) + jnp.dot(
        agg_rows, w_neigh, preferred_element_type=jnp.float32
    )
    activation, pull_back = jax.vjp(jax.nn.gelu, preact)
    grad_pre = pull_back(grad_out.astype(jnp.float32))[0].astype(jnp.bfloat16)
    contract = (((0,), (0,)), ((), ()))
    weight_terms = (
        lax.dot_general(feat_rows, grad_pre, contract, preferred_element_type=jnp.float32),
        lax.dot_general(agg_rows, grad_pre, contract, preferred_element_type=jnp.float32),
    )
    self_sum, neigh_sum = lax.psum((weight_terms[0], weight_terms[1]), ("rows", "cols"))
    grad_scale = 1.0 / math.sqrt(total_nodes)
    grad_self_w = self_sum * grad_scale
    grad_neigh_w = neigh_sum * grad_scale
    dims_back = (((1,), (1,)), ((), ()))
    self_rows = lax.dot_general(
        grad_pre, w_self, dims_back, preferred_element_type=jnp.float32
    ).astype(jnp.bfloat16)
    agg_grad_rows = lax.dot_general(
        grad_pre, w_neigh, dims_back, preferred_element_type=jnp.float32
    ).astype(jnp.bfloat16)
    self_part, grad_agg = (
        lax.all_to_all(self_rows, "cols", split_axis=1, concat_axis=0, tiled=True),
        lax.all_to_all(agg_grad_rows, "cols", split_axis=1, concat_axis=0, tiled=True),
    )
    grad_blocks = grad_agg.reshape(blocks, tile_rows, feat_cols)
    per_ref = jnp.einsum(
        "bkij,bif->bkjf", adj_vals, grad_blocks, preferred_element_type=jnp.float32
    )
    pool_slots = blocks + partitions * capacity
    pick_table = (
        jnp.arange(pool_slots, dtype=jnp.int32)[:, None] == colref.reshape(1, blocks * per_block)
    ).astype(jnp.float32)
    pooled = jnp.dot(
        pick_table,
        per_ref.reshape(blocks * per_block, tile_rows * feat_cols),
        precision=lax.Precision.HIGHEST,
        preferred_element_type=jnp.float32,
    )
    shares = pooled.astype(jnp.bfloat16).reshape(pool_slots, tile_rows, feat_cols)
    remote_shares = shares[blocks:].reshape(partitions, capacity, tile_rows, feat_cols)
    returned = lax.all_to_all(remote_shares, "rows", split_axis=0, concat_axis=0, tiled=True)
    gathered_back = jnp.dot(
        choose.T,
        returned.reshape(partitions * capacity, tile_rows * feat_cols),
        preferred_element_type=jnp.float32,
    )
    grad_feats = self_part.astype(jnp.float32) + shares[:blocks].astype(jnp.float32).reshape(
        node_rows, feat_cols
    )
    grad_feats = grad_feats + gathered_back.reshape(node_rows, feat_cols)
    return (activation.astype(jnp.bfloat16), grad_self_w, grad_neigh_w, grad_feats)


def solution(mesh):
    in_specs = (
        P("rows", "cols"),
        P("rows", None, None, None),
        P("rows", None),
        P("rows", None, None),
        P(),
        P(),
        P(("rows", "cols"), None),
    )
    out_specs = (P(("rows", "cols"), None), P(), P(), P("rows", "cols"))
    return jax.shard_map(body, mesh=mesh, in_specs=in_specs, out_specs=out_specs, check_vma=False)
```

profile of v0, /device:TPU:0, one launch (start us, length us, event | category | flops | bytes accessed | tf_op | source)
XLA Modules:
  0.0 388.8 jit_solution(16417296102142203751)
XLA Ops:
  7.2 1.4 copy.44
  8.6 5.2 %all-to-all-start.1 = ((s32[1,8,2]{2,0,1:T(1,128)}), s32[1,8,2]{2,0,1:T(1,128)S(1)}, u32[]{:S(2)}, u32[]{:S(2)}) async-start(s32[1,8,2]{2,0,1:T(1,128)} %copy.44), calls=%async_computation.1 | async-start | bytes 8192 | tf_op jit(solution)/shard_map/all_to_all | solution.py:18
  13.8 1.5 reshape.73
  15.3 3.1 all-to-all-done.1
  18.4 0.5 broadcast.41
  18.9 0.7 reduce.3
  19.7 0.4 fusion.23
  20.0 0.9 copy.60
  20.9 3.5 all-to-all-start.2
  24.6 0.1 copy.43
  24.7 9.4 %all-to-all-done.2 = bf16[8,2,128,128]{3,2,1,0:T(8,128)(2,1)S(1)} async-done(((bf16[8,2,128,128]{3,2,1,0:T(8,128)(2,1)}), bf16[8,2,128,128]{3,2,1,0:T(8,128)(2,1)S(1)}, u32[]{:S(2)}, u32[]{:S(2)}) %all-to-all-start.2) | async-done | bytes 524320 | tf_op jit(solution)/shard_map/all_to_all | solution.py:24
  34.1 4.9 %all-to-all-start = ((bf16[4,1024,128]{2,1,0:T(8,128)(2,1)}), bf16[4,1024,128]{2,1,0:T(8,128)(2,1)S(1)}, u32[]{:S(2)}, u32[]{:S(2)}) async-start(bf16[4,1024,128]{2,1,0:T(8,128)(2,1)} %bitcast), calls=%async_computation | async-start | bytes 2097152 | tf_op jit(solution)/shard_map/all_to_all | solution.py:36
  38.9 1.5 pad_maximum_fusion
  40.5 13.9 %gather_fusion = bf16[512,128,128]{2,1,0:T(8,128)(2,1)} fusion(bf16[48,128,128]{2,1,0:T(8,128)(2,1)S(1)} %pad_maximum_fusion, s32[1024]{0:T(1024)S(1)} %pad_clamp_fusion), kind=kCustom, calls=%fused_computation | custom fusion | bytes 33556480 | tf_op jit(solution)/shard_map/jit(_take)/gather | solution.py:32
  54.4 13.0 %bitcast_convert_fusion = bf16[32,128,128]{1,2,0:T(8,128)(2,1)S(1)} fusion(bf16[32,16,128,128]{3,2,1,0:T(8,128)(2,1)} %param.8, bf16[32,16,128,128]{3,2,1,0:T(8,128)(2,1)} %bitcast.72, pred[32,16]{1,0:T(8,128)(4,1)S(1)} %copy.43), kind=kOutput, calls=%fused_computation.27 | convolution fusion | flops 2156396544 | bytes 34603520 | tf_op jit(solution)/shard_map/bkij,bkjf->bif/dot_general | solution.py:33
  67.4 1.3 copy.46
  68.7 5.2 %all-to-all-start.3 = ((bf16[4,1024,128]{1,2,0:T(8,128)(2,1)}), bf16[4,1024,128]{1,2,0:T(8,128)(2,1)}, u32[]{:S(2)}, u32[]{:S(2)}) async-start(bf16[4,1024,128]{1,2,0:T(8,128)(2,1)} %copy.46), calls=%async_computation.3 | async-start | bytes 2097152 | tf_op jit(solution)/shard_map/all_to_all | solution.py:37
  73.9 0.5 copy.42
  74.5 2.1 fusion.31
  76.5 20.4 %all-to-all-done.3 = bf16[4,1024,128]{1,2,0:T(8,128)(2,1)} async-done(((bf16[4,1024,128]{1,2,0:T(8,128)(2,1)}), bf16[4,1024,128]{1,2,0:T(8,128)(2,1)}, u32[]{:S(2)}, u32[]{:S(2)}) %all-to-all-start.3) | async-done | bytes 1048608 | tf_op jit(solution)/shard_map/all_to_all | solution.py:37
  97.0 5.1 %fusion.12 = (bf16[1024,512]{1,0:T(8,128)(2,1)S(1)}, bf16[1024,512]{1,0:T(8,128)(2,1)}) fusion(bf16[1024,512]{1,0:T(8,128)(2,1)S(1)} %copy-done.7, f32[1024,512]{1,0:T(8,128)} %fusion.31, bf16[1024,512]{0,1:T(8,128)(2,1)} %bitcast.11, bf16[512,512]{1,0:T(8,128)(2,1)S(1)} %copy-done), kind=kOutput, calls=%fused_computation.17 | convolution fusion | flops 549453824 | bytes 6815744 | tf_op jit(solution)/shard_map/dot_general | solution.py:39
  102.0 1.7 convolution_bitcast_fusion.1
  103.8 0.7 convolution_convert_fusion.1
  104.5 1.3 copy.50
  105.8 3.5 all-to-all-start.5
  109.4 0.2 all-reduce.3.cloned.1.call-start
  109.6 3.0 fusion.32
  112.7 1.8 convolution_convert_fusion.2
  114.5 142.1 %all-reduce.3.cloned.1.call-done = (f32[512,512]{0,1:T(8,128)}, f32[512,512]{0,1:T(8,128)}) async-done(((f32[512,512]{0,1:T(8,128)}, f32[512,512]{0,1:T(8,128)}), (f32[512,512]{0,1:T(8,128)}, f32[512,512]{0,1:T(8,128)})) %all-reduce.3.cloned.1.call-update) | async-done | bytes 2097168 | tf_op jit(solution)/shard_map/psum | solution.py:49
  256.6 2.8 broadcast_multiply_fusion
  259.4 2.5 copy.53
  261.9 1.3 copy.54
  263.2 3.5 all-to-all-start.4
  266.8 21.4 %convolution_bitcast_fusion = f32[32,16,128,128]{2,3,1,0:T(8,128)} fusion(bf16[32,128,128,1]{2,1,3,0:T(8,128)(2,1)S(1)} %bitcast.73, bf16[32,16,128,128]{3,2,1,0:T(8,128)(2,1)} %param.8), kind=kOutput, calls=%fused_computation.9 | convolution fusion | flops 2147483648 | bytes 51380224 | tf_op jit(solution)/shard_map/bkij,bif->bkjf/dot_general | solution.py:65
  288.1 33.4 %copy.52 = f32[32,16,128,128]{3,2,1,0:T(8,128)} copy(f32[32,16,128,128]{2,3,1,0:T(8,128)} %convolution_bitcast_fusion) | data formatting | bytes 67108864 | tf_op jit(solution)/shard_map/bkij,bif->bkjf/dot_general | solution.py:65
  321.5 38.5 %fusion.3 = bf16[48,16384]{1,0:T(8,128)(2,1)S(1)} fusion(f32[64,8,128,128]{3,2,1,0:T(8,128)} %bitcast.71, s32[512]{0:T(512)S(1)} %eq.35), kind=kOutput, calls=%fused_computation.4 | convolution fusion | flops 4832649216 | bytes 35129344 | tf_op jit(solution)/shard_map/dot_general | solution.py:72
  360.1 1.0 copy.62
  361.2 0.2 copy-done.2
  361.4 0.8 copy-done.3
  362.2 3.5 all-to-all-start.6
  365.7 1.4 slice_convert_fusion
  367.0 1.5 reshape.82
  368.5 1.5 convert_bitcast_fusion
  370.0 1.8 copy.48
  371.8 3.6 all-to-all-done.6
  375.4 0.6 fusion.24
  375.9 1.5 reshape.80
  377.4 4.5 %fusion.20 = f32[4096,128]{1,0:T(8,128)} fusion(f32[4096,128]{1,0:T(8,128)} %reshape.80, f32[4096,128]{1,0:T(8,128)} %reshape.82, f32[4,1024,128]{2,1,0:T(8,128)} %copy.48), kind=kLoop, calls=%fused_computation.26 | loop fusion | flops 1048576 | bytes 8388608 | tf_op jit(solution)/shard_map/add | solution.py:89
  (31 shorter events, 0.5 us)
Async XLA Ops:
  7.2 89.8 %copy-start = (bf16[512,512]{1,0:T(8,128)(2,1)S(1)}, bf16[512,512]{1,0:T(8,128)(2,1)}, u32[]{:S(2)}) copy-start(bf16[512,512]{1,0:T(8,128)(2,1)} %param.12) | copy-start | bytes 1572868
  8.6 9.8 %all-to-all-start.1 = ((s32[1,8,2]{2,0,1:T(1,128)}), s32[1,8,2]{2,0,1:T(1,128)S(1)}, u32[]{:S(2)}, u32[]{:S(2)}) async-start(s32[1,8,2]{2,0,1:T(1,128)} %copy.44), calls=%async_computation.1 | async-start | bytes 8192 | tf_op jit(solution)/shard_map/all_to_all | solution.py:18
  15.3 9.1 %copy-start.6 = (s32[32,16]{0,1:T(8,128)S(1)}, s32[32,16]{0,1:T(8,128)}, u32[]{:S(2)}) copy-start(s32[32,16]{0,1:T(8,128)} %param.9) | copy-start | bytes 6148
  20.9 13.2 %all-to-all-start.2 = ((bf16[8,2,128,128]{3,2,1,0:T(8,128)(2,1)}), bf16[8,2,128,128]{3,2,1,0:T(8,128)(2,1)S(1)}, u32[]{:S(2)}, u32[]{:S(2)}) async-start(bf16[8,2,128,128]{3,2,1,0:T(8,128)(2,1)} %bitcast.29), calls=%async_computation.2 | async-start | bytes 1048576 | tf_op jit(solution)/shard_map/all_to_all | solution.py:24
  34.1 4.9 %copy-start.4 = (bf16[8,2,128,128]{3,2,1,0:T(8,128)(2,1)}, bf16[8,2,128,128]{3,2,1,0:T(8,128)(2,1)S(1)}, u32[]{:S(2)}) copy-start(bf16[8,2,128,128]{3,2,1,0:T(8,128)(2,1)S(1)} %all-to-all-done.2) | copy-start | bytes 1572868
  34.1 34.6 %all-to-all-start = ((bf16[4,1024,128]{2,1,0:T(8,128)(2,1)}), bf16[4,1024,128]{2,1,0:T(8,128)(2,1)S(1)}, u32[]{:S(2)}, u32[]{:S(2)}) async-start(bf16[4,1024,128]{2,1,0:T(8,128)(2,1)} %bitcast), calls=%async_computation | async-start | bytes 2097152 | tf_op jit(solution)/shard_map/all_to_all | solution.py:36
  68.7 5.8 %copy-start.5 = (bf16[512,512]{1,0:T(8,128)(2,1)S(1)}, bf16[512,512]{1,0:T(8,128)(2,1)}, u32[]{:S(2)}) copy-start(bf16[512,512]{1,0:T(8,128)(2,1)} %param.11) | copy-start | bytes 1572868
  68.7 28.2 %all-to-all-start.3 = ((bf16[4,1024,128]{1,2,0:T(8,128)(2,1)}), bf16[4,1024,128]{1,2,0:T(8,128)(2,1)}, u32[]{:S(2)}, u32[]{:S(2)}) async-start(bf16[4,1024,128]{1,2,0:T(8,128)(2,1)} %copy.46), calls=%async_computation.3 | async-start | bytes 2097152 | tf_op jit(solution)/shard_map/all_to_all | solution.py:37
  74.5 22.5 %copy-start.7 = (bf16[1024,512]{1,0:T(8,128)(2,1)S(1)}, bf16[1024,512]{1,0:T(8,128)(2,1)}, u32[]{:S(2)}) copy-start(bf16[1024,512]{1,0:T(8,128)(2,1)} %param.13) | copy-start | bytes 3145732
  102.0 2.5 copy-start.8
  104.5 5.1 %copy-start.9 = (bf16[1024,512]{1,0:T(8,128)(2,1)S(1)}, bf16[1024,512]{1,0:T(8,128)(2,1)}, u32[]{:S(2)}) copy-start(bf16[1024,512]{1,0:T(8,128)(2,1)} %copy-done.8) | copy-start | bytes 3145732
  105.8 157.4 %all-to-all-start.5 = ((bf16[1024,4,128]{2,0,1:T(8,128)(2,1)}), bf16[1024,4,128]{2,0,1:T(8,128)(2,1)S(1)}, u32[]{:S(2)}, u32[]{:S(2)}) async-start(bf16[1024,4,128]{2,0,1:T(8,128)(2,1)} %copy.50), calls=%async_computation.5 | async-start | bytes 2097152 | tf_op jit(solution)/shard_map/all_to_all | solution.py:62
  109.4 147.3 %all-reduce.3.cloned.1.call-start = ((), (), s32[]{:S(2)}) async-start(), calls=%async_computation.7 | async-start | bytes 4194304 | tf_op jit(solution)/shard_map/psum | solution.py:49
  263.2 97.9 %all-to-all-start.4 = ((bf16[1024,4,128]{0,2,1:T(8,128)(2,1)}), bf16[1024,4,128]{0,2,1:T(8,128)(2,1)S(1)}, u32[]{:S(2)}, u32[]{:S(2)}) async-start(bf16[1024,4,128]{0,2,1:T(8,128)(2,1)} %bitcast.79), calls=%async_computation.4 | async-start | bytes 2097152 | tf_op jit(solution)/shard_map/all_to_all | solution.py:61
  360.1 1.3 copy-start.2
  361.2 1.0 copy-start.3
  362.2 13.2 %all-to-all-start.6 = ((bf16[8,2,128,128]{3,2,1,0:T(8,128)(2,1)}), bf16[8,2,128,128]{3,2,1,0:T(8,128)(2,1)S(1)}, u32[]{:S(2)}, u32[]{:S(2)}) async-start(bf16[8,2,128,128]{3,2,1,0:T(8,128)(2,1)} %bitcast.35), calls=%async_computation.6 | async-start | bytes 1048576 | tf_op jit(solution)/shard_map/all_to_all | solution.py:80
  377.4 4.5 %copy-start.1 = (bf16[512,512]{1,0:T(8,128)(2,1)S(1)}, bf16[512,512]{1,0:T(8,128)(2,1)}, u32[]{:S(2)}) copy-start(bf16[512,512]{1,0:T(8,128)(2,1)} %param.12) | copy-start | bytes 1572868
Sparse Core Ops, SparseCore 0:
  116.3 140.3 all-reduce.2
where the time goes:
time: 390 us; the launch traced here: 389 us
  waiting for transfers between devices  179 us (46%)
  matrix products  88.2 us (23%)
  local copies, waits for them, and re-layouts  66 us (17%)
  starting transfers between devices  29.5 us (8%)
  between operations  14.3 us (4%)
  other arithmetic  12.3 us (3%)
    psum x1, waiting for transfers between devices, body(): lax.psum((weight_terms[0], weight_terms[1]), ('rows', 'cols'))  142 us
    dot_general x1, matrix products, body(): jnp.dot(pick_table, per_ref.reshape(blocks * per_block, tile_rows * feat_...  38.5 us
    dot_general x1, local copies, waits for them, and re-layouts, body(): jnp.einsum('bkij,bif->bkjf', adj_vals, grad_blocks, preferred_element_typ...  33.4 us
    dot_general x1, matrix products, body(): jnp.einsum('bkij,bif->bkjf', adj_vals, grad_blocks, preferred_element_typ...  21.4 us
    all_to_all x1, waiting for transfers between devices, body(): lax.all_to_all(aggregated, 'cols', split_axis=0, concat_axis=1, tiled=True)  20.4 us
    gather x1, local copies, waits for them, and re-layouts, body(): picked = jnp.take(tile_pool, colref, axis=0)  13.9 us
    dot_general x1, matrix products, body(): jnp.einsum('bkij,bkjf->bif', adj_vals, picked, preferred_element_type=jnp...  13 us
    all_to_all x1, waiting for transfers between devices, body(): lax.all_to_all(outgoing, 'rows', split_axis=0, concat_axis=0, tiled=True)  9.36 us
  transfers between devices with their start and end apart: 8, of which 5 were waited for; matrix products, arithmetic and copies ran while one was open for 38% of the time, Pallas kernels for 0%

commit v1 on v0

v1 whole, which is shorter than its diff:
```python
import math

import jax
import jax.numpy as jnp
from jax import lax
from jax.experimental import pallas as pl
from jax.experimental.pallas import tpu as pltpu
from jax.sharding import PartitionSpec as P


BF16, F32 = jnp.bfloat16, jnp.float32
CHUNKS = 2
VMEM_LIMIT = 56 * 1024 * 1024


def params(dims):
    return pltpu.CompilerParams(
        dimension_semantics=("arbitrary",) * dims, vmem_limit_bytes=VMEM_LIMIT
    )


def full(shape):
    return pl.BlockSpec(shape, lambda *_: (0,) * len(shape))


def rows_at(index, tile):
    return pl.ds(pl.multiple_of(index * tile, tile), tile)


def select_tiles(wanted, feats, tile):
    slots, width = wanted.shape[0], feats.shape[1]

    def kernel(wanted_ref, feats_ref, out_ref):
        for slot in range(slots):
            source = jnp.maximum(wanted_ref[slot], 0)
            out_ref[slot * tile : (slot + 1) * tile, :] = feats_ref[rows_at(source, tile), :]

    return pl.pallas_call(
        kernel,
        out_shape=jax.ShapeDtypeStruct((slots * tile, width), feats.dtype),
        grid_spec=pltpu.PrefetchScalarGridSpec(
            num_scalar_prefetch=1,
            grid=(1,),
            in_specs=[full(feats.shape)],
            out_specs=full((slots * tile, width)),
        ),
        compiler_params=params(1),
        name="select_tiles",
    )(wanted, feats)


def aggregate(col, colref, feats, arrived, adj, chunk, parts):
    blocks, per_block, tile, _ = adj.shape
    width = feats.shape[1]
    own = feats.shape[0]
    per_part = blocks // parts
    per_chunk = per_part // CHUNKS
    chunk_rows = per_chunk * tile

    def tile_of(k, t, col_ref):
        return (k ^ col_ref[0]) * per_part + chunk * per_chunk + t

    def kernel(col_ref, colref_ref, feats_ref, arrived_ref, *refs):
        adj_refs, outs, pool = refs[:parts], refs[parts : 2 * parts], refs[-1]
        t = pl.program_id(0)

        @pl.when(t == 0)
        def _():
            pool[:own, :] = feats_ref[...]
            pool[own:, :] = arrived_ref[...]

        for k in range(parts):
            b = tile_of(k, t, col_ref)
            right = jnp.concatenate(
                [pool[rows_at(colref_ref[b, q], tile), :] for q in range(per_block)], axis=0
            )
            left = jnp.concatenate([adj_refs[k][0, q] for q in range(per_block)], axis=1)
            outs[k][...] = jnp.dot(left, right, preferred_element_type=F32).astype(BF16)

    def adj_spec(k):
        return pl.BlockSpec(
            (1, per_block, tile, tile), lambda t, c, r: (tile_of(k, t, c), 0, 0, 0)
        )

    return pl.pallas_call(
        kernel,
        out_shape=[jax.ShapeDtypeStruct((chunk_rows, width), BF16)] * parts,
        grid_spec=pltpu.PrefetchScalarGridSpec(
            num_scalar_prefetch=2,
            grid=(per_chunk,),
            in_specs=[full(feats.shape), full(arrived.shape)]
            + [adj_spec(k) for k in range(parts)],
            out_specs=[pl.BlockSpec((tile, width), lambda t, c, r: (t, 0))] * parts,
            scratch_shapes=[pltpu.VMEM((own + arrived.shape[0], width), BF16)],
        ),
        compiler_params=params(1),
        name="aggregate",
    )(col, colref, feats, arrived, *[adj] * parts)


def permuted(w_ref, col_ref, parts, width):
    return jnp.concatenate(
        [w_ref[rows_at(k ^ col_ref[0], width), :] for k in range(parts)], axis=0
    )


NT = (((1,), (1,)), ((), ()))
TN = (((0,), (0,)), ((), ()))


def dense(col, feat_parts, agg_parts, w_self, w_neigh, grad_out, act_prev, chunk):
    parts = len(feat_parts)
    chunk_rows, width = agg_parts[0].shape
    hidden = w_self.shape[1]
    steps = 2
    rows = chunk_rows // steps
    root = math.sqrt(2.0 / math.pi)

    def kernel(col_ref, *refs):
        f_refs, a_refs = refs[:parts], refs[parts : 2 * parts]
        ws_ref, wn_ref, go_ref = refs[2 * parts : 2 * parts + 3]
        outs = refs[2 * parts + 3 + (act_prev is not None) :]
        act_ref, g_ref, back = outs[0], outs[1], outs[2:]
        ws = permuted(ws_ref, col_ref, parts, width)
        wn = permuted(wn_ref, col_ref, parts, width)
        f = jnp.concatenate([r[...] for r in f_refs], axis=1)
        a = jnp.concatenate([r[...] for r in a_refs], axis=1)
        v = jnp.dot(f, ws, preferred_element_type=F32) + jnp.dot(a, wn, preferred_element_type=F32)
        square = v * v
        tanh = jnp.tanh(root * (v + 0.044715 * (square * v)))
        half = 0.5 * (1.0 + tanh)
        act_ref[...] = (v * half).astype(BF16)
        slope = half + 0.5 * v * (1.0 - tanh * tanh) * (root * (1.0 + 3 * 0.044715 * square))
        g = (go_ref[...].astype(F32) * slope).astype(BF16)
        g_ref[...] = g
        spread = lax.dot_general(g, wn, NT, preferred_element_type=F32).astype(BF16)
        for k, out in enumerate(back):
            out[...] = spread[:, k * width : (k + 1) * width]

    offset = chunk * steps
    in_specs = (
        [pl.BlockSpec((rows, width), lambda i, c: (offset + i, 0))] * parts
        + [pl.BlockSpec((rows, width), lambda i, c: (i, 0))] * parts
        + [full(w_self.shape), full(w_neigh.shape)]
        + [pl.BlockSpec((rows, hidden), lambda i, c: (offset + i, 0))]
    )
    args = [col, *feat_parts, *agg_parts, w_self, w_neigh, grad_out]
    aliases = {}
    if act_prev is not None:
        in_specs.append(pl.BlockSpec(memory_space=pl.ANY))
        aliases = {len(args): 0}
        args.append(act_prev)
    return pl.pallas_call(
        kernel,
        out_shape=[
            jax.ShapeDtypeStruct((chunk_rows * CHUNKS, hidden), BF16),
            jax.ShapeDtypeStruct((chunk_rows, hidden), BF16),
        ]
        + [jax.ShapeDtypeStruct((chunk_rows, width), BF16)] * parts,
        grid_spec=pltpu.PrefetchScalarGridSpec(
            num_scalar_prefetch=1,
            grid=(steps,),
            in_specs=in_specs,
            out_specs=[
                pl.BlockSpec((rows, hidden), lambda i, c: (offset + i, 0)),
                pl.BlockSpec((rows, hidden), lambda i, c: (i, 0)),
            ]
            + [pl.BlockSpec((rows, width), lambda i, c: (i, 0))] * parts,
        ),
        input_output_aliases=aliases,
        compiler_params=params(1),
        name="dense",
    )(*args)


def weights(col, feat_parts, agg_chunks, grads, w_self):
    parts = len(feat_parts)
    rows, width = feat_parts[0].shape
    hidden = w_self.shape[1]

    def kernel(col_ref, *refs):
        f_refs = refs[:parts]
        a_refs = refs[parts : parts + parts * CHUNKS]
        g_refs = refs[parts + parts * CHUNKS : parts + parts * CHUNKS + CHUNKS]
        ws_ref = refs[parts + parts * CHUNKS + CHUNKS]
        outs = refs[parts + parts * CHUNKS + CHUNKS + 1 :]
        wg_ref, s_refs = outs[0], outs[1:]
        g = jnp.concatenate([r[...] for r in g_refs], axis=0)
        ws = permuted(ws_ref, col_ref, parts, width)
        s = lax.dot_general(g, ws, NT, preferred_element_type=F32).astype(BF16)
        for k, out in enumerate(s_refs):
            out[...] = s[:, k * width : (k + 1) * width]
        for k in range(parts):
            at = k ^ col_ref[0]
            wg_ref[rows_at(at, width), :] = lax.dot_general(
                f_refs[k][...], g, TN, preferred_element_type=F32
            )
            a = jnp.concatenate([a_refs[h * parts + k][...] for h in range(CHUNKS)], axis=0)
            wg_ref[rows_at(at + parts, width), :] = lax.dot_general(
                a, g, TN, preferred_element_type=F32
            )

    args = [*feat_parts, *[a for chunk in agg_chunks for a in chunk], *grads, w_self]
    out_shape = [jax.ShapeDtypeStruct((2 * parts * width, hidden), F32)] + [
        jax.ShapeDtypeStruct((rows, width), BF16)
    ] * parts
    return pl.pallas_call(
        kernel,
        out_shape=out_shape,
        grid_spec=pltpu.PrefetchScalarGridSpec(
            num_scalar_prefetch=1,
            grid=(1,),
            in_specs=[full(a.shape) for a in args],
            out_specs=[full(o.shape) for o in out_shape],
        ),
        compiler_params=params(1),
        name="weights",
    )(col, *args)


def pull(col, colref, grad_chunks, adj, slots):
    blocks, per_block, tile, _ = adj.shape
    parts = len(grad_chunks[0])
    chunk_rows, width = grad_chunks[0][0].shape
    per_part = blocks // parts
    pool = blocks + slots

    def kernel(col_ref, colref_ref, *refs):
        g_refs = refs[: parts * CHUNKS]
        adj_refs = refs[parts * CHUNKS : parts * CHUNKS + parts]
        local_ref, remote_ref, grads, acc = refs[parts * CHUNKS + parts :]
        t = pl.program_id(0)

        @pl.when(t == 0)
        def _():
            acc[...] = jnp.zeros_like(acc)
            for j in range(parts):
                for h in range(CHUNKS):
                    at = (j * CHUNKS + h) * chunk_rows
                    grads[at : at + chunk_rows, :] = g_refs[h * parts + j][...]

        for k in range(parts):
            b = (k ^ col_ref[0]) * per_part + t
            turned = grads[rows_at(k * per_part + t, tile), :].T
            for q in range(0, per_block, 2):
                pair = jnp.concatenate([adj_refs[k][0, q], adj_refs[k][0, q + 1]], axis=1)
                both = jnp.dot(turned, pair, preferred_element_type=F32)
                acc[colref_ref[b, q]] += both[:, :tile]
                acc[colref_ref[b, q + 1]] += both[:, tile:]

        @pl.when(t == per_part - 1)
        def _():
            for s in range(blocks):
                local_ref[s * tile : (s + 1) * tile, :] = acc[s].T.astype(BF16)
            for s in range(slots):
                remote_ref[s * tile : (s + 1) * tile, :] = acc[blocks + s].T.astype(BF16)

    def adj_spec(k):
        return pl.BlockSpec(
            (1, per_block, tile, tile), lambda t, c, r: ((k ^ c[0]) * per_part + t, 0, 0, 0)
        )

    flat = [g for chunk in grad_chunks for g in chunk]
    return pl.pallas_call(
        kernel,
        out_shape=[
            jax.ShapeDtypeStruct((blocks * tile, width), BF16),
            jax.ShapeDtypeStruct((slots * tile, width), BF16),
        ],
        grid_spec=pltpu.PrefetchScalarGridSpec(
            num_scalar_prefetch=2,
            grid=(per_part,),
            in_specs=[full(g.shape) for g in flat] + [adj_spec(k) for k in range(parts)],
            out_specs=[full((blocks * tile, width)), full((slots * tile, width))],
            scratch_shapes=[
                pltpu.VMEM((blocks * tile, width), BF16),
                pltpu.VMEM((pool, width, tile), F32),
            ],
        ),
        compiler_params=params(1),
        name="pull",
    )(col, colref, *flat, *[adj] * parts)


def finish(col, wanted, self_parts, local, returned, tile):
    parts = len(self_parts)
    rows, _ = self_parts[0].shape
    slots = wanted.shape[0]

    def kernel(col_ref, wanted_ref, *refs):
        s_refs = refs[:parts]
        local_ref, returned_ref, out_ref = refs[parts:]
        for k in range(parts):
            at = rows_at(k ^ col_ref[0], rows)
            out_ref[at, :] = s_refs[k][...].astype(F32) + local_ref[at, :].astype(F32)
        for s in range(slots):
            target = wanted_ref[s]

            @pl.when(target >= 0)
            def _():
                out_ref[rows_at(target, tile), :] += returned_ref[
                    s * tile : (s + 1) * tile, :
                ].astype(F32)

    args = [*self_parts, local, returned]
    return pl.pallas_call(
        kernel,
        out_shape=jax.ShapeDtypeStruct(local.shape, F32),
        grid_spec=pltpu.PrefetchScalarGridSpec(
            num_scalar_prefetch=2,
            grid=(1,),
            in_specs=[full(a.shape) for a in args],
            out_specs=full(local.shape),
        ),
        compiler_params=params(1),
        name="finish",
    )(col, wanted, *args)


def swap(x, axis, k):
    n = lax.axis_size(axis)
    return lax.ppermute(x, axis, [(i, i ^ k) for i in range(n)])


def exchange(pieces, axis):
    out = [pieces[0]]
    for k in range(1, len(pieces)):
        out.append(swap(pieces[k], axis, k))
    return out


def across_rows(x):
    return lax.all_to_all(x, "rows", split_axis=0, concat_axis=0, tiled=True)


def body(feats, adj_vals, colref, fetch_ids, w_self, w_neigh, grad_out):
    node_rows, width = feats.shape
    _, _, tile, _ = adj_vals.shape
    partitions = lax.axis_size("rows")
    parts = lax.axis_size("cols")
    slots = partitions * fetch_ids.shape[2]
    total_nodes = node_rows * partitions
    c = lax.axis_index("cols")
    col = c.astype(jnp.int32).reshape(1)
    part_rows = node_rows // parts

    feat_parts = exchange(
        [lax.dynamic_slice_in_dim(feats, (c ^ k) * part_rows, part_rows) for k in range(parts)],
        "cols",
    )
    wanted = across_rows(fetch_ids.reshape(partitions, -1)).reshape(slots)
    outgoing = select_tiles(wanted, feats, tile).reshape(partitions, -1, width)
    arrived = across_rows(outgoing).reshape(slots * tile, width)

    agg_chunks = []
    for h in range(CHUNKS):
        pieces = aggregate(col, colref, feats, arrived, adj_vals, h, parts)
        agg_chunks.append(exchange(pieces, "cols"))
    act, grads, grad_chunks = None, [], []
    for h in range(CHUNKS):
        act, g, *back = dense(
            col, feat_parts, agg_chunks[h], w_self, w_neigh, grad_out, act, h
        )
        grads.append(g)
        grad_chunks.append(exchange(back, "cols"))
    partial, *self_rows = weights(col, feat_parts, agg_chunks, grads, w_self)
    self_parts = exchange(self_rows, "cols")

    hidden = w_self.shape[1]
    piece = across_rows(partial.reshape(partitions, -1, hidden)).sum(0)
    sub = piece.shape[0] // parts
    mine = sum(
        exchange(
            [lax.dynamic_slice_in_dim(piece, (c ^ k) * sub, sub) for k in range(parts)], "cols"
        )
    )
    mine = (mine * (1.0 / math.sqrt(total_nodes))).astype(BF16)
    whole = jnp.zeros((parts * sub, hidden), BF16)
    for k, part in enumerate(exchange([mine] * parts, "cols")):
        whole = lax.dynamic_update_slice_in_dim(whole, part, (c ^ k) * sub, 0)
    whole = across_rows(jnp.broadcast_to(whole[None], (partitions, *whole.shape)))
    whole = whole.reshape(2, parts * width, hidden).astype(F32)

    local, remote = pull(col, colref, grad_chunks, adj_vals, slots)
    returned = across_rows(remote.reshape(partitions, -1, width)).reshape(slots * tile, width)
    grad_feats = finish(col, wanted, self_parts, local, returned, tile)
    return (act, whole[0], whole[1], grad_feats)


def solution(mesh):
    in_specs = (
        P("rows", "cols"),
        P("rows", None, None, None),
        P("rows", None),
        P("rows", None, None),
        P(),
        P(),
        P(("rows", "cols"), None),
    )
    out_specs = (P(("rows", "cols"), None), P(), P(), P("rows", "cols"))
    return jax.shard_map(body, mesh=mesh, in_specs=in_specs, out_specs=out_specs, check_vma=False)
```

time: 390 us -> 186 us (0.48)
  waiting for transfers between devices: 179 us -> 54.9 us
  matrix products: 88.2 us -> 0 us
  local copies, waits for them, and re-layouts: 66 us -> 9.82 us
  Pallas kernels: 0 us -> 50 us
  starting transfers between devices: 29.5 us -> 55.7 us
  between operations: 14.3 us -> 1.02 us
  other arithmetic: 12.3 us -> 0.9 us
  blocking collectives: 0 us -> 9.67 us
    psum x1 -> x0, waiting for transfers between devices: 142 us -> none  [body(): lax.psum((weight_terms[0], weight_terms[1]), ('rows', 'cols'))]
    dot_general x11 -> x0, matrix products: 88.2 us -> none  [the longest x1 38.5 us: body(): jnp.dot(pick_table, per_ref.reshape(blocks * per_block, tile_rows * feat_...]
    pallas_call x0 -> x8, Pallas kernels: none -> 50 us  [the longest x2 15.4 us: aggregate(): pl.pallas_call(kernel, out_shape=[jax.ShapeDtypeStruct((chunk_rows, width...]
    ppermute x0 -> x24, starting transfers between devices: none -> 40.8 us  [swap(): return lax.ppermute(x, axis, [(i, i ^ k) for i in range(n)])]
    dot_general x1 -> x0, local copies, waits for them, and re-layouts: 33.4 us -> none  [body(): jnp.einsum('bkij,bif->bkjf', adj_vals, grad_blocks, preferred_element_typ...]
    ppermute x0 -> x24, waiting for transfers between devices: none -> 33.1 us  [swap(): return lax.ppermute(x, axis, [(i, i ^ k) for i in range(n)])]
    all_to_all x7 -> x4, waiting for transfers between devices: 36.4 us -> 21.8 us  [across_rows(): return lax.all_to_all(x, 'rows', split_axis=0, concat_axis=0, tiled=True)]
    all_to_all x7 -> x4, starting transfers between devices: 29.3 us -> 14.9 us  [across_rows(): return lax.all_to_all(x, 'rows', split_axis=0, concat_axis=0, tiled=True)]
  transfers between devices with their start and end apart: 8 -> 28, of which waited for: 5 -> 8; matrix products, arithmetic and copies ran while one was open for 38% -> 1% of each run, Pallas kernels for 0% -> 21%
where the time goes in v1:
time: 186 us; the launch traced here: 182 us
  starting transfers between devices  55.7 us (30%)
  waiting for transfers between devices  54.9 us (30%)
  Pallas kernels  50 us (27%)
  local copies, waits for them, and re-layouts  9.82 us (5%)
  blocking collectives  9.67 us (5%)
    ppermute x24, starting transfers between devices, swap(): return lax.ppermute(x, axis, [(i, i ^ k) for i in range(n)])  40.8 us
    ppermute x24, waiting for transfers between devices, swap(): return lax.ppermute(x, axis, [(i, i ^ k) for i in range(n)])  33.1 us
    all_to_all x4, waiting for transfers between devices, across_rows(): return lax.all_to_all(x, 'rows', split_axis=0, concat_axis=0, tiled=True)  21.8 us
    pallas_call x2, Pallas kernels, aggregate(): pl.pallas_call(kernel, out_shape=[jax.ShapeDtypeStruct((chunk_rows, width...  15.4 us
    all_to_all x4, starting transfers between devices, across_rows(): return lax.all_to_all(x, 'rows', split_axis=0, concat_axis=0, tiled=True)  14.9 us
    pallas_call x1, Pallas kernels, pull(): pl.pallas_call(kernel, out_shape=[jax.ShapeDtypeStruct((blocks * tile, wi...  14 us
    all_to_all x1, blocking collectives, across_rows(): return lax.all_to_all(x, 'rows', split_axis=0, concat_axis=0, tiled=True)  9.67 us
    pallas_call x2, Pallas kernels, dense(): pl.pallas_call(kernel, out_shape=[jax.ShapeDtypeStruct((chunk_rows * CHUN...  8.53 us
  transfers between devices with their start and end apart: 28, of which 8 were waited for; matrix products, arithmetic and copies ran while one was open for 1% of the time, Pallas kernels for 21%

profile of v1, /device:TPU:0, one launch (start us, length us, event | category | flops | bytes accessed | tf_op | source)
XLA Modules:
  0.0 182.0 jit_solution(8739176497665648693)
XLA Ops:
  0.6 0.8 copy.20
  1.5 9.7 %all_to_all.29 = s32[8,1,2]{2,1,0:T(1,128)S(1)} all-to-all(s32[8,1,2]{2,1,0:T(1,128)S(1)} %copy.20), channel_id=1, replica_groups=mesh['rows'=8,'cols'=4] {'rows'}, dimensions={0} | all-to-all | bytes 128 | tf_op jit(solution)/shard_map/all_to_all | solution.py:333
  12.9 2.8 %select_tiles.1 = bf16[2048,128]{1,0:T(8,128)(2,1)} custom-call(s32[16]{0:T(128)} %reshape.61.wanted_ref, bf16[4096,128]{1,0:T(8,128)(2,1)} %feats_ref.5), custom_call_target="tpu_custom_call" | custom-call | tf_op jit(solution)/shard_map/select_tiles/pallas_call | solution.py:38
  15.8 3.5 %all-to-all-start.1 = ((bf16[8,256,128]{2,1,0:T(8,128)(2,1)}), bf16[8,256,128]{2,1,0:T(8,128)(2,1)S(1)}, u32[]{:S(2)}, u32[]{:S(2)}) async-start(bf16[8,256,128]{2,1,0:T(8,128)(2,1)} %bitcast.13), calls=%async_computation.1 | async-start | bytes 1048576 | tf_op jit(solution)/shard_map/all_to_all | solution.py:333
  19.3 0.8 constant_dynamic-slice_fusion.3
  20.1 1.6 collective-permute-start
  21.7 2.6 %collective-permute-start.1 = (bf16[1024,128]{1,0:T(8,128)(2,1)S(1)}, bf16[1024,128]{1,0:T(8,128)(2,1)S(1)}, u32[]{:S(2)}, u32[]{:S(2)}) collective-permute-start(bf16[1024,128]{1,0:T(8,128)(2,1)S(1)} %get-tuple-element.63), channel_id=1, source_target_pairs={{0,2},{1,3},{2,0},{3,1},{4,6},{5,7},{6,4},{7,5},{8,10},{9,11},{10,... | collective-permute-start | bytes 786440 | tf_op jit(solution)/shard_map/ppermute | solution.py:322
  24.5 0.7 copy.21.colref_ref
  25.2 3.8 %all-to-all-done.1 = bf16[8,256,128]{2,1,0:T(8,128)(2,1)S(1)} async-done(((bf16[8,256,128]{2,1,0:T(8,128)(2,1)}), bf16[8,256,128]{2,1,0:T(8,128)(2,1)S(1)}, u32[]{:S(2)}, u32[]{:S(2)}) %all-to-all-start.1) | async-done | bytes 524320 | tf_op jit(solution)/shard_map/all_to_all | solution.py:333
  28.9 0.8 copy-done.1
  29.7 7.7 %aggregate.3 = (bf16[512,128]{1,0:T(8,128)(2,1)}, bf16[512,128]{1,0:T(8,128)(2,1)}, bf16[512,128]{1,0:T(8,128)(2,1)}, bf16[512,128]{1,0:T(8,128)(2,1)}) custom-call(s32[1]{0:T(128)} %bitcast.col_ref, s32[32,16]{1,0:T(8,128)} %copy.21.colref_ref, bf16[4096,128]{1,0:T(8,128)(2,1)} %feats_ref.5, bf16[2048,128]{1,0:T(8,128)(2,1)} %bitcast.9, ...), custom_call_target="tpu_custom_call" | custom-call | tf_op jit(solution)/shard_map/aggregate/pallas_call | solution.py:85
  37.5 1.6 collective-permute-start.6
  39.1 7.7 %aggregate.2 = (bf16[512,128]{1,0:T(8,128)(2,1)}, bf16[512,128]{1,0:T(8,128)(2,1)}, bf16[512,128]{1,0:T(8,128)(2,1)}, bf16[512,128]{1,0:T(8,128)(2,1)}) custom-call(s32[1]{0:T(128)} %bitcast.col_ref, s32[32,16]{1,0:T(8,128)} %copy.21.colref_ref, bf16[4096,128]{1,0:T(8,128)(2,1)} %feats_ref.5, bf16[2048,128]{1,0:T(8,128)(2,1)} %bitcast.10, ...), custom_call_target="tpu_custom_call" | custom-call | tf_op jit(solution)/shard_map/aggregate/pallas_call | solution.py:85
  46.8 2.7 %collective-permute-start.7 = (bf16[512,128]{1,0:T(8,128)(2,1)S(1)}, bf16[512,128]{1,0:T(8,128)(2,1)S(1)}, u32[]{:S(2)}, u32[]{:S(2)}) collective-permute-start(bf16[512,128]{1,0:T(8,128)(2,1)S(1)} %copy-done.30), channel_id=1, source_target_pairs={{0,2},{1,3},{2,0},{3,1},{4,6},{5,7},{6,4},{7,5},{8,10},{9,11},{10,... | collective-permute-start | bytes 393224 | tf_op jit(solution)/shard_map/ppermute | solution.py:322
  49.8 0.7 collective-permute-start.3
  50.5 3.5 %collective-permute-start.4 = (bf16[512,128]{1,0:T(8,128)(2,1)}, bf16[512,128]{1,0:T(8,128)(2,1)S(1)}, u32[]{:S(2)}, u32[]{:S(2)}) collective-permute-start(bf16[512,128]{1,0:T(8,128)(2,1)} %get-tuple-element.33), channel_id=1, source_target_pairs={{0,2},{1,3},{2,0},{3,1},{4,6},{5,7},{6,4},{7,5},{8,10},{9,11},{10,... | collective-permute-start | bytes 393224 | tf_op jit(solution)/shard_map/ppermute | solution.py:322
  54.2 9.8 %collective-permute-done.7.refs_6_ = bf16[512,128]{1,0:T(8,128)(2,1)S(1)} collective-permute-done((bf16[512,128]{1,0:T(8,128)(2,1)S(1)}, bf16[512,128]{1,0:T(8,128)(2,1)S(1)}, u32[]{:S(2)}, u32[]{:S(2)}) %collective-permute-start.7) | collective-permute-done | bytes 131104 | tf_op jit(solution)/shard_map/ppermute | solution.py:322
  64.7 4.3 %dense.2 = (bf16[1024,512]{1,0:T(8,128)(2,1)}, bf16[512,512]{1,0:T(8,128)(2,1)}, bf16[512,128]{1,0:T(8,128)(2,1)}, bf16[512,128]{1,0:T(8,128)(2,1)}, bf16[512,128]{1,0:T(8,128)(2,1)}, /*index=5*/bf16[512,128]{1,0:T(8,128)(2,1)}) custom-call(s32[1]{0:T(128)} %bitcast.col_ref, bf16[1024,128]{1,0:T(8,128)(2,1)} %get-tuple-element.65.refs_0_, ...), custom_call_target="tpu_custom_call" | custom-call | tf_op jit(solution)/shard_map/dense/pallas_call | solution.py:153
  69.7 4.3 %dense.3 = (bf16[1024,512]{1,0:T(8,128)(2,1)}, bf16[512,512]{1,0:T(8,128)(2,1)}, bf16[512,128]{1,0:T(8,128)(2,1)}, bf16[512,128]{1,0:T(8,128)(2,1)}, bf16[512,128]{1,0:T(8,128)(2,1)}, /*index=5*/bf16[512,128]{1,0:T(8,128)(2,1)}) custom-call(s32[1]{0:T(128)} %bitcast.col_ref, ...), custom_call_target="tpu_custom_call", output_to_operand_aliasing={{0}: (12, {})} | custom-call | tf_op jit(solution)/shard_map/dense/pallas_call | solution.py:153
  74.0 5.2 %weights.1 = (f32[1024,512]{1,0:T(8,128)}, bf16[1024,128]{1,0:T(8,128)(2,1)}, bf16[1024,128]{1,0:T(8,128)(2,1)}, bf16[1024,128]{1,0:T(8,128)(2,1)}, bf16[1024,128]{1,0:T(8,128)(2,1)}) custom-call(s32[1]{0:T(128)} %bitcast.col_ref, bf16[1024,128]{1,0:T(8,128)(2,1)} %get-tuple-element.65.refs_0_, bf16[1024,128]{1,0:T(8,128)(2,1)} %copy-done.2, ...), custom_call_target="tpu_custom_call" | custom-call | tf_op jit(solution)/shard_map/weights/pallas_call | solution.py:207
  79.2 3.7 %all-to-all-start.2 = ((f32[8,128,512]{2,1,0:T(8,128)}), f32[8,128,512]{2,1,0:T(8,128)S(1)}, u32[]{:S(2)}, u32[]{:S(2)}) async-start(f32[8,128,512]{2,1,0:T(8,128)} %bitcast.12), calls=%async_computation.2 | async-start | bytes 4194304 | tf_op jit(solution)/shard_map/all_to_all | solution.py:333
  83.0 3.4 %collective-permute-start.18 = (bf16[512,128]{1,0:T(8,128)(2,1)}, bf16[512,128]{1,0:T(8,128)(2,1)S(1)}, u32[]{:S(2)}, u32[]{:S(2)}) collective-permute-start(bf16[512,128]{1,0:T(8,128)(2,1)} %get-tuple-element.49), channel_id=1, source_target_pairs={{0,1},{1,0},{2,3},{3,2},{4,5},{5,4},{6,7},{7,6},{8,9},{9,8},{10,11... | collective-permute-start | bytes 393224 | tf_op jit(solution)/shard_map/ppermute | solution.py:322
  86.4 0.7 collective-permute-start.19
  87.1 1.7 collective-permute-start.20
  88.8 1.0 collective-permute-start.21
  89.9 1.6 collective-permute-start.22
  91.5 18.0 %all-to-all-done.2 = f32[8,128,512]{2,1,0:T(8,128)S(1)} async-done(((f32[8,128,512]{2,1,0:T(8,128)}), f32[8,128,512]{2,1,0:T(8,128)S(1)}, u32[]{:S(2)}, u32[]{:S(2)}) %all-to-all-start.2) | async-done | bytes 2097184 | tf_op jit(solution)/shard_map/all_to_all | solution.py:333
  109.8 2.8 %collective-permute-start.23 = (bf16[512,128]{1,0:T(8,128)(2,1)S(1)}, bf16[512,128]{1,0:T(8,128)(2,1)S(1)}, u32[]{:S(2)}, u32[]{:S(2)}) collective-permute-start(bf16[512,128]{1,0:T(8,128)(2,1)S(1)} %copy-done.25), channel_id=1, source_target_pairs={{0,3},{1,2},{2,1},{3,0},{4,7},{5,6},{6,5},{7,4},{8,11},{9,10},{10,... | collective-permute-start | bytes 393224 | tf_op jit(solution)/shard_map/ppermute | solution.py:322
  112.6 1.1 collective-permute-start.11
  113.8 2.2 %collective-permute-start.10 = (f32[32,512]{1,0:T(8,128)S(1)}, f32[32,512]{1,0:T(8,128)S(1)}, u32[]{:S(2)}, u32[]{:S(2)}) collective-permute-start(f32[32,512]{1,0:T(8,128)S(1)} %get-tuple-element.68), channel_id=1, source_target_pairs={{0,2},{1,3},{2,0},{3,1},{4,6},{5,7},{6,4},{7,5},{8,10},{9,11},{10,... | collective-permute-start | bytes 196616 | tf_op jit(solution)/shard_map/ppermute | solution.py:322
  116.0 1.1 collective-permute-start.9
  118.1 14.0 %pull.1 = (bf16[4096,128]{1,0:T(8,128)(2,1)}, bf16[2048,128]{1,0:T(8,128)(2,1)}) custom-call(s32[1]{0:T(128)} %bitcast.col_ref, s32[32,16]{1,0:T(8,128)} %copy.21.colref_ref, bf16[512,128]{1,0:T(8,128)(2,1)} %get-tuple-element.48.refs_0_, bf16[512,128]{1,0:T(8,128)(2,1)} %copy-done.15, bf16[512,128]{1,0:T(8,128)(2,1)} %copy-done.16, ...), custom_call_target="tpu_custom_call" | custom-call | tf_op jit(solution)/shard_map/pull/pallas_call | solution.py:264
  132.1 3.5 %all-to-all-start.4 = ((bf16[8,256,128]{2,1,0:T(8,128)(2,1)}), bf16[8,256,128]{2,1,0:T(8,128)(2,1)S(1)}, u32[]{:S(2)}, u32[]{:S(2)}) async-start(bf16[8,256,128]{2,1,0:T(8,128)(2,1)} %bitcast.16), calls=%async_computation.4 | async-start | bytes 1048576 | tf_op jit(solution)/shard_map/all_to_all | solution.py:333
  135.7 4.2 %collective-permute-start.12 = (bf16[32,512]{1,0:T(8,128)(2,1)S(1)}, bf16[32,512]{1,0:T(8,128)(2,1)S(1)}, u32[]{:S(2)}, u32[]{:S(2)}) collective-permute-start(bf16[32,512]{1,0:T(8,128)(2,1)S(1)} %get-tuple-element.59), channel_id=1, source_target_pairs={{0,1},{1,0},{2,3},{3,2},{4,5},{5,4},{6,7},{7,6},{8,9},{9,8},{10,11... | collective-permute-start | bytes 98312 | tf_op jit(solution)/shard_map/ppermute | solution.py:322
  139.9 1.4 collective-permute-start.13
  141.3 1.4 collective-permute-start.14
  142.7 2.2 %collective-permute-done.13 = bf16[32,512]{1,0:T(8,128)(2,1)S(1)} collective-permute-done((bf16[32,512]{1,0:T(8,128)(2,1)S(1)}, bf16[32,512]{1,0:T(8,128)(2,1)S(1)}, u32[]{:S(2)}, u32[]{:S(2)}) %collective-permute-start.13) | collective-permute-done | bytes 32800 | tf_op jit(solution)/shard_map/ppermute | solution.py:322
  144.9 2.1 %collective-permute-done.14 = bf16[32,512]{1,0:T(8,128)(2,1)S(1)} collective-permute-done((bf16[32,512]{1,0:T(8,128)(2,1)S(1)}, bf16[32,512]{1,0:T(8,128)(2,1)S(1)}, u32[]{:S(2)}, u32[]{:S(2)}) %collective-permute-start.14) | collective-permute-done | bytes 32800 | tf_op jit(solution)/shard_map/ppermute | solution.py:322
  147.0 1.1 broadcast_in_dim.10
  148.2 4.2 %all-to-all-start.3 = ((bf16[8,128,512]{2,1,0:T(8,128)(2,1)}), bf16[8,128,512]{2,1,0:T(8,128)(2,1)S(1)}, u32[]{:S(2)}, u32[]{:S(2)}) async-start(bf16[8,128,512]{2,1,0:T(8,128)(2,1)} %broadcast_in_dim.10), calls=%async_computation.3 | async-start | bytes 2097152 | tf_op jit(solution)/shard_map/all_to_all | solution.py:333
  152.4 1.9 %collective-permute-start.15 = (bf16[1024,128]{1,0:T(8,128)(2,1)S(1)}, bf16[1024,128]{1,0:T(8,128)(2,1)S(1)}, u32[]{:S(2)}, u32[]{:S(2)}) collective-permute-start(bf16[1024,128]{1,0:T(8,128)(2,1)S(1)} %copy-done.24), channel_id=1, source_target_pairs={{0,1},{1,0},{2,3},{3,2},{4,5},{5,4},{6,7},{7,6},{8,9},{9,8},{10,11... | collective-permute-start | bytes 786440 | tf_op jit(solution)/shard_map/ppermute | solution.py:322
  154.3 1.4 collective-permute-start.16
  155.6 1.4 collective-permute-start.17
  157.1 9.2 %collective-permute-done.15.refs_1_ = bf16[1024,128]{1,0:T(8,128)(2,1)S(1)} collective-permute-done((bf16[1024,128]{1,0:T(8,128)(2,1)S(1)}, bf16[1024,128]{1,0:T(8,128)(2,1)S(1)}, u32[]{:S(2)}, u32[]{:S(2)}) %collective-permute-start.15) | collective-permute-done | bytes 262176 | tf_op jit(solution)/shard_map/ppermute | solution.py:322
  166.3 9.3 %collective-permute-done.16.refs_2_ = bf16[1024,128]{1,0:T(8,128)(2,1)S(1)} collective-permute-done((bf16[1024,128]{1,0:T(8,128)(2,1)S(1)}, bf16[1024,128]{1,0:T(8,128)(2,1)S(1)}, u32[]{:S(2)}, u32[]{:S(2)}) %collective-permute-start.16) | collective-permute-done | bytes 262176 | tf_op jit(solution)/shard_map/ppermute | solution.py:322
  175.6 0.7 copy-done.13
  176.4 4.0 %finish.1 = f32[4096,128]{1,0:T(8,128)} custom-call(s32[1]{0:T(128)} %bitcast.col_ref, s32[16]{0:T(128)} %reshape.61.wanted_ref, bf16[1024,128]{1,0:T(8,128)(2,1)} %get-tuple-element.44.refs_0_, bf16[1024,128]{1,0:T(8,128)(2,1)} %copy-done.12, bf16[1024,128]{1,0:T(8,128)(2,1)} %copy-done.13, bf16[1024,128]{1,0:T(8,128)(2,1)} %copy-done.14, ...), custom_call_target="tpu_custom_call" | custom-call | tf_op jit(solution)/shard_map/finish/pallas_call | solution.py:306
  180.4 1.6 fusion
  (94 shorter events, 5.4 us)
Async XLA Ops:
  0.6 18.7 %copy-start = (bf16[4096,128]{1,0:T(8,128)(2,1)S(1)}, bf16[4096,128]{1,0:T(8,128)(2,1)}, u32[]{:S(2)}) copy-start(bf16[4096,128]{1,0:T(8,128)(2,1)} %feats_ref.5) | copy-start | bytes 3145732
  12.9 11.5 %copy-start.21 = (s32[32,16]{0,1:T(8,128)S(1)}, s32[32,16]{0,1:T(8,128)}, u32[]{:S(2)}) copy-start(s32[32,16]{0,1:T(8,128)} %param.9) | copy-start | bytes 6148
  15.8 13.2 %all-to-all-start.1 = ((bf16[8,256,128]{2,1,0:T(8,128)(2,1)}), bf16[8,256,128]{2,1,0:T(8,128)(2,1)S(1)}, u32[]{:S(2)}, u32[]{:S(2)}) async-start(bf16[8,256,128]{2,1,0:T(8,128)(2,1)} %bitcast.13), calls=%async_computation.1 | async-start | bytes 1048576 | tf_op jit(solution)/shard_map/all_to_all | solution.py:333
  20.1 29.4 %collective-permute-start = (bf16[1024,128]{1,0:T(8,128)(2,1)S(1)}, bf16[1024,128]{1,0:T(8,128)(2,1)S(1)}, u32[]{:S(2)}, u32[]{:S(2)}) collective-permute-start(bf16[1024,128]{1,0:T(8,128)(2,1)S(1)} %get-tuple-element.64), channel_id=1, source_target_pairs={{0,1},{1,0},{2,3},{3,2},{4,5},{5,4},{6,7},{7,6},{8,9},{9,8},{10,11... | collective-permute-start | bytes 786440 | tf_op jit(solution)/shard_map/ppermute | solution.py:322
  21.7 28.1 %collective-permute-start.1 = (bf16[1024,128]{1,0:T(8,128)(2,1)S(1)}, bf16[1024,128]{1,0:T(8,128)(2,1)S(1)}, u32[]{:S(2)}, u32[]{:S(2)}) collective-permute-start(bf16[1024,128]{1,0:T(8,128)(2,1)S(1)} %get-tuple-element.63), channel_id=1, source_target_pairs={{0,2},{1,3},{2,0},{3,1},{4,6},{5,7},{6,4},{7,5},{8,10},{9,11},{10,... | collective-permute-start | bytes 786440 | tf_op jit(solution)/shard_map/ppermute | solution.py:322
  24.3 26.2 %collective-permute-start.2 = (bf16[1024,128]{1,0:T(8,128)(2,1)S(1)}, bf16[1024,128]{1,0:T(8,128)(2,1)S(1)}, u32[]{:S(2)}, u32[]{:S(2)}) collective-permute-start(bf16[1024,128]{1,0:T(8,128)(2,1)S(1)} %get-tuple-element.62), channel_id=1, source_target_pairs={{0,3},{1,2},{2,1},{3,0},{4,7},{5,6},{6,5},{7,4},{8,11},{9,10},{10,... | collective-permute-start | bytes 786440 | tf_op jit(solution)/shard_map/ppermute | solution.py:322
  37.4 9.4 %copy-start.30 = (bf16[512,128]{1,0:T(8,128)(2,1)S(1)}, bf16[512,128]{1,0:T(8,128)(2,1)}, u32[]{:S(2)}) copy-start(bf16[512,128]{1,0:T(8,128)(2,1)} %get-tuple-element.37) | copy-start | bytes 393220
  37.4 12.0 %copy-start.29 = (bf16[512,128]{1,0:T(8,128)(2,1)S(1)}, bf16[512,128]{1,0:T(8,128)(2,1)}, u32[]{:S(2)}) copy-start(bf16[512,128]{1,0:T(8,128)(2,1)} %get-tuple-element.38) | copy-start | bytes 393220
  37.5 16.5 %collective-permute-start.6 = (bf16[512,128]{1,0:T(8,128)(2,1)}, bf16[512,128]{1,0:T(8,128)(2,1)S(1)}, u32[]{:S(2)}, u32[]{:S(2)}) collective-permute-start(bf16[512,128]{1,0:T(8,128)(2,1)} %get-tuple-element.36), channel_id=1, source_target_pairs={{0,1},{1,0},{2,3},{3,2},{4,5},{5,4},{6,7},{7,6},{8,9},{9,8},{10,11... | collective-permute-start | bytes 393224 | tf_op jit(solution)/shard_map/ppermute | solution.py:322
  46.8 17.1 %collective-permute-start.7 = (bf16[512,128]{1,0:T(8,128)(2,1)S(1)}, bf16[512,128]{1,0:T(8,128)(2,1)S(1)}, u32[]{:S(2)}, u32[]{:S(2)}) collective-permute-start(bf16[512,128]{1,0:T(8,128)(2,1)S(1)} %copy-done.30), channel_id=1, source_target_pairs={{0,2},{1,3},{2,0},{3,1},{4,6},{5,7},{6,4},{7,5},{8,10},{9,11},{10,... | collective-permute-start | bytes 393224 | tf_op jit(solution)/shard_map/ppermute | solution.py:322
  49.5 14.5 %copy-start.2 = (bf16[1024,128]{1,0:T(8,128)(2,1)}, bf16[1024,128]{1,0:T(8,128)(2,1)S(1)}, u32[]{:S(2)}) copy-start(bf16[1024,128]{1,0:T(8,128)(2,1)S(1)} %collective-permute-done.refs_1_) | copy-start | bytes 786436
  49.5 14.5 %collective-permute-start.8 = (bf16[512,128]{1,0:T(8,128)(2,1)S(1)}, bf16[512,128]{1,0:T(8,128)(2,1)S(1)}, u32[]{:S(2)}, u32[]{:S(2)}) collective-permute-start(bf16[512,128]{1,0:T(8,128)(2,1)S(1)} %copy-done.29), channel_id=1, source_target_pairs={{0,3},{1,2},{2,1},{3,0},{4,7},{5,6},{6,5},{7,4},{8,11},{9,10},{10,... | collective-permute-start | bytes 393224 | tf_op jit(solution)/shard_map/ppermute | solution.py:322
  49.8 14.2 %copy-start.3 = (bf16[1024,128]{1,0:T(8,128)(2,1)}, bf16[1024,128]{1,0:T(8,128)(2,1)S(1)}, u32[]{:S(2)}) copy-start(bf16[1024,128]{1,0:T(8,128)(2,1)S(1)} %collective-permute-done.1.refs_2_) | copy-start | bytes 786436
  49.8 19.2 %collective-permute-start.3 = (bf16[512,128]{1,0:T(8,128)(2,1)}, bf16[512,128]{1,0:T(8,128)(2,1)S(1)}, u32[]{:S(2)}, u32[]{:S(2)}) collective-permute-start(bf16[512,128]{1,0:T(8,128)(2,1)} %get-tuple-element.32), channel_id=1, source_target_pairs={{0,1},{1,0},{2,3},{3,2},{4,5},{5,4},{6,7},{7,6},{8,9},{9,8},{10,11... | collective-permute-start | bytes 393224 | tf_op jit(solution)/shard_map/ppermute | solution.py:322
  50.5 13.5 %copy-start.4 = (bf16[1024,128]{1,0:T(8,128)(2,1)}, bf16[1024,128]{1,0:T(8,128)(2,1)S(1)}, u32[]{:S(2)}) copy-start(bf16[1024,128]{1,0:T(8,128)(2,1)S(1)} %collective-permute-done.2.refs_3_) | copy-start | bytes 786436
  50.5 18.5 %collective-permute-start.4 = (bf16[512,128]{1,0:T(8,128)(2,1)}, bf16[512,128]{1,0:T(8,128)(2,1)S(1)}, u32[]{:S(2)}, u32[]{:S(2)}) collective-permute-start(bf16[512,128]{1,0:T(8,128)(2,1)} %get-tuple-element.33), channel_id=1, source_target_pairs={{0,2},{1,3},{2,0},{3,1},{4,6},{5,7},{6,4},{7,5},{8,10},{9,11},{10,... | collective-permute-start | bytes 393224 | tf_op jit(solution)/shard_map/ppermute | solution.py:322
  54.0 10.1 %copy-start.6 = (bf16[512,128]{1,0:T(8,128)(2,1)}, bf16[512,128]{1,0:T(8,128)(2,1)S(1)}, u32[]{:S(2)}) copy-start(bf16[512,128]{1,0:T(8,128)(2,1)S(1)} %collective-permute-done.6.refs_5_) | copy-start | bytes 393220
  54.0 15.0 %collective-permute-start.5 = (bf16[512,128]{1,0:T(8,128)(2,1)}, bf16[512,128]{1,0:T(8,128)(2,1)S(1)}, u32[]{:S(2)}, u32[]{:S(2)}) collective-permute-start(bf16[512,128]{1,0:T(8,128)(2,1)} %get-tuple-element.34), channel_id=1, source_target_pairs={{0,3},{1,2},{2,1},{3,0},{4,7},{5,6},{6,5},{7,4},{8,11},{9,10},{10,... | collective-permute-start | bytes 393224 | tf_op jit(solution)/shard_map/ppermute | solution.py:322
  79.2 7.2 %copy-start.28 = (bf16[512,128]{1,0:T(8,128)(2,1)S(1)}, bf16[512,128]{1,0:T(8,128)(2,1)}, u32[]{:S(2)}) copy-start(bf16[512,128]{1,0:T(8,128)(2,1)} %get-tuple-element.50) | copy-start | bytes 393220
  79.2 7.9 %copy-start.27 = (bf16[512,128]{1,0:T(8,128)(2,1)S(1)}, bf16[512,128]{1,0:T(8,128)(2,1)}, u32[]{:S(2)}) copy-start(bf16[512,128]{1,0:T(8,128)(2,1)} %get-tuple-element.51) | copy-start | bytes 393220
  79.2 10.7 %copy-start.26 = (bf16[512,128]{1,0:T(8,128)(2,1)S(1)}, bf16[512,128]{1,0:T(8,128)(2,1)}, u32[]{:S(2)}) copy-start(bf16[512,128]{1,0:T(8,128)(2,1)} %get-tuple-element.54) | copy-start | bytes 393220
  79.2 30.3 %all-to-all-start.2 = ((f32[8,128,512]{2,1,0:T(8,128)}), f32[8,128,512]{2,1,0:T(8,128)S(1)}, u32[]{:S(2)}, u32[]{:S(2)}) async-start(f32[8,128,512]{2,1,0:T(8,128)} %bitcast.12), calls=%async_computation.2 | async-start | bytes 4194304 | tf_op jit(solution)/shard_map/all_to_all | solution.py:333
  83.0 26.8 %copy-start.25 = (bf16[512,128]{1,0:T(8,128)(2,1)S(1)}, bf16[512,128]{1,0:T(8,128)(2,1)}, u32[]{:S(2)}) copy-start(bf16[512,128]{1,0:T(8,128)(2,1)} %get-tuple-element.55) | copy-start | bytes 393220
  83.0 26.8 %collective-permute-start.18 = (bf16[512,128]{1,0:T(8,128)(2,1)}, bf16[512,128]{1,0:T(8,128)(2,1)S(1)}, u32[]{:S(2)}, u32[]{:S(2)}) collective-permute-start(bf16[512,128]{1,0:T(8,128)(2,1)} %get-tuple-element.49), channel_id=1, source_target_pairs={{0,1},{1,0},{2,3},{3,2},{4,5},{5,4},{6,7},{7,6},{8,9},{9,8},{10,11... | collective-permute-start | bytes 393224 | tf_op jit(solution)/shard_map/ppermute | solution.py:322
  86.4 26.2 %collective-permute-start.19 = (bf16[512,128]{1,0:T(8,128)(2,1)S(1)}, bf16[512,128]{1,0:T(8,128)(2,1)S(1)}, u32[]{:S(2)}, u32[]{:S(2)}) collective-permute-start(bf16[512,128]{1,0:T(8,128)(2,1)S(1)} %copy-done.28), channel_id=1, source_target_pairs={{0,2},{1,3},{2,0},{3,1},{4,6},{5,7},{6,4},{7,5},{8,10},{9,11},{10,... | collective-permute-start | bytes 393224 | tf_op jit(solution)/shard_map/ppermute | solution.py:322
  87.1 26.7 %collective-permute-start.20 = (bf16[512,128]{1,0:T(8,128)(2,1)S(1)}, bf16[512,128]{1,0:T(8,128)(2,1)S(1)}, u32[]{:S(2)}, u32[]{:S(2)}) collective-permute-start(bf16[512,128]{1,0:T(8,128)(2,1)S(1)} %copy-done.27), channel_id=1, source_target_pairs={{0,3},{1,2},{2,1},{3,0},{4,7},{5,6},{6,5},{7,4},{8,11},{9,10},{10,... | collective-permute-start | bytes 393224 | tf_op jit(solution)/shard_map/ppermute | solution.py:322
  88.8 27.2 %collective-permute-start.21 = (bf16[512,128]{1,0:T(8,128)(2,1)}, bf16[512,128]{1,0:T(8,128)(2,1)S(1)}, u32[]{:S(2)}, u32[]{:S(2)}) collective-permute-start(bf16[512,128]{1,0:T(8,128)(2,1)} %get-tuple-element.53), channel_id=1, source_target_pairs={{0,1},{1,0},{2,3},{3,2},{4,5},{5,4},{6,7},{7,6},{8,9},{9,8},{10,11... | collective-permute-start | bytes 393224 | tf_op jit(solution)/shard_map/ppermute | solution.py:322
  89.9 27.2 %collective-permute-start.22 = (bf16[512,128]{1,0:T(8,128)(2,1)S(1)}, bf16[512,128]{1,0:T(8,128)(2,1)S(1)}, u32[]{:S(2)}, u32[]{:S(2)}) collective-permute-start(bf16[512,128]{1,0:T(8,128)(2,1)S(1)} %copy-done.26), channel_id=1, source_target_pairs={{0,2},{1,3},{2,0},{3,1},{4,6},{5,7},{6,4},{7,5},{8,10},{9,11},{10,... | collective-permute-start | bytes 393224 | tf_op jit(solution)/shard_map/ppermute | solution.py:322
  109.8 7.7 %copy-start.15 = (bf16[512,128]{1,0:T(8,128)(2,1)}, bf16[512,128]{1,0:T(8,128)(2,1)S(1)}, u32[]{:S(2)}) copy-start(bf16[512,128]{1,0:T(8,128)(2,1)S(1)} %collective-permute-done.18.refs_1_) | copy-start | bytes 393220
  109.8 7.7 %collective-permute-start.23 = (bf16[512,128]{1,0:T(8,128)(2,1)S(1)}, bf16[512,128]{1,0:T(8,128)(2,1)S(1)}, u32[]{:S(2)}, u32[]{:S(2)}) collective-permute-start(bf16[512,128]{1,0:T(8,128)(2,1)S(1)} %copy-done.25), channel_id=1, source_target_pairs={{0,3},{1,2},{2,1},{3,0},{4,7},{5,6},{6,5},{7,4},{8,11},{9,10},{10,... | collective-permute-start | bytes 393224 | tf_op jit(solution)/shard_map/ppermute | solution.py:322
  112.6 4.9 %copy-start.16 = (bf16[512,128]{1,0:T(8,128)(2,1)}, bf16[512,128]{1,0:T(8,128)(2,1)S(1)}, u32[]{:S(2)}) copy-start(bf16[512,128]{1,0:T(8,128)(2,1)S(1)} %collective-permute-done.19.refs_2_) | copy-start | bytes 393220
  112.6 23.0 %collective-permute-start.11 = (f32[32,512]{1,0:T(8,128)S(1)}, f32[32,512]{1,0:T(8,128)S(1)}, u32[]{:S(2)}, u32[]{:S(2)}) collective-permute-start(f32[32,512]{1,0:T(8,128)S(1)} %get-tuple-element.67), channel_id=1, source_target_pairs={{0,3},{1,2},{2,1},{3,0},{4,7},{5,6},{6,5},{7,4},{8,11},{9,10},{10,... | collective-permute-start | bytes 196616 | tf_op jit(solution)/shard_map/ppermute | solution.py:322
  113.8 3.7 %copy-start.17 = (bf16[512,128]{1,0:T(8,128)(2,1)}, bf16[512,128]{1,0:T(8,128)(2,1)S(1)}, u32[]{:S(2)}) copy-start(bf16[512,128]{1,0:T(8,128)(2,1)S(1)} %collective-permute-done.20.refs_3_) | copy-start | bytes 393220
  113.8 21.9 %collective-permute-start.10 = (f32[32,512]{1,0:T(8,128)S(1)}, f32[32,512]{1,0:T(8,128)S(1)}, u32[]{:S(2)}, u32[]{:S(2)}) collective-permute-start(f32[32,512]{1,0:T(8,128)S(1)} %get-tuple-element.68), channel_id=1, source_target_pairs={{0,2},{1,3},{2,0},{3,1},{4,6},{5,7},{6,4},{7,5},{8,10},{9,11},{10,... | collective-permute-start | bytes 196616 | tf_op jit(solution)/shard_map/ppermute | solution.py:322
  116.0 19.6 %collective-permute-start.9 = (f32[32,512]{1,0:T(8,128)S(1)}, f32[32,512]{1,0:T(8,128)S(1)}, u32[]{:S(2)}, u32[]{:S(2)}) collective-permute-start(f32[32,512]{1,0:T(8,128)S(1)} %get-tuple-element.66), channel_id=1, source_target_pairs={{0,1},{1,0},{2,3},{3,2},{4,5},{5,4},{6,7},{7,6},{8,9},{9,8},{10,11... | collective-permute-start | bytes 196616 | tf_op jit(solution)/shard_map/ppermute | solution.py:322
  132.1 14.9 %all-to-all-start.4 = ((bf16[8,256,128]{2,1,0:T(8,128)(2,1)}), bf16[8,256,128]{2,1,0:T(8,128)(2,1)S(1)}, u32[]{:S(2)}, u32[]{:S(2)}) async-start(bf16[8,256,128]{2,1,0:T(8,128)(2,1)} %bitcast.16), calls=%async_computation.4 | async-start | bytes 1048576 | tf_op jit(solution)/shard_map/all_to_all | solution.py:333
  135.6 16.8 %copy-start.24 = (bf16[1024,128]{1,0:T(8,128)(2,1)S(1)}, bf16[1024,128]{1,0:T(8,128)(2,1)}, u32[]{:S(2)}) copy-start(bf16[1024,128]{1,0:T(8,128)(2,1)} %get-tuple-element.45) | copy-start | bytes 786436
  135.6 18.7 %copy-start.23 = (bf16[1024,128]{1,0:T(8,128)(2,1)S(1)}, bf16[1024,128]{1,0:T(8,128)(2,1)}, u32[]{:S(2)}) copy-start(bf16[1024,128]{1,0:T(8,128)(2,1)} %get-tuple-element.46) | copy-start | bytes 786436
  135.6 20.0 %copy-start.22 = (bf16[1024,128]{1,0:T(8,128)(2,1)S(1)}, bf16[1024,128]{1,0:T(8,128)(2,1)}, u32[]{:S(2)}) copy-start(bf16[1024,128]{1,0:T(8,128)(2,1)} %get-tuple-element.47) | copy-start | bytes 786436
  135.7 7.0 %collective-permute-start.12 = (bf16[32,512]{1,0:T(8,128)(2,1)S(1)}, bf16[32,512]{1,0:T(8,128)(2,1)S(1)}, u32[]{:S(2)}, u32[]{:S(2)}) collective-permute-start(bf16[32,512]{1,0:T(8,128)(2,1)S(1)} %get-tuple-element.59), channel_id=1, source_target_pairs={{0,1},{1,0},{2,3},{3,2},{4,5},{5,4},{6,7},{7,6},{8,9},{9,8},{10,11... | collective-permute-start | bytes 98312 | tf_op jit(solution)/shard_map/ppermute | solution.py:322
  139.9 5.0 %collective-permute-start.13 = (bf16[32,512]{1,0:T(8,128)(2,1)S(1)}, bf16[32,512]{1,0:T(8,128)(2,1)S(1)}, u32[]{:S(2)}, u32[]{:S(2)}) collective-permute-start(bf16[32,512]{1,0:T(8,128)(2,1)S(1)} %get-tuple-element.59), channel_id=1, source_target_pairs={{0,2},{1,3},{2,0},{3,1},{4,6},{5,7},{6,4},{7,5},{8,10},{9,11},{10,... | collective-permute-start | bytes 98312 | tf_op jit(solution)/shard_map/ppermute | solution.py:322
  141.3 5.7 %collective-permute-start.14 = (bf16[32,512]{1,0:T(8,128)(2,1)S(1)}, bf16[32,512]{1,0:T(8,128)(2,1)S(1)}, u32[]{:S(2)}, u32[]{:S(2)}) collective-permute-start(bf16[32,512]{1,0:T(8,128)(2,1)S(1)} %get-tuple-element.59), channel_id=1, source_target_pairs={{0,3},{1,2},{2,1},{3,0},{4,7},{5,6},{6,5},{7,4},{8,11},{9,10},{10,... | collective-permute-start | bytes 98312 | tf_op jit(solution)/shard_map/ppermute | solution.py:322
  147.0 28.6 %copy-start.5 = (bf16[8,256,128]{2,1,0:T(8,128)(2,1)}, bf16[8,256,128]{2,1,0:T(8,128)(2,1)S(1)}, u32[]{:S(2)}) copy-start(bf16[8,256,128]{2,1,0:T(8,128)(2,1)S(1)} %all-to-all-done.4) | copy-start | bytes 1572868
  148.2 32.3 %all-to-all-start.3 = ((bf16[8,128,512]{2,1,0:T(8,128)(2,1)}), bf16[8,128,512]{2,1,0:T(8,128)(2,1)S(1)}, u32[]{:S(2)}, u32[]{:S(2)}) async-start(bf16[8,128,512]{2,1,0:T(8,128)(2,1)} %broadcast_in_dim.10), calls=%async_computation.3 | async-start | bytes 2097152 | tf_op jit(solution)/shard_map/all_to_all | solution.py:333
  152.4 13.9 %collective-permute-start.15 = (bf16[1024,128]{1,0:T(8,128)(2,1)S(1)}, bf16[1024,128]{1,0:T(8,128)(2,1)S(1)}, u32[]{:S(2)}, u32[]{:S(2)}) collective-permute-start(bf16[1024,128]{1,0:T(8,128)(2,1)S(1)} %copy-done.24), channel_id=1, source_target_pairs={{0,1},{1,0},{2,3},{3,2},{4,5},{5,4},{6,7},{7,6},{8,9},{9,8},{10,11... | collective-permute-start | bytes 786440 | tf_op jit(solution)/shard_map/ppermute | solution.py:322
  154.3 21.4 %collective-permute-start.16 = (bf16[1024,128]{1,0:T(8,128)(2,1)S(1)}, bf16[1024,128]{1,0:T(8,128)(2,1)S(1)}, u32[]{:S(2)}, u32[]{:S(2)}) collective-permute-start(bf16[1024,128]{1,0:T(8,128)(2,1)S(1)} %copy-done.23), channel_id=1, source_target_pairs={{0,2},{1,3},{2,0},{3,1},{4,6},{5,7},{6,4},{7,5},{8,10},{9,11},{10,... | collective-permute-start | bytes 786440 | tf_op jit(solution)/shard_map/ppermute | solution.py:322
  155.6 20.0 %collective-permute-start.17 = (bf16[1024,128]{1,0:T(8,128)(2,1)S(1)}, bf16[1024,128]{1,0:T(8,128)(2,1)S(1)}, u32[]{:S(2)}, u32[]{:S(2)}) collective-permute-start(bf16[1024,128]{1,0:T(8,128)(2,1)S(1)} %copy-done.22), channel_id=1, source_target_pairs={{0,3},{1,2},{2,1},{3,0},{4,7},{5,6},{6,5},{7,4},{8,11},{9,10},{10,... | collective-permute-start | bytes 786440 | tf_op jit(solution)/shard_map/ppermute | solution.py:322
  166.3 9.3 %copy-start.12 = (bf16[1024,128]{1,0:T(8,128)(2,1)}, bf16[1024,128]{1,0:T(8,128)(2,1)S(1)}, u32[]{:S(2)}) copy-start(bf16[1024,128]{1,0:T(8,128)(2,1)S(1)} %collective-permute-done.15.refs_1_) | copy-start | bytes 786436
  (11 other events, 8.5 us)

commit v2 on v1

v2 whole, which is shorter than its diff:
```python
import math

import jax
import jax.numpy as jnp
from jax import lax
from jax.experimental import pallas as pl
from jax.experimental.pallas import tpu as pltpu
from jax.sharding import PartitionSpec as P


BF16, F32 = jnp.bfloat16, jnp.float32
CHUNKS = 2
VMEM_LIMIT = 56 * 1024 * 1024


def params(dims):
    return pltpu.CompilerParams(
        dimension_semantics=("arbitrary",) * dims, vmem_limit_bytes=VMEM_LIMIT
    )


def full(shape):
    return pl.BlockSpec(shape, lambda *_: (0,) * len(shape))


def rows_at(index, tile):
    return pl.ds(pl.multiple_of(index * tile, tile), tile)


SMEM = pl.BlockSpec(memory_space=pltpu.SMEM)
ANY = pl.BlockSpec(memory_space=pl.ANY)


def id_rows(refs):
    rows = []
    for ref in refs:
        rows += [(ref, j) for j in range(ref.shape[0])]
    return rows


def select_tiles(row, ids, feats, tile, cap):
    count, width = sum(a.shape[0] for a in ids), feats.shape[1]

    def kernel(row_ref, *refs):
        id_refs, feats_ref = refs[: len(ids)], refs[len(ids)]
        outs, sems = refs[len(ids) + 1 : -1], refs[-1]
        where = id_rows(id_refs)
        copies = []
        for k in range(1, count):
            ref, j = where[k]
            for s in range(cap):
                source = jnp.maximum(ref[j, row_ref[0] * cap + s], 0)
                copies.append(
                    pltpu.make_async_copy(
                        feats_ref.at[rows_at(source, tile)],
                        outs[k - 1].at[s * tile : (s + 1) * tile],
                        sems.at[(k - 1) * cap + s],
                    )
                )
                copies[-1].start()
        for copy in copies:
            copy.wait()

    return pl.pallas_call(
        kernel,
        out_shape=[jax.ShapeDtypeStruct((cap * tile, width), feats.dtype)] * (count - 1),
        grid=(1,),
        in_specs=[SMEM] * (1 + len(ids)) + [ANY],
        out_specs=[full((cap * tile, width))] * (count - 1),
        scratch_shapes=[pltpu.SemaphoreType.DMA(((count - 1) * cap,))],
        name="select_tiles",
    )(row, *ids, feats)


def aggregate(col, colref, feats, arrived, adj, chunk, parts):
    blocks, per_block, tile, _ = adj.shape
    width = feats.shape[1]
    own = feats.shape[0]
    step = arrived[0].shape[0]
    count = len(arrived)
    per_part = blocks // parts
    per_chunk = per_part // CHUNKS
    chunk_rows = per_chunk * tile

    def tile_of(k, t, col_ref):
        return (k ^ col_ref[0]) * per_part + chunk * per_chunk + t

    def kernel(col_ref, colref_ref, feats_ref, *refs):
        arrived_refs, refs = refs[:count], refs[count:]
        adj_refs, outs, pool = refs[:parts], refs[parts : 2 * parts], refs[-1]
        t = pl.program_id(0)

        @pl.when(t == 0)
        def _():
            pool[:own, :] = feats_ref[...]
            for n, ref in enumerate(arrived_refs):
                pool[own + (n + 1) * step : own + (n + 2) * step, :] = ref[...]

        for k in range(parts):
            b = tile_of(k, t, col_ref)
            right = jnp.concatenate(
                [pool[rows_at(colref_ref[b, q], tile), :] for q in range(per_block)], axis=0
            )
            left = jnp.concatenate([adj_refs[k][0, q] for q in range(per_block)], axis=1)
            outs[k][...] = jnp.dot(left, right, preferred_element_type=F32).astype(BF16)

    def adj_spec(k):
        return pl.BlockSpec(
            (1, per_block, tile, tile), lambda t, c, r: (tile_of(k, t, c), 0, 0, 0)
        )

    return pl.pallas_call(
        kernel,
        out_shape=[jax.ShapeDtypeStruct((chunk_rows, width), BF16)] * parts,
        grid_spec=pltpu.PrefetchScalarGridSpec(
            num_scalar_prefetch=2,
            grid=(per_chunk,),
            in_specs=[full(feats.shape)]
            + [full(a.shape) for a in arrived]
            + [adj_spec(k) for k in range(parts)],
            out_specs=[pl.BlockSpec((tile, width), lambda t, c, r: (t, 0))] * parts,
            scratch_shapes=[pltpu.VMEM((own + (count + 1) * step, width), BF16)],
        ),
        compiler_params=params(1),
        name="aggregate",
    )(col, colref, feats, *arrived, *[adj] * parts)


def permuted(w_ref, col_ref, parts, width):
    return jnp.concatenate(
        [w_ref[rows_at(k ^ col_ref[0], width), :] for k in range(parts)], axis=0
    )


NT = (((1,), (1,)), ((), ()))
TN = (((0,), (0,)), ((), ()))


def dense(col, feat_rows, agg_parts, w_self, w_neigh, grad_out, act_prev, chunk):
    parts = len(agg_parts)
    chunk_rows, width = agg_parts[0].shape
    hidden = w_self.shape[1]
    steps = 2
    rows = chunk_rows // steps
    root = math.sqrt(2.0 / math.pi)

    def kernel(col_ref, *refs):
        f_ref, a_refs = refs[0], refs[1 : 1 + parts]
        ws_ref, wn_ref, go_ref = refs[1 + parts : 4 + parts]
        outs = refs[4 + parts + (act_prev is not None) :]
        act_ref, g_ref, back = outs[0], outs[1], outs[2:]
        ws = ws_ref[...]
        wn = permuted(wn_ref, col_ref, parts, width)
        f = jnp.concatenate([f_ref[j] for j in range(parts)], axis=1)
        a = jnp.concatenate([r[...] for r in a_refs], axis=1)
        v = jnp.dot(f, ws, preferred_element_type=F32) + jnp.dot(a, wn, preferred_element_type=F32)
        square = v * v
        tanh = jnp.tanh(root * (v + 0.044715 * (square * v)))
        half = 0.5 * (1.0 + tanh)
        act_ref[...] = (v * half).astype(BF16)
        slope = half + 0.5 * v * (1.0 - tanh * tanh) * (root * (1.0 + 3 * 0.044715 * square))
        g = (go_ref[...].astype(F32) * slope).astype(BF16)
        g_ref[...] = g
        spread = lax.dot_general(g, wn, NT, preferred_element_type=F32).astype(BF16)
        for k, out in enumerate(back):
            out[...] = spread[:, k * width : (k + 1) * width]

    offset = chunk * steps
    in_specs = (
        [pl.BlockSpec((parts, rows, width), lambda i, c: (0, offset + i, 0))]
        + [pl.BlockSpec((rows, width), lambda i, c: (i, 0))] * parts
        + [full(w_self.shape), full(w_neigh.shape)]
        + [pl.BlockSpec((rows, hidden), lambda i, c: (offset + i, 0))]
    )
    args = [col, feat_rows, *agg_parts, w_self, w_neigh, grad_out]
    aliases = {}
    if act_prev is not None:
        in_specs.append(pl.BlockSpec(memory_space=pl.ANY))
        aliases = {len(args): 0}
        args.append(act_prev)
    return pl.pallas_call(
        kernel,
        out_shape=[
            jax.ShapeDtypeStruct((chunk_rows * CHUNKS, hidden), BF16),
            jax.ShapeDtypeStruct((chunk_rows, hidden), BF16),
        ]
        + [jax.ShapeDtypeStruct((chunk_rows, width), BF16)] * parts,
        grid_spec=pltpu.PrefetchScalarGridSpec(
            num_scalar_prefetch=1,
            grid=(steps,),
            in_specs=in_specs,
            out_specs=[
                pl.BlockSpec((rows, hidden), lambda i, c: (offset + i, 0)),
                pl.BlockSpec((rows, hidden), lambda i, c: (i, 0)),
            ]
            + [pl.BlockSpec((rows, width), lambda i, c: (i, 0))] * parts,
        ),
        input_output_aliases=aliases,
        compiler_params=params(1),
        name="dense",
    )(*args)


def weights(col, row, feat_rows, agg_chunks, grads, w_self):
    parts, rows, width = feat_rows.shape
    hidden = w_self.shape[1]

    def kernel(col_ref, row_ref, *refs):
        f_ref, refs = refs[0], refs[1:]
        a_refs, refs = refs[: parts * CHUNKS], refs[parts * CHUNKS :]
        g_refs, ws_ref = refs[:CHUNKS], refs[CHUNKS]
        keep_ref, send_ref, *s_refs = refs[CHUNKS + 1 :]
        g = jnp.concatenate([r[...] for r in g_refs], axis=0)
        ws = permuted(ws_ref, col_ref, parts, width)
        s = lax.dot_general(g, ws, NT, preferred_element_type=F32).astype(BF16)
        for k, out in enumerate(s_refs):
            out[...] = s[:, k * width : (k + 1) * width]

        def emit(self_ref, neigh_ref):
            g = jnp.concatenate([r[...] for r in g_refs], axis=0)
            for k in range(parts):
                self_ref[k * width : (k + 1) * width, :] = lax.dot_general(
                    f_ref[k], g, TN, preferred_element_type=F32
                )
                a = jnp.concatenate([a_refs[h * parts + k][...] for h in range(CHUNKS)], axis=0)
                neigh_ref[rows_at(k ^ col_ref[0], width), :] = lax.dot_general(
                    a, g, TN, preferred_element_type=F32
                )

        even = row_ref[0] % 2 == 0
        pl.when(even)(lambda: emit(keep_ref, send_ref))
        pl.when(jnp.logical_not(even))(lambda: emit(send_ref, keep_ref))

    args = [feat_rows, *[a for chunk in agg_chunks for a in chunk], *grads, w_self]
    out_shape = [jax.ShapeDtypeStruct((parts * width, hidden), F32)] * 2 + [
        jax.ShapeDtypeStruct((rows, width), BF16)
    ] * parts
    return pl.pallas_call(
        kernel,
        out_shape=out_shape,
        grid_spec=pltpu.PrefetchScalarGridSpec(
            num_scalar_prefetch=2,
            grid=(1,),
            in_specs=[full(a.shape) for a in args],
            out_specs=[full(o.shape) for o in out_shape],
        ),
        compiler_params=params(1),
        name="weights",
    )(col, row, *args)


def combine(row, keep, received, chips):
    total, hidden = keep.shape
    rows = total // chips

    def kernel(row_ref, keep_ref, received_ref, *outs):
        for q, out in enumerate(outs):
            at = rows_at((row_ref[0] // 2) ^ q, rows)
            out[...] = keep_ref[at, :] + received_ref[at, :]

    return pl.pallas_call(
        kernel,
        out_shape=[jax.ShapeDtypeStruct((rows, hidden), F32)] * chips,
        grid_spec=pltpu.PrefetchScalarGridSpec(
            num_scalar_prefetch=1,
            grid=(1,),
            in_specs=[full(keep.shape)] * 2,
            out_specs=[full((rows, hidden))] * chips,
        ),
        compiler_params=params(1),
        name="combine",
    )(row, keep, received)


def assemble(row, pieces):
    rows, hidden = pieces[0].shape
    chips = len(pieces)

    def kernel(row_ref, *refs):
        for q in range(chips):
            refs[-1][rows_at((row_ref[0] // 2) ^ q, rows), :] = refs[q][...]

    return pl.pallas_call(
        kernel,
        out_shape=jax.ShapeDtypeStruct((chips * rows, hidden), BF16),
        grid_spec=pltpu.PrefetchScalarGridSpec(
            num_scalar_prefetch=1,
            grid=(1,),
            in_specs=[full((rows, hidden))] * chips,
            out_specs=full((chips * rows, hidden)),
        ),
        compiler_params=params(1),
        name="assemble",
    )(row, *pieces)


def widen(row, mine, other):
    def kernel(row_ref, mine_ref, other_ref, self_ref, neigh_ref):
        even = row_ref[0] % 2 == 0
        first, second = mine_ref[...].astype(F32), other_ref[...].astype(F32)
        self_ref[...] = jnp.where(even, first, second)
        neigh_ref[...] = jnp.where(even, second, first)

    return pl.pallas_call(
        kernel,
        out_shape=[jax.ShapeDtypeStruct(mine.shape, F32)] * 2,
        grid_spec=pltpu.PrefetchScalarGridSpec(
            num_scalar_prefetch=1,
            grid=(1,),
            in_specs=[full(mine.shape)] * 2,
            out_specs=[full(mine.shape)] * 2,
        ),
        compiler_params=params(1),
        name="widen",
    )(row, mine, other)


def pull(col, colref, grads, adj, partitions, cap, chunk, before):
    blocks, per_block, tile, _ = adj.shape
    parts = len(grads)
    _, width = grads[0].shape
    per_part = blocks // parts
    steps = per_part // CHUNKS
    last = chunk == CHUNKS - 1
    pool = blocks + partitions * cap
    extra = [] if before is None else [before]

    def kernel(col_ref, colref_ref, *refs):
        g_refs, adj_refs = refs[:parts], refs[parts : 2 * parts]
        refs = refs[2 * parts :]
        before_ref = refs[: len(extra)]
        outs, acc, sem = refs[len(extra) : -2], refs[-2], refs[-1]
        t = pl.program_id(0)

        @pl.when(t == 0)
        def _():
            if extra:
                copy = pltpu.make_async_copy(before_ref[0], acc, sem)
                copy.start()
                copy.wait()
            else:
                acc[...] = jnp.zeros_like(acc)

        for k in range(parts):
            b = (k ^ col_ref[0]) * per_part + chunk * steps + t
            turned = g_refs[k][rows_at(t, tile), :].T
            for q in range(0, per_block, 2):
                pair = jnp.concatenate([adj_refs[k][0, q], adj_refs[k][0, q + 1]], axis=1)
                both = jnp.dot(turned, pair, preferred_element_type=F32)
                acc[colref_ref[b, q]] += both[:, :tile]
                acc[colref_ref[b, q + 1]] += both[:, tile:]

        @pl.when(t == steps - 1)
        def _():
            if last:
                for n, out in enumerate(outs):
                    first = blocks + n * cap if n else 0
                    for s in range(out.shape[0] // tile):
                        out[s * tile : (s + 1) * tile, :] = acc[first + s].T.astype(BF16)
            else:
                copy = pltpu.make_async_copy(acc, outs[0], sem)
                copy.start()
                copy.wait()

    def adj_spec(k):
        return pl.BlockSpec(
            (1, per_block, tile, tile),
            lambda t, c, r: ((k ^ c[0]) * per_part + chunk * steps + t, 0, 0, 0),
        )

    if last:
        out_shape = [jax.ShapeDtypeStruct((blocks * tile, width), BF16)]
        out_shape += [jax.ShapeDtypeStruct((cap * tile, width), BF16)] * (partitions - 1)
        out_specs = [full(o.shape) for o in out_shape]
    else:
        out_shape = [jax.ShapeDtypeStruct((pool, width, tile), F32)]
        out_specs = [ANY]
    return pl.pallas_call(
        kernel,
        out_shape=out_shape,
        grid_spec=pltpu.PrefetchScalarGridSpec(
            num_scalar_prefetch=2,
            grid=(steps,),
            in_specs=[full(g.shape) for g in grads]
            + [adj_spec(k) for k in range(parts)]
            + [ANY] * len(extra),
            out_specs=out_specs,
            scratch_shapes=[
                pltpu.VMEM((pool, width, tile), F32),
                pltpu.SemaphoreType.DMA(()),
            ],
        ),
        compiler_params=params(1),
        name="pull",
    )(col, colref, *grads, *[adj] * parts, *extra)


def finish(col, row, ids, self_parts, local, returned, tile, cap):
    parts = len(self_parts)
    rows, _ = self_parts[0].shape
    count = len(returned)

    def kernel(col_ref, row_ref, *refs):
        id_refs, refs = refs[: len(ids)], refs[len(ids) :]
        s_refs, local_ref = refs[:parts], refs[parts]
        returned_refs, out_ref = refs[parts + 1 : -1], refs[-1]
        where = id_rows(id_refs)
        for k in range(parts):
            at = rows_at(k ^ col_ref[0], rows)
            out_ref[at, :] = s_refs[k][...].astype(F32) + local_ref[at, :].astype(F32)
        for n in range(count):
            ref, j = where[n + 1]
            for s in range(cap):
                target = ref[j, row_ref[0] * cap + s]

                @pl.when(target >= 0)
                def _():
                    out_ref[rows_at(target, tile), :] += returned_refs[n][
                        s * tile : (s + 1) * tile, :
                    ].astype(F32)

    args = [*self_parts, local, *returned]
    return pl.pallas_call(
        kernel,
        out_shape=jax.ShapeDtypeStruct(local.shape, F32),
        grid_spec=pltpu.PrefetchScalarGridSpec(
            num_scalar_prefetch=2,
            grid=(1,),
            in_specs=[SMEM] * len(ids) + [full(a.shape) for a in args],
            out_specs=full(local.shape),
        ),
        compiler_params=params(1),
        name="finish",
    )(col, row, *ids, *args)


def swap(x, axis, k):
    n = lax.axis_size(axis)
    return lax.ppermute(x, axis, [(i, i ^ k) for i in range(n)])


def exchange(pieces, axis, stride=1):
    out = [pieces[0]]
    for k in range(1, len(pieces)):
        out.append(swap(pieces[k], axis, k * stride))
    return out


def tree_sum(parts):
    while len(parts) > 1:
        parts = [parts[n] + parts[n + 1] for n in range(0, len(parts), 2)]
    return parts[0]


def body(feats, adj_vals, colref, fetch_ids, w_self, w_neigh, grad_out):
    node_rows, width = feats.shape
    blocks, _, tile, _ = adj_vals.shape
    partitions = lax.axis_size("rows")
    parts = lax.axis_size("cols")
    cap = fetch_ids.shape[2]
    chips = partitions // 2
    total_nodes = node_rows * partitions
    row_index, col_index = lax.axis_index("rows"), lax.axis_index("cols")
    col = col_index.astype(jnp.int32).reshape(1)
    row = row_index.astype(jnp.int32).reshape(1)

    feat_rows = lax.all_to_all(
        feats.reshape(parts, node_rows // parts, width), "cols", 0, 0, tiled=True
    )
    known = fetch_ids.reshape(1, partitions * cap)
    known = jnp.pad(known, ((0, 0), (0, -known.shape[1] % 128)))
    ids, hop = [known], 1
    while hop < partitions:
        ids.append(swap(known, "rows", hop))
        known = jnp.concatenate([known, ids[-1]], axis=0)
        hop *= 2
    outgoing = select_tiles(row, ids, feats, tile, cap)
    arrived = exchange([None, *outgoing], "rows")[1:]
    slot = jnp.maximum(colref - blocks, 0)
    slot = ((slot // cap) ^ row_index) * cap + slot % cap
    places = jnp.where(colref < blocks, colref, blocks + slot).astype(jnp.int32)

    agg_chunks = []
    for h in range(CHUNKS):
        pieces = aggregate(col, places, feats, arrived, adj_vals, h, parts)
        agg_chunks.append(exchange(pieces, "cols"))
    act, grads, grad_chunks = None, [], []
    for h in range(CHUNKS):
        act, g, *back = dense(
            col, feat_rows, agg_chunks[h], w_self, w_neigh, grad_out, act, h
        )
        grads.append(g)
        grad_chunks.append(exchange(back, "cols"))
    keep, send, *self_rows = weights(col, row, feat_rows, agg_chunks, grads, w_self)
    self_parts = exchange(self_rows, "cols")

    received = exchange([keep, send], "rows")[1]
    pieces = combine(row, keep, received, chips)
    partial = tree_sum(exchange(pieces, "rows", 2)).astype(BF16)
    mine = tree_sum([p.astype(F32) for p in exchange([partial] * parts, "cols")])
    mine = (mine * (1.0 / math.sqrt(total_nodes))).astype(BF16)
    half = assemble(row, exchange([mine] * chips, "rows", 2))
    grad_self_w, grad_neigh_w = widen(row, half, exchange([half, half], "rows")[1])

    before = None
    for h in range(CHUNKS):
        before, *remote = pull(col, places, grad_chunks[h], adj_vals, partitions, cap, h, before)
    returned = exchange([None, *remote], "rows")[1:]
    grad_feats = finish(col, row, ids, self_parts, before, returned, tile, cap)
    return (act, grad_self_w, grad_neigh_w, grad_feats)


def solution(mesh):
    in_specs = (
        P("rows", "cols"),
        P("rows", None, None, None),
        P("rows", None),
        P("rows", None, None),
        P(),
        P(),
        P(("rows", "cols"), None),
    )
    out_specs = (P(("rows", "cols"), None), P(), P(), P("rows", "cols"))
    return jax.shard_map(body, mesh=mesh, in_specs=in_specs, out_specs=out_specs, check_vma=False)
```

time: 186 us -> 192 us (1.032)
  Pallas kernels: 50 us -> 62.3 us
  blocking collectives: 9.67 us -> 0 us
  starting transfers between devices: 55.7 us -> 58.8 us
    ppermute x24 -> x43, waiting for transfers between devices: 33.1 us -> 55.8 us  [swap(): return lax.ppermute(x, axis, [(i, i ^ k) for i in range(n)])]
    all_to_all x4 -> x1, waiting for transfers between devices: 21.8 us -> 0.01 us  [body(): lax.all_to_all(feats.reshape(parts, node_rows // parts, width), 'cols', 0...]
    pallas_call x2 -> x6, Pallas kernels: 16.8 us -> 29.3 us  [the longest x2 19.5 us: pull(): pl.pallas_call(kernel, out_shape=out_shape, grid_spec=pltpu.PrefetchScala...]
    ppermute x24 -> x43, starting transfers between devices: 40.8 us -> 52.5 us  [swap(): return lax.ppermute(x, axis, [(i, i ^ k) for i in range(n)])]
    all_to_all x1 -> x0, blocking collectives: 9.67 us -> none  [across_rows(): return lax.all_to_all(x, 'rows', split_axis=0, concat_axis=0, tiled=True)]
    all_to_all x4 -> x1, starting transfers between devices: 14.9 us -> 6.36 us  [body(): lax.all_to_all(feats.reshape(parts, node_rows // parts, width), 'cols', 0...]
    unnamed x63 -> x102, local copies, waits for them, and re-layouts: 4.32 us -> 8.93 us
  transfers between devices with their start and end apart: 28 -> 44, of which waited for: 8 -> 19; matrix products, arithmetic and copies ran while one was open for 1% -> 1% of each run, Pallas kernels for 21% -> 25%
where the time goes in v2:
time: 192 us; the launch traced here: 189 us
  Pallas kernels  62.3 us (32%)
  starting transfers between devices  58.8 us (31%)
  waiting for transfers between devices  55.8 us (29%)
  local copies, waits for them, and re-layouts  9.02 us (5%)
    ppermute x43, waiting for transfers between devices, swap(): return lax.ppermute(x, axis, [(i, i ^ k) for i in range(n)])  55.8 us
    ppermute x43, starting transfers between devices, swap(): return lax.ppermute(x, axis, [(i, i ^ k) for i in range(n)])  52.5 us
    pallas_call x2, Pallas kernels, pull(): pl.pallas_call(kernel, out_shape=out_shape, grid_spec=pltpu.PrefetchScala...  19.5 us
    pallas_call x2, Pallas kernels, aggregate(): pl.pallas_call(kernel, out_shape=[jax.ShapeDtypeStruct((chunk_rows, width...  15.4 us
    unnamed x102, local copies, waits for them, and re-layouts  8.93 us
    pallas_call x2, Pallas kernels, dense(): pl.pallas_call(kernel, out_shape=[jax.ShapeDtypeStruct((chunk_rows * CHUN...  8.25 us
    all_to_all x1, starting transfers between devices, body(): lax.all_to_all(feats.reshape(parts, node_rows // parts, width), 'cols', 0...  6.36 us
    pallas_call x1, Pallas kernels, weights(): pl.pallas_call(kernel, out_shape=out_shape, grid_spec=pltpu.PrefetchScala...  5.98 us
  transfers between devices with their start and end apart: 44, of which 19 were waited for; matrix products, arithmetic and copies ran while one was open for 1% of the time, Pallas kernels for 25%

profile of v2, /device:TPU:0, one launch (start us, length us, event | category | flops | bytes accessed | tf_op | source)
XLA Modules:
  0.0 188.9 jit_solution(4810113044436825173)
XLA Ops:
  0.6 6.4 %all-to-all-start = ((bf16[4,1024,128]{2,1,0:T(8,128)(2,1)}), bf16[4,1024,128]{2,1,0:T(8,128)(2,1)S(1)}, u32[]{:S(2)}, u32[]{:S(2)}) async-start(bf16[4,1024,128]{2,1,0:T(8,128)(2,1)} %bitcast.3), calls=%async_computation | async-start | bytes 2097152 | tf_op jit(solution)/shard_map/all_to_all | solution.py:467
  9.1 1.6 collective-permute-start.1
  10.6 2.1 %collective-permute-done.1.refs_2_ = s32[2,128]{1,0:T(2,128)S(1)} collective-permute-done((s32[2,128]{1,0:T(2,128)S(1)}, s32[2,128]{1,0:T(2,128)S(1)}, u32[]{:S(2)}, u32[]{:S(2)}) %collective-permute-start.1) | collective-permute-done | bytes 1056 | tf_op jit(solution)/shard_map/ppermute | solution.py:439
  12.7 1.6 collective-permute-start.2
  14.3 2.1 %collective-permute-done.2.refs_3_ = s32[4,128]{1,0:T(4,128)S(1)} collective-permute-done((s32[4,128]{1,0:T(4,128)S(1)}, s32[4,128]{1,0:T(4,128)S(1)}, u32[]{:S(2)}, u32[]{:S(2)}) %collective-permute-start.2) | collective-permute-done | bytes 2080 | tf_op jit(solution)/shard_map/ppermute | solution.py:439
  17.0 2.6 %select_tiles.1 = (bf16[256,128]{1,0:T(8,128)(2,1)}, bf16[256,128]{1,0:T(8,128)(2,1)}, bf16[256,128]{1,0:T(8,128)(2,1)}, bf16[256,128]{1,0:T(8,128)(2,1)}, bf16[...) custom-call(s32[1]{0:T(128)} %bitcast.2.row_ref, s32[1,128]{1,0:T(1,128)} %copy-done.38, ...), custom_call_target="tpu_custom_call" | custom-call | tf_op jit(solution)/shard_map/select_tiles/pallas_call | solution.py:64
  19.7 1.5 collective-permute-start.4
  23.4 2.4 %collective-permute-start.8 = (bf16[256,128]{1,0:T(8,128)(2,1)}, bf16[256,128]{1,0:T(8,128)(2,1)S(1)}, u32[]{:S(2)}, u32[]{:S(2)}) collective-permute-start(bf16[256,128]{1,0:T(8,128)(2,1)} %get-tuple-element.56), channel_id=1, source_target_pairs={{0,24},{4,28},{8,16},{12,20},{16,8},{20,12},{24,0},{28,4},{1,25},{... | collective-permute-start | bytes 196616 | tf_op jit(solution)/shard_map/ppermute | solution.py:439
  27.4 1.6 collective-permute-done.8.refs_5_
  29.0 1.9 %collective-permute-done.9.refs_6_ = bf16[256,128]{1,0:T(8,128)(2,1)S(1)} collective-permute-done((bf16[256,128]{1,0:T(8,128)(2,1)}, bf16[256,128]{1,0:T(8,128)(2,1)S(1)}, u32[]{:S(2)}, u32[]{:S(2)}) %collective-permute-start.9) | collective-permute-done | bytes 65568 | tf_op jit(solution)/shard_map/ppermute | solution.py:439
  31.5 7.7 %aggregate.3 = (bf16[512,128]{1,0:T(8,128)(2,1)}, bf16[512,128]{1,0:T(8,128)(2,1)}, bf16[512,128]{1,0:T(8,128)(2,1)}, bf16[512,128]{1,0:T(8,128)(2,1)}) custom-call(s32[1]{0:T(128)} %bitcast.col_ref, s32[32,16]{1,0:T(8,128)} %compare_select_fusion.colref_ref, bf16[4096,128]{1,0:T(8,128)(2,1)} %feats_ref.3, bf16[256,128]{1,0:T(8,128)(2,1)} %copy-done.10, ...), custom_call_target="tpu_custom_call" | custom-call | tf_op jit(solution)/shard_map/aggregate/pallas_call | solution.py:112
  39.2 2.1 %collective-permute-start.13 = (bf16[512,128]{1,0:T(8,128)(2,1)}, bf16[512,128]{1,0:T(8,128)(2,1)S(1)}, u32[]{:S(2)}, u32[]{:S(2)}) collective-permute-start(bf16[512,128]{1,0:T(8,128)(2,1)} %get-tuple-element.63), channel_id=1, source_target_pairs={{0,1},{1,0},{2,3},{3,2},{4,5},{5,4},{6,7},{7,6},{8,9},{9,8},{10,11... | collective-permute-start | bytes 393224 | tf_op jit(solution)/shard_map/ppermute | solution.py:439
  41.3 2.4 %collective-permute-start.14 = (bf16[512,128]{1,0:T(8,128)(2,1)}, bf16[512,128]{1,0:T(8,128)(2,1)S(1)}, u32[]{:S(2)}, u32[]{:S(2)}) collective-permute-start(bf16[512,128]{1,0:T(8,128)(2,1)} %get-tuple-element.64), channel_id=1, source_target_pairs={{0,2},{1,3},{2,0},{3,1},{4,6},{5,7},{6,4},{7,5},{8,10},{9,11},{10,... | collective-permute-start | bytes 393224 | tf_op jit(solution)/shard_map/ppermute | solution.py:439
  43.8 7.7 %aggregate.2 = (bf16[512,128]{1,0:T(8,128)(2,1)}, bf16[512,128]{1,0:T(8,128)(2,1)}, bf16[512,128]{1,0:T(8,128)(2,1)}, bf16[512,128]{1,0:T(8,128)(2,1)}) custom-call(s32[1]{0:T(128)} %bitcast.col_ref, s32[32,16]{1,0:T(8,128)} %compare_select_fusion.colref_ref, bf16[4096,128]{1,0:T(8,128)(2,1)} %feats_ref.3, bf16[256,128]{1,0:T(8,128)(2,1)} %copy-done.10, ...), custom_call_target="tpu_custom_call" | custom-call | tf_op jit(solution)/shard_map/aggregate/pallas_call | solution.py:112
  52.6 3.3 %collective-permute-start.11 = (bf16[512,128]{1,0:T(8,128)(2,1)}, bf16[512,128]{1,0:T(8,128)(2,1)S(1)}, u32[]{:S(2)}, u32[]{:S(2)}) collective-permute-start(bf16[512,128]{1,0:T(8,128)(2,1)} %get-tuple-element.60), channel_id=1, source_target_pairs={{0,2},{1,3},{2,0},{3,1},{4,6},{5,7},{6,4},{7,5},{8,10},{9,11},{10,... | collective-permute-start | bytes 393224 | tf_op jit(solution)/shard_map/ppermute | solution.py:439
  57.0 4.1 %dense.2 = (bf16[1024,512]{1,0:T(8,128)(2,1)}, bf16[512,512]{1,0:T(8,128)(2,1)}, bf16[512,128]{1,0:T(8,128)(2,1)}, bf16[512,128]{1,0:T(8,128)(2,1)}, bf16[512,128]{1,0:T(8,128)(2,1)}, /*index=5*/bf16[512,128]{1,0:T(8,128)(2,1)}) custom-call(s32[1]{0:T(128)} %bitcast.col_ref, bf16[4,1024,128]{2,1,0:T(8,128)(2,1)} %copy-done, ...), custom_call_target="tpu_custom_call" | custom-call | tf_op jit(solution)/shard_map/dense/pallas_call | solution.py:181
  61.1 4.6 %collective-permute-done.11.refs_3_.refs_7_ = bf16[512,128]{1,0:T(8,128)(2,1)S(1)} collective-permute-done((bf16[512,128]{1,0:T(8,128)(2,1)}, bf16[512,128]{1,0:T(8,128)(2,1)S(1)}, u32[]{:S(2)}, u32[]{:S(2)}) %collective-permute-start.11) | collective-permute-done | bytes 131104 | tf_op jit(solution)/shard_map/ppermute | solution.py:439
  66.5 4.1 %dense.3 = (bf16[1024,512]{1,0:T(8,128)(2,1)}, bf16[512,512]{1,0:T(8,128)(2,1)}, bf16[512,128]{1,0:T(8,128)(2,1)}, bf16[512,128]{1,0:T(8,128)(2,1)}, bf16[512,128]{1,0:T(8,128)(2,1)}, /*index=5*/bf16[512,128]{1,0:T(8,128)(2,1)}) custom-call(s32[1]{0:T(128)} %bitcast.col_ref, bf16[4,1024,128]{2,1,0:T(8,128)(2,1)} %copy-done, ...), custom_call_target="tpu_custom_call", output_to_operand_aliasing={{0}: (9, {})} | custom-call | tf_op jit(solution)/shard_map/dense/pallas_call | solution.py:181
  70.6 6.0 %weights.1 = (f32[512,512]{1,0:T(8,128)}, f32[512,512]{1,0:T(8,128)}, bf16[1024,128]{1,0:T(8,128)(2,1)}, bf16[1024,128]{1,0:T(8,128)(2,1)}, bf16[1024,128]{1,0:T(8,128)(2,1)}, /*index=5*/bf16[1024,128]{1,0:T(8,128)(2,1)}) custom-call(s32[1]{0:T(128)} %bitcast.col_ref, s32[1]{0:T(128)} %bitcast.2.row_ref, bf16[4,1024,128]{2,1,0:T(8,128)(2,1)} %copy-done, ...), custom_call_target="tpu_custom_call" | custom-call | tf_op jit(solution)/shard_map/weights/pallas_call | solution.py:238
  76.7 2.9 %collective-permute-done.16.received_ref = f32[512,512]{1,0:T(8,128)S(1)} collective-permute-done((f32[512,512]{1,0:T(8,128)}, f32[512,512]{1,0:T(8,128)S(1)}, u32[]{:S(2)}, u32[]{:S(2)}) %collective-permute-start.16) | collective-permute-done | bytes 1048608 | tf_op jit(solution)/shard_map/ppermute | solution.py:439
  80.6 2.6 %combine.1 = (f32[128,512]{1,0:T(8,128)}, f32[128,512]{1,0:T(8,128)}, f32[128,512]{1,0:T(8,128)}, f32[128,512]{1,0:T(8,128)}) custom-call(s32[1]{0:T(128)} %bitcast.2.row_ref, f32[512,512]{1,0:T(8,128)} %get-tuple-element.70.keep_ref, f32[512,512]{1,0:T(8,128)} %copy-done.1), custom_call_target="tpu_custom_call" | custom-call | tf_op jit(solution)/shard_map/combine/pallas_call | solution.py:261
  84.1 1.5 collective-permute-start.18
  86.6 5.9 %collective-permute-done.17 = f32[128,512]{1,0:T(8,128)S(1)} collective-permute-done((f32[128,512]{1,0:T(8,128)}, f32[128,512]{1,0:T(8,128)S(1)}, u32[]{:S(2)}, u32[]{:S(2)}) %collective-permute-start.17) | collective-permute-done | bytes 262176 | tf_op jit(solution)/shard_map/ppermute | solution.py:439
  92.5 5.5 %collective-permute-done.18 = f32[128,512]{1,0:T(8,128)S(1)} collective-permute-done((f32[128,512]{1,0:T(8,128)}, f32[128,512]{1,0:T(8,128)S(1)}, u32[]{:S(2)}, u32[]{:S(2)}) %collective-permute-start.18) | collective-permute-done | bytes 262176 | tf_op jit(solution)/shard_map/ppermute | solution.py:439
  99.1 2.3 %collective-permute-start.22 = (bf16[128,512]{1,0:T(8,128)(2,1)S(1)}, bf16[128,512]{1,0:T(8,128)(2,1)S(1)}, u32[]{:S(2)}, u32[]{:S(2)}) collective-permute-start(bf16[128,512]{1,0:T(8,128)(2,1)S(1)} %add_convert_fusion), channel_id=1, source_target_pairs={{0,3},{1,2},{2,1},{3,0},{4,7},{5,6},{6,5},{7,4},{8,11},{9,10},{10,... | collective-permute-start | bytes 393224 | tf_op jit(solution)/shard_map/ppermute | solution.py:439
  103.5 3.8 %collective-permute-done.22 = bf16[128,512]{1,0:T(8,128)(2,1)S(1)} collective-permute-done((bf16[128,512]{1,0:T(8,128)(2,1)S(1)}, bf16[128,512]{1,0:T(8,128)(2,1)S(1)}, u32[]{:S(2)}, u32[]{:S(2)}) %collective-permute-start.22) | collective-permute-done | bytes 131104 | tf_op jit(solution)/shard_map/ppermute | solution.py:439
  107.3 6.1 %collective-permute-done.21 = bf16[128,512]{1,0:T(8,128)(2,1)S(1)} collective-permute-done((bf16[128,512]{1,0:T(8,128)(2,1)S(1)}, bf16[128,512]{1,0:T(8,128)(2,1)S(1)}, u32[]{:S(2)}, u32[]{:S(2)}) %collective-permute-start.21) | collective-permute-done | bytes 131104 | tf_op jit(solution)/shard_map/ppermute | solution.py:439
  113.5 1.6 collective-permute-start.25
  115.1 1.5 collective-permute-start.24
  117.1 3.0 %collective-permute-start.34 = (bf16[512,128]{1,0:T(8,128)(2,1)S(1)}, bf16[512,128]{1,0:T(8,128)(2,1)S(1)}, u32[]{:S(2)}, u32[]{:S(2)}) collective-permute-start(bf16[512,128]{1,0:T(8,128)(2,1)S(1)} %copy-done.47), channel_id=1, source_target_pairs={{0,2},{1,3},{2,0},{3,1},{4,6},{5,7},{6,4},{7,5},{8,10},{9,11},{10,... | collective-permute-start | bytes 393224 | tf_op jit(solution)/shard_map/ppermute | solution.py:439
  120.6 1.6 collective-permute-done.24.refs_2_
  123.5 1.9 %assemble.1.mine_ref = bf16[512,512]{1,0:T(8,128)(2,1)} custom-call(s32[1]{0:T(128)} %bitcast.2.row_ref, bf16[128,512]{1,0:T(8,128)(2,1)} %copy-done.9, bf16[128,512]{1,0:T(8,128)(2,1)} %copy-done.28, bf16[128,512]{1,0:T(8,128)(2,1)} %copy-done.27, bf16[128,512]{1,0:T(8,128)(2,1)} %copy-done.26), custom_call_target="tpu_custom_call" | custom-call | tf_op jit(solution)/shard_map/assemble/pallas_call | solution.py:283
  125.4 2.8 %collective-permute-start.35 = (bf16[512,128]{1,0:T(8,128)(2,1)S(1)}, bf16[512,128]{1,0:T(8,128)(2,1)S(1)}, u32[]{:S(2)}, u32[]{:S(2)}) collective-permute-start(bf16[512,128]{1,0:T(8,128)(2,1)S(1)} %copy-done.44), channel_id=1, source_target_pairs={{0,3},{1,2},{2,1},{3,0},{4,7},{5,6},{6,5},{7,4},{8,11},{9,10},{10,... | collective-permute-start | bytes 393224 | tf_op jit(solution)/shard_map/ppermute | solution.py:439
  128.2 1.7 collective-permute-start.31
  129.9 2.8 %collective-permute-start.32 = (bf16[512,128]{1,0:T(8,128)(2,1)S(1)}, bf16[512,128]{1,0:T(8,128)(2,1)S(1)}, u32[]{:S(2)}, u32[]{:S(2)}) collective-permute-start(bf16[512,128]{1,0:T(8,128)(2,1)S(1)} %copy-done.45), channel_id=1, source_target_pairs={{0,3},{1,2},{2,1},{3,0},{4,7},{5,6},{6,5},{7,4},{8,11},{9,10},{10,... | collective-permute-start | bytes 393224 | tf_op jit(solution)/shard_map/ppermute | solution.py:439
  134.3 8.8 %pull.2.refs_8_ = f32[48,128,128]{2,1,0:T(8,128)} custom-call(s32[1]{0:T(128)} %bitcast.col_ref, s32[32,16]{1,0:T(8,128)} %compare_select_fusion.colref_ref, bf16[512,128]{1,0:T(8,128)(2,1)} %get-tuple-element.86.refs_0_, bf16[512,128]{1,0:T(8,128)(2,1)} %copy-done.20, bf16[512,128]{1,0:T(8,128)(2,1)} %copy-done.21, bf16[512,128]{1,0:T(8,128)(2,1)} %copy-done.25, ...), custom_call_target="tpu_custom_call" | custom-call | tf_op jit(solution)/shard_map/pull/pallas_call | solution.py:378
  143.9 10.7 %pull.3 = (bf16[4096,128]{1,0:T(8,128)(2,1)}, bf16[256,128]{1,0:T(8,128)(2,1)}, bf16[256,128]{1,0:T(8,128)(2,1)}, bf16[256,128]{1,0:T(8,128)(2,1)}, bf16[256,128...) custom-call(s32[1]{0:T(128)} %bitcast.col_ref, ...), custom_call_target="tpu_custom_call" | custom-call | tf_op jit(solution)/shard_map/pull/pallas_call | solution.py:378
  154.6 1.6 collective-permute-start.37
  157.7 2.1 %collective-permute-start.27 = (bf16[1024,128]{1,0:T(8,128)(2,1)S(1)}, bf16[1024,128]{1,0:T(8,128)(2,1)S(1)}, u32[]{:S(2)}, u32[]{:S(2)}) collective-permute-start(bf16[1024,128]{1,0:T(8,128)(2,1)S(1)} %copy-done.43), channel_id=1, source_target_pairs={{0,1},{1,0},{2,3},{3,2},{4,5},{5,4},{6,7},{7,6},{8,9},{9,8},{10,11... | collective-permute-start | bytes 786440 | tf_op jit(solution)/shard_map/ppermute | solution.py:439
  159.8 2.6 %collective-permute-start.28 = (bf16[1024,128]{1,0:T(8,128)(2,1)S(1)}, bf16[1024,128]{1,0:T(8,128)(2,1)S(1)}, u32[]{:S(2)}, u32[]{:S(2)}) collective-permute-start(bf16[1024,128]{1,0:T(8,128)(2,1)S(1)} %copy-done.42), channel_id=1, source_target_pairs={{0,2},{1,3},{2,0},{3,1},{4,6},{5,7},{6,4},{7,5},{8,10},{9,11},{10,... | collective-permute-start | bytes 786440 | tf_op jit(solution)/shard_map/ppermute | solution.py:439
  162.5 1.5 collective-permute-start.29
  164.2 4.3 %collective-permute-done.40.refs_13_ = bf16[256,128]{1,0:T(8,128)(2,1)S(1)} collective-permute-done((bf16[256,128]{1,0:T(8,128)(2,1)}, bf16[256,128]{1,0:T(8,128)(2,1)S(1)}, u32[]{:S(2)}, u32[]{:S(2)}) %collective-permute-start.40) | collective-permute-done | bytes 65568 | tf_op jit(solution)/shard_map/ppermute | solution.py:439
  168.4 1.8 collective-permute-start.41
  170.2 3.6 %collective-permute-done.41.refs_14_ = bf16[256,128]{1,0:T(8,128)(2,1)S(1)} collective-permute-done((bf16[256,128]{1,0:T(8,128)(2,1)}, bf16[256,128]{1,0:T(8,128)(2,1)S(1)}, u32[]{:S(2)}, u32[]{:S(2)}) %collective-permute-start.41) | collective-permute-done | bytes 65568 | tf_op jit(solution)/shard_map/ppermute | solution.py:439
  174.6 4.3 %collective-permute-done.42.refs_15_ = bf16[256,128]{1,0:T(8,128)(2,1)S(1)} collective-permute-done((bf16[256,128]{1,0:T(8,128)(2,1)}, bf16[256,128]{1,0:T(8,128)(2,1)S(1)}, u32[]{:S(2)}, u32[]{:S(2)}) %collective-permute-start.42) | collective-permute-done | bytes 65568 | tf_op jit(solution)/shard_map/ppermute | solution.py:439
  178.9 2.3 %collective-permute-done.28.refs_6_ = bf16[1024,128]{1,0:T(8,128)(2,1)S(1)} collective-permute-done((bf16[1024,128]{1,0:T(8,128)(2,1)S(1)}, bf16[1024,128]{1,0:T(8,128)(2,1)S(1)}, u32[]{:S(2)}, u32[]{:S(2)}) %collective-permute-start.28) | collective-permute-done | bytes 262176 | tf_op jit(solution)/shard_map/ppermute | solution.py:439
  182.0 3.4 %finish.1 = f32[4096,128]{1,0:T(8,128)} custom-call(s32[1]{0:T(128)} %bitcast.col_ref, s32[1]{0:T(128)} %bitcast.2.row_ref, s32[1,128]{1,0:T(1,128)} %copy-done.38, s32[1,128]{1,0:T(1,128)} %copy-done.39, s32[2,128]{1,0:T(2,128)} %copy-done.36, s32[4,128]{1,0:T(4,128)} %copy-done.37, bf16[1024,128]{1,0:T(8,128)(2,1)} %get-tuple-element.78.refs_4_, ...), custom_call_target="tpu_custom_call" | custom-call | tf_op jit(solution)/shard_map/finish/pallas_call | solution.py:423
  186.2 2.7 %widen.1 = (f32[512,512]{1,0:T(8,128)}, f32[512,512]{1,0:T(8,128)}) custom-call(s32[1]{0:T(128)} %bitcast.2.row_ref, bf16[512,512]{1,0:T(8,128)(2,1)} %assemble.1.mine_ref, bf16[512,512]{1,0:T(8,128)(2,1)} %copy-done.8), custom_call_target="tpu_custom_call" | custom-call | tf_op jit(solution)/shard_map/widen/pallas_call | solution.py:304
  (161 shorter events, 25.2 us)
Async XLA Ops:
  0.6 55.3 %all-to-all-start = ((bf16[4,1024,128]{2,1,0:T(8,128)(2,1)}), bf16[4,1024,128]{2,1,0:T(8,128)(2,1)S(1)}, u32[]{:S(2)}, u32[]{:S(2)}) async-start(bf16[4,1024,128]{2,1,0:T(8,128)(2,1)} %bitcast.3), calls=%async_computation | async-start | bytes 2097152 | tf_op jit(solution)/shard_map/all_to_all | solution.py:467
  7.8 1.2 collective-permute-start
  9.1 3.6 %collective-permute-start.1 = (s32[2,128]{1,0:T(2,128)S(1)}, s32[2,128]{1,0:T(2,128)S(1)}, u32[]{:S(2)}, u32[]{:S(2)}) collective-permute-start(s32[2,128]{1,0:T(2,128)S(1)} %pad_add_fusion.1), channel_id=1, source_target_pairs={{0,8},{4,12},{8,0},{12,4},{16,24},{20,28},{24,16},{28,20},{1,9},{5... | collective-permute-start | bytes 3080 | tf_op jit(solution)/shard_map/ppermute | solution.py:439
  12.7 3.7 %collective-permute-start.2 = (s32[4,128]{1,0:T(4,128)S(1)}, s32[4,128]{1,0:T(4,128)S(1)}, u32[]{:S(2)}, u32[]{:S(2)}) collective-permute-start(s32[4,128]{1,0:T(4,128)S(1)} %pad_add_fusion), channel_id=1, source_target_pairs={{0,16},{4,20},{8,24},{12,28},{16,0},{20,4},{24,8},{28,12},{1,17},{... | collective-permute-start | bytes 6152 | tf_op jit(solution)/shard_map/ppermute | solution.py:439
  19.6 3.7 %collective-permute-start.3 = (bf16[256,128]{1,0:T(8,128)(2,1)}, bf16[256,128]{1,0:T(8,128)(2,1)S(1)}, u32[]{:S(2)}, u32[]{:S(2)}) collective-permute-start(bf16[256,128]{1,0:T(8,128)(2,1)} %get-tuple-element.51), channel_id=1, source_target_pairs={{0,4},{4,0},{8,12},{12,8},{16,20},{20,16},{24,28},{28,24},{1,5},{5... | collective-permute-start | bytes 196616 | tf_op jit(solution)/shard_map/ppermute | solution.py:439
  19.7 6.0 %collective-permute-start.4 = (bf16[256,128]{1,0:T(8,128)(2,1)}, bf16[256,128]{1,0:T(8,128)(2,1)S(1)}, u32[]{:S(2)}, u32[]{:S(2)}) collective-permute-start(bf16[256,128]{1,0:T(8,128)(2,1)} %get-tuple-element.52), channel_id=1, source_target_pairs={{0,8},{4,12},{8,0},{12,4},{16,24},{20,28},{24,16},{28,20},{1,9},{5... | collective-permute-start | bytes 196616 | tf_op jit(solution)/shard_map/ppermute | solution.py:439
  21.3 5.4 %collective-permute-start.5 = (bf16[256,128]{1,0:T(8,128)(2,1)}, bf16[256,128]{1,0:T(8,128)(2,1)S(1)}, u32[]{:S(2)}, u32[]{:S(2)}) collective-permute-start(bf16[256,128]{1,0:T(8,128)(2,1)} %get-tuple-element.53), channel_id=1, source_target_pairs={{0,12},{4,8},{8,4},{12,0},{16,28},{20,24},{24,20},{28,16},{1,13},{... | collective-permute-start | bytes 196616 | tf_op jit(solution)/shard_map/ppermute | solution.py:439
  21.6 5.0 %collective-permute-start.6 = (bf16[256,128]{1,0:T(8,128)(2,1)}, bf16[256,128]{1,0:T(8,128)(2,1)S(1)}, u32[]{:S(2)}, u32[]{:S(2)}) collective-permute-start(bf16[256,128]{1,0:T(8,128)(2,1)} %get-tuple-element.54), channel_id=1, source_target_pairs={{0,16},{4,20},{8,24},{12,28},{16,0},{20,4},{24,8},{28,12},{1,17},{... | collective-permute-start | bytes 196616 | tf_op jit(solution)/shard_map/ppermute | solution.py:439
  23.1 4.3 %collective-permute-start.7 = (bf16[256,128]{1,0:T(8,128)(2,1)}, bf16[256,128]{1,0:T(8,128)(2,1)S(1)}, u32[]{:S(2)}, u32[]{:S(2)}) collective-permute-start(bf16[256,128]{1,0:T(8,128)(2,1)} %get-tuple-element.55), channel_id=1, source_target_pairs={{0,20},{4,16},{8,28},{12,24},{16,4},{20,0},{24,12},{28,8},{1,21},{... | collective-permute-start | bytes 196616 | tf_op jit(solution)/shard_map/ppermute | solution.py:439
  23.4 5.6 %collective-permute-start.8 = (bf16[256,128]{1,0:T(8,128)(2,1)}, bf16[256,128]{1,0:T(8,128)(2,1)S(1)}, u32[]{:S(2)}, u32[]{:S(2)}) collective-permute-start(bf16[256,128]{1,0:T(8,128)(2,1)} %get-tuple-element.56), channel_id=1, source_target_pairs={{0,24},{4,28},{8,16},{12,20},{16,8},{20,12},{24,0},{28,4},{1,25},{... | collective-permute-start | bytes 196616 | tf_op jit(solution)/shard_map/ppermute | solution.py:439
  25.7 5.2 %collective-permute-start.9 = (bf16[256,128]{1,0:T(8,128)(2,1)}, bf16[256,128]{1,0:T(8,128)(2,1)S(1)}, u32[]{:S(2)}, u32[]{:S(2)}) collective-permute-start(bf16[256,128]{1,0:T(8,128)(2,1)} %get-tuple-element.57), channel_id=1, source_target_pairs={{0,28},{4,24},{8,20},{12,16},{16,12},{20,8},{24,4},{28,0},{1,29},{... | collective-permute-start | bytes 196616 | tf_op jit(solution)/shard_map/ppermute | solution.py:439
  39.2 16.6 %collective-permute-start.13 = (bf16[512,128]{1,0:T(8,128)(2,1)}, bf16[512,128]{1,0:T(8,128)(2,1)S(1)}, u32[]{:S(2)}, u32[]{:S(2)}) collective-permute-start(bf16[512,128]{1,0:T(8,128)(2,1)} %get-tuple-element.63), channel_id=1, source_target_pairs={{0,1},{1,0},{2,3},{3,2},{4,5},{5,4},{6,7},{7,6},{8,9},{9,8},{10,11... | collective-permute-start | bytes 393224 | tf_op jit(solution)/shard_map/ppermute | solution.py:439
  41.3 14.6 %collective-permute-start.14 = (bf16[512,128]{1,0:T(8,128)(2,1)}, bf16[512,128]{1,0:T(8,128)(2,1)S(1)}, u32[]{:S(2)}, u32[]{:S(2)}) collective-permute-start(bf16[512,128]{1,0:T(8,128)(2,1)} %get-tuple-element.64), channel_id=1, source_target_pairs={{0,2},{1,3},{2,0},{3,1},{4,6},{5,7},{6,4},{7,5},{8,10},{9,11},{10,... | collective-permute-start | bytes 393224 | tf_op jit(solution)/shard_map/ppermute | solution.py:439
  43.7 12.2 %collective-permute-start.15 = (bf16[512,128]{1,0:T(8,128)(2,1)}, bf16[512,128]{1,0:T(8,128)(2,1)S(1)}, u32[]{:S(2)}, u32[]{:S(2)}) collective-permute-start(bf16[512,128]{1,0:T(8,128)(2,1)} %get-tuple-element.65), channel_id=1, source_target_pairs={{0,3},{1,2},{2,1},{3,0},{4,7},{5,6},{6,5},{7,4},{8,11},{9,10},{10,... | collective-permute-start | bytes 393224 | tf_op jit(solution)/shard_map/ppermute | solution.py:439
  51.5 9.6 %collective-permute-start.10 = (bf16[512,128]{1,0:T(8,128)(2,1)}, bf16[512,128]{1,0:T(8,128)(2,1)S(1)}, u32[]{:S(2)}, u32[]{:S(2)}) collective-permute-start(bf16[512,128]{1,0:T(8,128)(2,1)} %get-tuple-element.59), channel_id=1, source_target_pairs={{0,1},{1,0},{2,3},{3,2},{4,5},{5,4},{6,7},{7,6},{8,9},{9,8},{10,11... | collective-permute-start | bytes 393224 | tf_op jit(solution)/shard_map/ppermute | solution.py:439
  52.6 13.2 %collective-permute-start.11 = (bf16[512,128]{1,0:T(8,128)(2,1)}, bf16[512,128]{1,0:T(8,128)(2,1)S(1)}, u32[]{:S(2)}, u32[]{:S(2)}) collective-permute-start(bf16[512,128]{1,0:T(8,128)(2,1)} %get-tuple-element.60), channel_id=1, source_target_pairs={{0,2},{1,3},{2,0},{3,1},{4,6},{5,7},{6,4},{7,5},{8,10},{9,11},{10,... | collective-permute-start | bytes 393224 | tf_op jit(solution)/shard_map/ppermute | solution.py:439
  55.8 9.9 %collective-permute-start.12 = (bf16[512,128]{1,0:T(8,128)(2,1)}, bf16[512,128]{1,0:T(8,128)(2,1)S(1)}, u32[]{:S(2)}, u32[]{:S(2)}) collective-permute-start(bf16[512,128]{1,0:T(8,128)(2,1)} %get-tuple-element.61), channel_id=1, source_target_pairs={{0,3},{1,2},{2,1},{3,0},{4,7},{5,6},{6,5},{7,4},{8,11},{9,10},{10,... | collective-permute-start | bytes 393224 | tf_op jit(solution)/shard_map/ppermute | solution.py:439
  76.6 48.8 %copy-start.44 = (bf16[512,128]{1,0:T(8,128)(2,1)S(1)}, bf16[512,128]{1,0:T(8,128)(2,1)}, u32[]{:S(2)}) copy-start(bf16[512,128]{1,0:T(8,128)(2,1)} %get-tuple-element.89) | copy-start | bytes 393220
  76.6 51.6 %copy-start.48 = (bf16[512,128]{1,0:T(8,128)(2,1)S(1)}, bf16[512,128]{1,0:T(8,128)(2,1)}, u32[]{:S(2)}) copy-start(bf16[512,128]{1,0:T(8,128)(2,1)} %get-tuple-element.83) | copy-start | bytes 393220
  76.6 51.6 %copy-start.46 = (bf16[512,128]{1,0:T(8,128)(2,1)S(1)}, bf16[512,128]{1,0:T(8,128)(2,1)}, u32[]{:S(2)}) copy-start(bf16[512,128]{1,0:T(8,128)(2,1)} %get-tuple-element.84) | copy-start | bytes 393220
  76.6 53.3 %copy-start.45 = (bf16[512,128]{1,0:T(8,128)(2,1)S(1)}, bf16[512,128]{1,0:T(8,128)(2,1)}, u32[]{:S(2)}) copy-start(bf16[512,128]{1,0:T(8,128)(2,1)} %get-tuple-element.85) | copy-start | bytes 393220
  76.6 2.9 %collective-permute-start.16 = (f32[512,512]{1,0:T(8,128)}, f32[512,512]{1,0:T(8,128)S(1)}, u32[]{:S(2)}, u32[]{:S(2)}) collective-permute-start(f32[512,512]{1,0:T(8,128)} %get-tuple-element.71), channel_id=1, source_target_pairs={{0,4},{4,0},{8,12},{12,8},{16,20},{20,16},{24,28},{28,24},{1,5},{5... | collective-permute-start | bytes 3145736 | tf_op jit(solution)/shard_map/ppermute | solution.py:439
  83.1 9.4 %collective-permute-start.17 = (f32[128,512]{1,0:T(8,128)}, f32[128,512]{1,0:T(8,128)S(1)}, u32[]{:S(2)}, u32[]{:S(2)}) collective-permute-start(f32[128,512]{1,0:T(8,128)} %get-tuple-element.73), channel_id=1, source_target_pairs={{0,8},{4,12},{8,0},{12,4},{16,24},{20,28},{24,16},{28,20},{1,9},{5... | collective-permute-start | bytes 786440 | tf_op jit(solution)/shard_map/ppermute | solution.py:439
  84.1 13.9 %collective-permute-start.18 = (f32[128,512]{1,0:T(8,128)}, f32[128,512]{1,0:T(8,128)S(1)}, u32[]{:S(2)}, u32[]{:S(2)}) collective-permute-start(f32[128,512]{1,0:T(8,128)} %get-tuple-element.74), channel_id=1, source_target_pairs={{0,16},{4,20},{8,24},{12,28},{16,0},{20,4},{24,8},{28,12},{1,17},{... | collective-permute-start | bytes 786440 | tf_op jit(solution)/shard_map/ppermute | solution.py:439
  85.6 12.4 %collective-permute-start.19 = (f32[128,512]{1,0:T(8,128)}, f32[128,512]{1,0:T(8,128)S(1)}, u32[]{:S(2)}, u32[]{:S(2)}) collective-permute-start(f32[128,512]{1,0:T(8,128)} %get-tuple-element.75), channel_id=1, source_target_pairs={{0,24},{4,28},{8,16},{12,20},{16,8},{20,12},{24,0},{28,4},{1,25},{... | collective-permute-start | bytes 786440 | tf_op jit(solution)/shard_map/ppermute | solution.py:439
  99.1 8.2 %collective-permute-start.22 = (bf16[128,512]{1,0:T(8,128)(2,1)S(1)}, bf16[128,512]{1,0:T(8,128)(2,1)S(1)}, u32[]{:S(2)}, u32[]{:S(2)}) collective-permute-start(bf16[128,512]{1,0:T(8,128)(2,1)S(1)} %add_convert_fusion), channel_id=1, source_target_pairs={{0,3},{1,2},{2,1},{3,0},{4,7},{5,6},{6,5},{7,4},{8,11},{9,10},{10,... | collective-permute-start | bytes 393224 | tf_op jit(solution)/shard_map/ppermute | solution.py:439
  101.4 12.0 %collective-permute-start.21 = (bf16[128,512]{1,0:T(8,128)(2,1)S(1)}, bf16[128,512]{1,0:T(8,128)(2,1)S(1)}, u32[]{:S(2)}, u32[]{:S(2)}) collective-permute-start(bf16[128,512]{1,0:T(8,128)(2,1)S(1)} %add_convert_fusion), channel_id=1, source_target_pairs={{0,2},{1,3},{2,0},{3,1},{4,6},{5,7},{6,4},{7,5},{8,10},{9,11},{10,... | collective-permute-start | bytes 393224 | tf_op jit(solution)/shard_map/ppermute | solution.py:439
  102.6 10.8 %collective-permute-start.20 = (bf16[128,512]{1,0:T(8,128)(2,1)S(1)}, bf16[128,512]{1,0:T(8,128)(2,1)S(1)}, u32[]{:S(2)}, u32[]{:S(2)}) collective-permute-start(bf16[128,512]{1,0:T(8,128)(2,1)S(1)} %add_convert_fusion), channel_id=1, source_target_pairs={{0,1},{1,0},{2,3},{3,2},{4,5},{5,4},{6,7},{7,6},{8,9},{9,8},{10,11... | collective-permute-start | bytes 393224 | tf_op jit(solution)/shard_map/ppermute | solution.py:439
  113.5 7.1 %collective-permute-start.25 = (bf16[128,512]{1,0:T(8,128)(2,1)S(1)}, bf16[128,512]{1,0:T(8,128)(2,1)S(1)}, u32[]{:S(2)}, u32[]{:S(2)}) collective-permute-start(bf16[128,512]{1,0:T(8,128)(2,1)S(1)} %multiply_convert_fusion.refs_0_), channel_id=1, source_target_pairs={{0,24},{4,28},{8,16},{12,20},{16,8},{20,12},{24,0},{28,4},{1,25},{... | collective-permute-start | bytes 393224 | tf_op jit(solution)/shard_map/ppermute | solution.py:439
  115.1 7.1 %collective-permute-start.24 = (bf16[128,512]{1,0:T(8,128)(2,1)S(1)}, bf16[128,512]{1,0:T(8,128)(2,1)S(1)}, u32[]{:S(2)}, u32[]{:S(2)}) collective-permute-start(bf16[128,512]{1,0:T(8,128)(2,1)S(1)} %multiply_convert_fusion.refs_0_), channel_id=1, source_target_pairs={{0,16},{4,20},{8,24},{12,28},{16,0},{20,4},{24,8},{28,12},{1,17},{... | collective-permute-start | bytes 393224 | tf_op jit(solution)/shard_map/ppermute | solution.py:439
  116.6 5.6 %collective-permute-start.23 = (bf16[128,512]{1,0:T(8,128)(2,1)S(1)}, bf16[128,512]{1,0:T(8,128)(2,1)S(1)}, u32[]{:S(2)}, u32[]{:S(2)}) collective-permute-start(bf16[128,512]{1,0:T(8,128)(2,1)S(1)} %multiply_convert_fusion.refs_0_), channel_id=1, source_target_pairs={{0,8},{4,12},{8,0},{12,4},{16,24},{20,28},{24,16},{28,20},{1,9},{5... | collective-permute-start | bytes 393224 | tf_op jit(solution)/shard_map/ppermute | solution.py:439
  117.1 11.1 %collective-permute-start.33 = (bf16[512,128]{1,0:T(8,128)(2,1)S(1)}, bf16[512,128]{1,0:T(8,128)(2,1)S(1)}, u32[]{:S(2)}, u32[]{:S(2)}) collective-permute-start(bf16[512,128]{1,0:T(8,128)(2,1)S(1)} %copy-done.49), channel_id=1, source_target_pairs={{0,1},{1,0},{2,3},{3,2},{4,5},{5,4},{6,7},{7,6},{8,9},{9,8},{10,11... | collective-permute-start | bytes 393224 | tf_op jit(solution)/shard_map/ppermute | solution.py:439
  117.1 12.8 %collective-permute-start.34 = (bf16[512,128]{1,0:T(8,128)(2,1)S(1)}, bf16[512,128]{1,0:T(8,128)(2,1)S(1)}, u32[]{:S(2)}, u32[]{:S(2)}) collective-permute-start(bf16[512,128]{1,0:T(8,128)(2,1)S(1)} %copy-done.47), channel_id=1, source_target_pairs={{0,2},{1,3},{2,0},{3,1},{4,6},{5,7},{6,4},{7,5},{8,10},{9,11},{10,... | collective-permute-start | bytes 393224 | tf_op jit(solution)/shard_map/ppermute | solution.py:439
  125.4 60.0 %collective-permute-start.26 = (bf16[512,512]{1,0:T(8,128)(2,1)}, bf16[512,512]{1,0:T(8,128)(2,1)S(1)}, u32[]{:S(2)}, u32[]{:S(2)}) collective-permute-start(bf16[512,512]{1,0:T(8,128)(2,1)} %assemble.1.mine_ref), channel_id=1, source_target_pairs={{0,4},{4,0},{8,12},{12,8},{16,20},{20,16},{24,28},{28,24},{1,5},{5... | collective-permute-start | bytes 1572872 | tf_op jit(solution)/shard_map/ppermute | solution.py:439
  125.4 8.2 %collective-permute-start.35 = (bf16[512,128]{1,0:T(8,128)(2,1)S(1)}, bf16[512,128]{1,0:T(8,128)(2,1)S(1)}, u32[]{:S(2)}, u32[]{:S(2)}) collective-permute-start(bf16[512,128]{1,0:T(8,128)(2,1)S(1)} %copy-done.44), channel_id=1, source_target_pairs={{0,3},{1,2},{2,1},{3,0},{4,7},{5,6},{6,5},{7,4},{8,11},{9,10},{10,... | collective-permute-start | bytes 393224 | tf_op jit(solution)/shard_map/ppermute | solution.py:439
  128.2 14.9 %collective-permute-start.30 = (bf16[512,128]{1,0:T(8,128)(2,1)S(1)}, bf16[512,128]{1,0:T(8,128)(2,1)S(1)}, u32[]{:S(2)}, u32[]{:S(2)}) collective-permute-start(bf16[512,128]{1,0:T(8,128)(2,1)S(1)} %copy-done.48), channel_id=1, source_target_pairs={{0,1},{1,0},{2,3},{3,2},{4,5},{5,4},{6,7},{7,6},{8,9},{9,8},{10,11... | collective-permute-start | bytes 393224 | tf_op jit(solution)/shard_map/ppermute | solution.py:439
  128.2 14.9 %collective-permute-start.31 = (bf16[512,128]{1,0:T(8,128)(2,1)S(1)}, bf16[512,128]{1,0:T(8,128)(2,1)S(1)}, u32[]{:S(2)}, u32[]{:S(2)}) collective-permute-start(bf16[512,128]{1,0:T(8,128)(2,1)S(1)} %copy-done.46), channel_id=1, source_target_pairs={{0,2},{1,3},{2,0},{3,1},{4,6},{5,7},{6,4},{7,5},{8,10},{9,11},{10,... | collective-permute-start | bytes 393224 | tf_op jit(solution)/shard_map/ppermute | solution.py:439
  129.9 13.3 %collective-permute-start.32 = (bf16[512,128]{1,0:T(8,128)(2,1)S(1)}, bf16[512,128]{1,0:T(8,128)(2,1)S(1)}, u32[]{:S(2)}, u32[]{:S(2)}) collective-permute-start(bf16[512,128]{1,0:T(8,128)(2,1)S(1)} %copy-done.45), channel_id=1, source_target_pairs={{0,3},{1,2},{2,1},{3,0},{4,7},{5,6},{6,5},{7,4},{8,11},{9,10},{10,... | collective-permute-start | bytes 393224 | tf_op jit(solution)/shard_map/ppermute | solution.py:439
  154.6 3.2 %collective-permute-start.36 = (bf16[256,128]{1,0:T(8,128)(2,1)}, bf16[256,128]{1,0:T(8,128)(2,1)S(1)}, u32[]{:S(2)}, u32[]{:S(2)}) collective-permute-start(bf16[256,128]{1,0:T(8,128)(2,1)} %get-tuple-element.91), channel_id=1, source_target_pairs={{0,4},{4,0},{8,12},{12,8},{16,20},{20,16},{24,28},{28,24},{1,5},{5... | collective-permute-start | bytes 196616 | tf_op jit(solution)/shard_map/ppermute | solution.py:439
  154.6 5.2 %collective-permute-start.37 = (bf16[256,128]{1,0:T(8,128)(2,1)}, bf16[256,128]{1,0:T(8,128)(2,1)S(1)}, u32[]{:S(2)}, u32[]{:S(2)}) collective-permute-start(bf16[256,128]{1,0:T(8,128)(2,1)} %get-tuple-element.92), channel_id=1, source_target_pairs={{0,8},{4,12},{8,0},{12,4},{16,24},{20,28},{24,16},{28,20},{1,9},{5... | collective-permute-start | bytes 196616 | tf_op jit(solution)/shard_map/ppermute | solution.py:439
  156.2 6.2 %collective-permute-start.38 = (bf16[256,128]{1,0:T(8,128)(2,1)}, bf16[256,128]{1,0:T(8,128)(2,1)S(1)}, u32[]{:S(2)}, u32[]{:S(2)}) collective-permute-start(bf16[256,128]{1,0:T(8,128)(2,1)} %get-tuple-element.93), channel_id=1, source_target_pairs={{0,12},{4,8},{8,4},{12,0},{16,28},{20,24},{24,20},{28,16},{1,13},{... | collective-permute-start | bytes 196616 | tf_op jit(solution)/shard_map/ppermute | solution.py:439
  156.5 7.5 %collective-permute-start.39 = (bf16[256,128]{1,0:T(8,128)(2,1)}, bf16[256,128]{1,0:T(8,128)(2,1)S(1)}, u32[]{:S(2)}, u32[]{:S(2)}) collective-permute-start(bf16[256,128]{1,0:T(8,128)(2,1)} %get-tuple-element.94), channel_id=1, source_target_pairs={{0,16},{4,20},{8,24},{12,28},{16,0},{20,4},{24,8},{28,12},{1,17},{... | collective-permute-start | bytes 196616 | tf_op jit(solution)/shard_map/ppermute | solution.py:439
  157.7 21.2 %collective-permute-start.27 = (bf16[1024,128]{1,0:T(8,128)(2,1)S(1)}, bf16[1024,128]{1,0:T(8,128)(2,1)S(1)}, u32[]{:S(2)}, u32[]{:S(2)}) collective-permute-start(bf16[1024,128]{1,0:T(8,128)(2,1)S(1)} %copy-done.43), channel_id=1, source_target_pairs={{0,1},{1,0},{2,3},{3,2},{4,5},{5,4},{6,7},{7,6},{8,9},{9,8},{10,11... | collective-permute-start | bytes 786440 | tf_op jit(solution)/shard_map/ppermute | solution.py:439
  159.8 21.4 %collective-permute-start.28 = (bf16[1024,128]{1,0:T(8,128)(2,1)S(1)}, bf16[1024,128]{1,0:T(8,128)(2,1)S(1)}, u32[]{:S(2)}, u32[]{:S(2)}) collective-permute-start(bf16[1024,128]{1,0:T(8,128)(2,1)S(1)} %copy-done.42), channel_id=1, source_target_pairs={{0,2},{1,3},{2,0},{3,1},{4,6},{5,7},{6,4},{7,5},{8,10},{9,11},{10,... | collective-permute-start | bytes 786440 | tf_op jit(solution)/shard_map/ppermute | solution.py:439
  162.5 18.8 %collective-permute-start.29 = (bf16[1024,128]{1,0:T(8,128)(2,1)S(1)}, bf16[1024,128]{1,0:T(8,128)(2,1)S(1)}, u32[]{:S(2)}, u32[]{:S(2)}) collective-permute-start(bf16[1024,128]{1,0:T(8,128)(2,1)S(1)} %copy-done.41), channel_id=1, source_target_pairs={{0,3},{1,2},{2,1},{3,0},{4,7},{5,6},{6,5},{7,4},{8,11},{9,10},{10,... | collective-permute-start | bytes 786440 | tf_op jit(solution)/shard_map/ppermute | solution.py:439
  164.0 4.4 %collective-permute-start.40 = (bf16[256,128]{1,0:T(8,128)(2,1)}, bf16[256,128]{1,0:T(8,128)(2,1)S(1)}, u32[]{:S(2)}, u32[]{:S(2)}) collective-permute-start(bf16[256,128]{1,0:T(8,128)(2,1)} %get-tuple-element.95), channel_id=1, source_target_pairs={{0,20},{4,16},{8,28},{12,24},{16,4},{20,0},{24,12},{28,8},{1,21},{... | collective-permute-start | bytes 196616 | tf_op jit(solution)/shard_map/ppermute | solution.py:439
  168.4 5.4 %collective-permute-start.41 = (bf16[256,128]{1,0:T(8,128)(2,1)}, bf16[256,128]{1,0:T(8,128)(2,1)S(1)}, u32[]{:S(2)}, u32[]{:S(2)}) collective-permute-start(bf16[256,128]{1,0:T(8,128)(2,1)} %get-tuple-element.96), channel_id=1, source_target_pairs={{0,24},{4,28},{8,16},{12,20},{16,8},{20,12},{24,0},{28,4},{1,25},{... | collective-permute-start | bytes 196616 | tf_op jit(solution)/shard_map/ppermute | solution.py:439
  173.8 5.1 %collective-permute-start.42 = (bf16[256,128]{1,0:T(8,128)(2,1)}, bf16[256,128]{1,0:T(8,128)(2,1)S(1)}, u32[]{:S(2)}, u32[]{:S(2)}) collective-permute-start(bf16[256,128]{1,0:T(8,128)(2,1)} %get-tuple-element.97), channel_id=1, source_target_pairs={{0,28},{4,24},{8,20},{12,16},{16,12},{20,8},{24,4},{28,0},{1,29},{... | collective-permute-start | bytes 196616 | tf_op jit(solution)/shard_map/ppermute | solution.py:439
  (46 other events, 351.2 us)

commit v3 on v2

--- a/solution.py
+++ b/solution.py
@@ -10,13 +10,11 @@
 
 BF16, F32 = jnp.bfloat16, jnp.float32
 CHUNKS = 2
-VMEM_LIMIT = 56 * 1024 * 1024
-
-
-def params(dims):
-    return pltpu.CompilerParams(
-        dimension_semantics=("arbitrary",) * dims, vmem_limit_bytes=VMEM_LIMIT
-    )
+VMEM_LIMIT = 24 * 1024 * 1024
+
+
+def params():
+    return pltpu.CompilerParams(dimension_semantics=("arbitrary",), vmem_limit_bytes=VMEM_LIMIT)
 
 
 def full(shape):
@@ -36,6 +34,21 @@
     for ref in refs:
         rows += [(ref, j) for j in range(ref.shape[0])]
     return rows
+
+
+def begin(sources, targets, sems):
+    copies = [
+        pltpu.make_async_copy(source, target, sems.at[n])
+        for n, (source, target) in enumerate(zip(sources, targets))
+    ]
+    for copy in copies:
+        copy.start()
+    return copies
+
+
+def load(sources, targets, sems):
+    for copy in begin(sources, targets, sems):
+        copy.wait()
 
 
 def select_tiles(row, ids, feats, tile, cap):
@@ -68,62 +81,77 @@
         in_specs=[SMEM] * (1 + len(ids)) + [ANY],
         out_specs=[full((cap * tile, width))] * (count - 1),
         scratch_shapes=[pltpu.SemaphoreType.DMA(((count - 1) * cap,))],
+        compiler_params=params(),
         name="select_tiles",
     )(row, *ids, feats)
 
 
-def aggregate(col, colref, feats, arrived, adj, chunk, parts):
+def aggregate(col, colref, sources, adj, chunk, parts, pool_rows):
     blocks, per_block, tile, _ = adj.shape
-    width = feats.shape[1]
-    own = feats.shape[0]
-    step = arrived[0].shape[0]
-    count = len(arrived)
+    width = sources[0].shape[1]
+    count = len(sources)
+    fresh = count > 1
     per_part = blocks // parts
     per_chunk = per_part // CHUNKS
     chunk_rows = per_chunk * tile
-
-    def tile_of(k, t, col_ref):
-        return (k ^ col_ref[0]) * per_part + chunk * per_chunk + t
-
-    def kernel(col_ref, colref_ref, feats_ref, *refs):
-        arrived_refs, refs = refs[:count], refs[count:]
-        adj_refs, outs, pool = refs[:parts], refs[parts : 2 * parts], refs[-1]
-        t = pl.program_id(0)
-
-        @pl.when(t == 0)
-        def _():
-            pool[:own, :] = feats_ref[...]
-            for n, ref in enumerate(arrived_refs):
-                pool[own + (n + 1) * step : own + (n + 2) * step, :] = ref[...]
-
-        for k in range(parts):
-            b = tile_of(k, t, col_ref)
-            right = jnp.concatenate(
-                [pool[rows_at(colref_ref[b, q], tile), :] for q in range(per_block)], axis=0
+    shapes = [(chunk_rows, width)] * parts + [(pool_rows, width)] * fresh
+
+    def kernel(col_ref, colref_ref, *refs):
+        source_refs, adj_ref, outs = refs[:count], refs[count], refs[count + 1 : -3]
+        held, sems, adj_sems = refs[-3:]
+        pool = outs[parts] if fresh else source_refs[0]
+
+        def first(k):
+            return (k ^ col_ref[0]) * per_part + chunk * per_chunk
+
+        def fetch(t, k):
+            return pltpu.make_async_copy(
+                adj_ref.at[first(k) + t], held.at[t, k], adj_sems.at[t, k]
             )
-            left = jnp.concatenate([adj_refs[k][0, q] for q in range(per_block)], axis=1)
-            outs[k][...] = jnp.dot(left, right, preferred_element_type=F32).astype(BF16)
-
-    def adj_spec(k):
-        return pl.BlockSpec(
-            (1, per_block, tile, tile), lambda t, c, r: (tile_of(k, t, c), 0, 0, 0)
-        )
-
-    return pl.pallas_call(
-        kernel,
-        out_shape=[jax.ShapeDtypeStruct((chunk_rows, width), BF16)] * parts,
+
+        copies = []
+        if fresh:
+            own, step = source_refs[0].shape[0], source_refs[1].shape[0]
+            targets = [pool.at[:own]]
+            for n in range(1, count):
+                targets.append(pool.at[own + n * step : own + (n + 1) * step])
+            copies = begin(source_refs, targets, sems)
+        for t in range(per_chunk):
+            for k in range(parts):
+                fetch(t, k).start()
+        for copy in copies:
+            copy.wait()
+
+        @pl.loop(0, per_chunk)
+        def _(t):
+            for k in range(parts):
+                fetch(t, k).wait()
+            for k in range(parts):
+                b = first(k) + t
+                right = jnp.concatenate(
+                    [pool[rows_at(colref_ref[q, b], tile), :] for q in range(per_block)], axis=0
+                )
+                left = jnp.concatenate([held[t, k, q] for q in range(per_block)], axis=1)
+                result = jnp.dot(left, right, preferred_element_type=F32)
+                outs[k][rows_at(t, tile), :] = result.astype(BF16)
+
+    return pl.pallas_call(
+        kernel,
+        out_shape=[jax.ShapeDtypeStruct(shape, BF16) for shape in shapes],
         grid_spec=pltpu.PrefetchScalarGridSpec(
             num_scalar_prefetch=2,
-            grid=(per_chunk,),
-            in_specs=[full(feats.shape)]
-            + [full(a.shape) for a in arrived]
-            + [adj_spec(k) for k in range(parts)],
-            out_specs=[pl.BlockSpec((tile, width), lambda t, c, r: (t, 0))] * parts,
-            scratch_shapes=[pltpu.VMEM((own + (count + 1) * step, width), BF16)],
-        ),
-        compiler_params=params(1),
+            grid=(1,),
+            in_specs=([ANY] * count if fresh else [full(sources[0].shape)]) + [ANY],
+            out_specs=[full(shape) for shape in shapes],
+            scratch_shapes=[
+                pltpu.VMEM((per_chunk, parts, per_block, tile, tile), BF16),
+                pltpu.SemaphoreType.DMA((count,)),
+                pltpu.SemaphoreType.DMA((per_chunk, parts)),
+            ],
+        ),
+        compiler_params=params(),
         name="aggregate",
-    )(col, colref, feats, *arrived, *[adj] * parts)
+    )(col, colref, *sources, adj)
 
 
 def permuted(w_ref, col_ref, parts, width):
@@ -196,7 +224,7 @@
             + [pl.BlockSpec((rows, width), lambda i, c: (i, 0))] * parts,
         ),
         input_output_aliases=aliases,
-        compiler_params=params(1),
+        compiler_params=params(),
         name="dense",
     )(*args)
 
@@ -244,7 +272,7 @@
             in_specs=[full(a.shape) for a in args],
             out_specs=[full(o.shape) for o in out_shape],
         ),
-        compiler_params=params(1),
+        compiler_params=params(),
         name="weights",
     )(col, row, *args)
 
@@ -267,110 +295,120 @@
             in_specs=[full(keep.shape)] * 2,
             out_specs=[full((rows, hidden))] * chips,
         ),
-        compiler_params=params(1),
+        compiler_params=params(),
         name="combine",
     )(row, keep, received)
 
 
-def assemble(row, pieces):
-    rows, hidden = pieces[0].shape
-    chips = len(pieces)
+def widen(row, mine, other):
+    rows, hidden = mine[0].shape
+    chips = len(mine)
 
     def kernel(row_ref, *refs):
+        sources, outs = refs[: 2 * chips], refs[2 * chips : 2 * chips + 2]
+        pieces, wide, sems, out_sems = refs[2 * chips + 2 :]
+        copies = begin(sources, [pieces.at[n] for n in range(2 * chips)], sems)
+        even = row_ref[0] % 2 == 0
+        writes = []
         for q in range(chips):
-            refs[-1][rows_at((row_ref[0] // 2) ^ q, rows), :] = refs[q][...]
-
-    return pl.pallas_call(
-        kernel,
-        out_shape=jax.ShapeDtypeStruct((chips * rows, hidden), BF16),
+            at = rows_at((row_ref[0] // 2) ^ q, rows)
+            copies[q].wait()
+            copies[chips + q].wait()
+            first, second = pieces[q].astype(F32), pieces[chips + q].astype(F32)
+            wide[0, q] = jnp.where(even, first, second)
+            wide[1, q] = jnp.where(even, second, first)
+            for n, out in enumerate(outs):
+                writes.append(
+                    pltpu.make_async_copy(wide.at[n, q], out.at[at], out_sems.at[n, q])
+                )
+                writes[-1].start()
+        for write in writes:
+            write.wait()
+
+    return pl.pallas_call(
+        kernel,
+        out_shape=[jax.ShapeDtypeStruct((chips * rows, hidden), F32)] * 2,
         grid_spec=pltpu.PrefetchScalarGridSpec(
             num_scalar_prefetch=1,
             grid=(1,),
-            in_specs=[full((rows, hidden))] * chips,
-            out_specs=full((chips * rows, hidden)),
-        ),
-        compiler_params=params(1),
-        name="assemble",
-    )(row, *pieces)
-
-
-def widen(row, mine, other):
-    def kernel(row_ref, mine_ref, other_ref, self_ref, neigh_ref):
-        even = row_ref[0] % 2 == 0
-        first, second = mine_ref[...].astype(F32), other_ref[...].astype(F32)
-        self_ref[...] = jnp.where(even, first, second)
-        neigh_ref[...] = jnp.where(even, second, first)
-
-    return pl.pallas_call(
-        kernel,
-        out_shape=[jax.ShapeDtypeStruct(mine.shape, F32)] * 2,
-        grid_spec=pltpu.PrefetchScalarGridSpec(
-            num_scalar_prefetch=1,
-            grid=(1,),
-            in_specs=[full(mine.shape)] * 2,
-            out_specs=[full(mine.shape)] * 2,
-        ),
-        compiler_params=params(1),
+            in_specs=[ANY] * (2 * chips),
+            out_specs=[ANY] * 2,
+            scratch_shapes=[
+                pltpu.VMEM((2 * chips, rows, hidden), BF16),
+                pltpu.VMEM((2, chips, rows, hidden), F32),
+                pltpu.SemaphoreType.DMA((2 * chips,)),
+                pltpu.SemaphoreType.DMA((2, chips)),
+            ],
+        ),
+        compiler_params=params(),
         name="widen",
-    )(row, mine, other)
-
-
-def pull(col, colref, grads, adj, partitions, cap, chunk, before):
+    )(row, *mine, *other)
+
+
+def pull(col, row, colref, grads, adj, partitions, cap, chunk, before):
     blocks, per_block, tile, _ = adj.shape
     parts = len(grads)
-    _, width = grads[0].shape
+    chunk_rows, width = grads[0].shape
     per_part = blocks // parts
     steps = per_part // CHUNKS
     last = chunk == CHUNKS - 1
     pool = blocks + partitions * cap
     extra = [] if before is None else [before]
 
-    def kernel(col_ref, colref_ref, *refs):
-        g_refs, adj_refs = refs[:parts], refs[parts : 2 * parts]
-        refs = refs[2 * parts :]
-        before_ref = refs[: len(extra)]
-        outs, acc, sem = refs[len(extra) : -2], refs[-2], refs[-1]
-        t = pl.program_id(0)
-
-        @pl.when(t == 0)
-        def _():
-            if extra:
-                copy = pltpu.make_async_copy(before_ref[0], acc, sem)
-                copy.start()
-                copy.wait()
-            else:
-                acc[...] = jnp.zeros_like(acc)
-
-        for k in range(parts):
-            b = (k ^ col_ref[0]) * per_part + chunk * steps + t
-            turned = g_refs[k][rows_at(t, tile), :].T
-            for q in range(0, per_block, 2):
-                pair = jnp.concatenate([adj_refs[k][0, q], adj_refs[k][0, q + 1]], axis=1)
-                both = jnp.dot(turned, pair, preferred_element_type=F32)
-                acc[colref_ref[b, q]] += both[:, :tile]
-                acc[colref_ref[b, q + 1]] += both[:, tile:]
-
-        @pl.when(t == steps - 1)
-        def _():
-            if last:
-                for n, out in enumerate(outs):
-                    first = blocks + n * cap if n else 0
-                    for s in range(out.shape[0] // tile):
-                        out[s * tile : (s + 1) * tile, :] = acc[first + s].T.astype(BF16)
-            else:
-                copy = pltpu.make_async_copy(acc, outs[0], sem)
-                copy.start()
-                copy.wait()
-
-    def adj_spec(k):
-        return pl.BlockSpec(
-            (1, per_block, tile, tile),
-            lambda t, c, r: ((k ^ c[0]) * per_part + chunk * steps + t, 0, 0, 0),
-        )
+    def kernel(col_ref, row_ref, colref_ref, *refs):
+        g_refs, adj_ref, refs = refs[:parts], refs[parts], refs[parts + 1 :]
+        before_ref, outs = refs[: len(extra)], refs[len(extra) : -5]
+        grad, acc, held, sems, adj_sems = refs[-5:]
+
+        def first(k):
+            return (k ^ col_ref[0]) * per_part + chunk * steps
+
+        def fetch(t, k):
+            return pltpu.make_async_copy(
+                adj_ref.at[first(k) + t], held.at[t, k], adj_sems.at[t, k]
+            )
+
+        sources, targets = list(g_refs), [grad.at[k] for k in range(parts)]
+        if extra:
+            sources.append(before_ref[0])
+            targets.append(acc)
+        copies = begin(sources, targets, sems)
+        for t in range(steps):
+            for k in range(parts):
+                fetch(t, k).start()
+        if not extra:
+            acc[...] = jnp.zeros_like(acc)
+        for copy in copies:
+            copy.wait()
+
+        @pl.loop(0, steps)
+        def _(t):
+            for k in range(parts):
+                fetch(t, k).wait()
+            for k in range(parts):
+                b = first(k) + t
+                turned = grad[k, rows_at(t, tile), :].T
+                for q in range(0, per_block, 2):
+                    pair = jnp.concatenate([held[t, k, q], held[t, k, q + 1]], axis=1)
+                    both = jnp.dot(turned, pair, preferred_element_type=F32)
+                    acc[colref_ref[q, b]] += both[:, :tile]
+                    acc[colref_ref[q + 1, b]] += both[:, tile:]
+
+        if last:
+            local_ref, remote_ref = outs
+            for s in range(blocks):
+                local_ref[s * tile : (s + 1) * tile, :] = acc[s].T.astype(BF16)
+            for k in range(partitions):
+                for s in range(cap):
+                    remote_ref[k ^ row_ref[0], s * tile : (s + 1) * tile, :] = (
+                        acc[blocks + k * cap + s].T.astype(BF16)
+                    )
+        else:
+            load([acc], [outs[0]], sems)
 
     if last:
         out_shape = [jax.ShapeDtypeStruct((blocks * tile, width), BF16)]
-        out_shape += [jax.ShapeDtypeStruct((cap * tile, width), BF16)] * (partitions - 1)
+        out_shape += [jax.ShapeDtypeStruct((partitions, cap * tile, width), BF16)]
         out_specs = [full(o.shape) for o in out_shape]
     else:
         out_shape = [jax.ShapeDtypeStruct((pool, width, tile), F32)]
@@ -379,59 +417,64 @@
         kernel,
         out_shape=out_shape,
         grid_spec=pltpu.PrefetchScalarGridSpec(
-            num_scalar_prefetch=2,
-            grid=(steps,),
-            in_specs=[full(g.shape) for g in grads]
-            + [adj_spec(k) for k in range(parts)]
-            + [ANY] * len(extra),
+            num_scalar_prefetch=3,
+            grid=(1,),
+            in_specs=[ANY] * parts + [ANY] + [ANY] * len(extra),
             out_specs=out_specs,
             scratch_shapes=[
+                pltpu.VMEM((parts, chunk_rows, width), BF16),
                 pltpu.VMEM((pool, width, tile), F32),
-                pltpu.SemaphoreType.DMA(()),
+                pltpu.VMEM((steps, parts, per_block, tile, tile), BF16),
+                pltpu.SemaphoreType.DMA((parts + 1,)),
+                pltpu.SemaphoreType.DMA((steps, parts)),
             ],
         ),
-        compiler_params=params(1),
+        compiler_params=params(),
         name="pull",
-    )(col, colref, *grads, *[adj] * parts, *extra)
+    )(col, row, colref, *grads, adj, *extra)
 
 
 def finish(col, row, ids, self_parts, local, returned, tile, cap):
     parts = len(self_parts)
-    rows, _ = self_parts[0].shape
-    count = len(returned)
+    rows, width = self_parts[0].shape
+    count = returned.shape[0]
 
     def kernel(col_ref, row_ref, *refs):
         id_refs, refs = refs[: len(ids)], refs[len(ids) :]
-        s_refs, local_ref = refs[:parts], refs[parts]
-        returned_refs, out_ref = refs[parts + 1 : -1], refs[-1]
+        s_refs, (local_ref, returned_ref, out_ref, own, back, sems) = refs[:parts], refs[parts:]
+        load([*s_refs, returned_ref], [*[own.at[k] for k in range(parts)], back], sems)
         where = id_rows(id_refs)
         for k in range(parts):
             at = rows_at(k ^ col_ref[0], rows)
-            out_ref[at, :] = s_refs[k][...].astype(F32) + local_ref[at, :].astype(F32)
-        for n in range(count):
-            ref, j = where[n + 1]
+            out_ref[at, :] = own[k].astype(F32) + local_ref[at, :].astype(F32)
+        for n in range(1, count):
+            ref, j = where[n]
             for s in range(cap):
                 target = ref[j, row_ref[0] * cap + s]
 
                 @pl.when(target >= 0)
                 def _():
-                    out_ref[rows_at(target, tile), :] += returned_refs[n][
-                        s * tile : (s + 1) * tile, :
+                    out_ref[rows_at(target, tile), :] += back[
+                        n ^ row_ref[0], s * tile : (s + 1) * tile, :
                     ].astype(F32)
 
-    args = [*self_parts, local, *returned]
     return pl.pallas_call(
         kernel,
         out_shape=jax.ShapeDtypeStruct(local.shape, F32),
         grid_spec=pltpu.PrefetchScalarGridSpec(
             num_scalar_prefetch=2,
             grid=(1,),
-            in_specs=[SMEM] * len(ids) + [full(a.shape) for a in args],
+            in_specs=[SMEM] * len(ids) + [ANY] * parts + [full(local.shape), ANY],
             out_specs=full(local.shape),
-        ),
-        compiler_params=params(1),
+            scratch_shapes=[
+                pltpu.VMEM((parts, rows, width), BF16),
+                pltpu.VMEM(returned.shape, BF16),
+                pltpu.SemaphoreType.DMA((parts + 1,)),
+            ],
+        ),
+        compiler_params=params(),
         name="finish",
-    )(col, row, *ids, *args)
+    )(col, row, *ids, *self_parts, local, returned)
 
 
 def swap(x, axis, k):
@@ -474,16 +517,22 @@
         ids.append(swap(known, "rows", hop))
         known = jnp.concatenate([known, ids[-1]], axis=0)
         hop *= 2
-    outgoing = select_tiles(row, ids, feats, tile, cap)
+    outgoing = select_tiles(
+        row, ids, pltpu.with_memory_space_constraint(feats, pltpu.HBM), tile, cap
+    )
     arrived = exchange([None, *outgoing], "rows")[1:]
-    slot = jnp.maximum(colref - blocks, 0)
+    pooled = colref.T
+    slot = jnp.maximum(pooled - blocks, 0)
     slot = ((slot // cap) ^ row_index) * cap + slot % cap
-    places = jnp.where(colref < blocks, colref, blocks + slot).astype(jnp.int32)
-
-    agg_chunks = []
+    places = jnp.where(pooled < blocks, pooled, blocks + slot).astype(jnp.int32)
+
+    adj_vals = pltpu.with_memory_space_constraint(adj_vals, pltpu.HBM)
+    agg_chunks, sources = [], [feats, *arrived]
+    pool_rows = (blocks + partitions * cap) * tile
     for h in range(CHUNKS):
-        pieces = aggregate(col, places, feats, arrived, adj_vals, h, parts)
-        agg_chunks.append(exchange(pieces, "cols"))
+        pieces = aggregate(col, places, sources, adj_vals, h, parts, pool_rows)
+        sources = pieces[parts:] or sources
+        agg_chunks.append(exchange(pieces[:parts], "cols"))
     act, grads, grad_chunks = None, [], []
     for h in range(CHUNKS):
         act, g, *back = dense(
@@ -499,13 +548,18 @@
     partial = tree_sum(exchange(pieces, "rows", 2)).astype(BF16)
     mine = tree_sum([p.astype(F32) for p in exchange([partial] * parts, "cols")])
     mine = (mine * (1.0 / math.sqrt(total_nodes))).astype(BF16)
-    half = assemble(row, exchange([mine] * chips, "rows", 2))
-    grad_self_w, grad_neigh_w = widen(row, half, exchange([half, half], "rows")[1])
+    pieces = exchange([mine] * chips, "rows", 2)
+    other = []
+    for piece in pieces:
+        other.append(swap(piece, "rows", 1))
+    grad_self_w, grad_neigh_w = widen(row, pieces, other)
 
     before = None
     for h in range(CHUNKS):
-        before, *remote = pull(col, places, grad_chunks[h], adj_vals, partitions, cap, h, before)
-    returned = exchange([None, *remote], "rows")[1:]
+        before, *remote = pull(
+            col, row, places, grad_chunks[h], adj_vals, partitions, cap, h, before
+        )
+    returned = lax.all_to_all(remote[0], "rows", 0, 0, tiled=True)
     grad_feats = finish(col, row, ids, self_parts, before, returned, tile, cap)
     return (act, grad_self_w, grad_neigh_w, grad_feats)
 

time: 192 us -> 148 us (0.77); the launches traced: 189 us -> 148 us
  waiting for transfers between devices: 55.8 us -> 34.8 us
  Pallas kernels: 62.3 us -> 43.4 us
  starting transfers between devices: 58.8 us -> 64 us
  local copies, waits for them, and re-layouts: 9.02 us -> 4.27 us
    ppermute x43 -> x39, waiting for transfers between devices: 55.8 us -> 34.8 us  [swap(): return lax.ppermute(x, axis, [(i, i ^ k) for i in range(n)])]
    pallas_call x4 -> x3, Pallas kernels: 20 us -> 14.8 us  [the longest x2 11.7 us: aggregate(): pl.pallas_call(kernel, out_shape=[jax.ShapeDtypeStruct(shape, BF16) for s...]
    pallas_call x2, Pallas kernels: 19.5 us -> 14.4 us  [pull(): pl.pallas_call(kernel, out_shape=out_shape, grid_spec=pltpu.PrefetchScala...]
    unnamed x102 -> x29, local copies, waits for them, and re-layouts: 8.93 us -> 4.18 us
    all_to_all x0 -> x1, starting transfers between devices: none -> 3.51 us  [body(): returned = lax.all_to_all(remote[0], 'rows', 0, 0, tiled=True)]
    pallas_call x2, Pallas kernels: 8.25 us -> 5.77 us  [dense(): pl.pallas_call(kernel, out_shape=[jax.ShapeDtypeStruct((chunk_rows * CHUN...]
    pallas_call x1, Pallas kernels: 2.6 us -> 0.15 us  [combine(): pl.pallas_call(kernel, out_shape=[jax.ShapeDtypeStruct((rows, hidden), F3...]
    pallas_call x1, Pallas kernels: 5.98 us -> 3.93 us  [weights(): pl.pallas_call(kernel, out_shape=out_shape, grid_spec=pltpu.PrefetchScala...]
  transfers between devices with their start and end apart: 44 -> 41, of which waited for: 19 -> 13; matrix products, arithmetic and copies ran while one was open for 1% -> 1% of each run, Pallas kernels for 25% -> 22%
where the time goes in v3:
time: 148 us
  starting transfers between devices  64 us (43%)
  Pallas kernels  43.4 us (29%)
  waiting for transfers between devices  34.8 us (24%)
  local copies, waits for them, and re-layouts  4.27 us (3%)
    ppermute x39, starting transfers between devices, swap(): return lax.ppermute(x, axis, [(i, i ^ k) for i in range(n)])  54 us
    ppermute x39, waiting for transfers between devices, swap(): return lax.ppermute(x, axis, [(i, i ^ k) for i in range(n)])  34.8 us
    pallas_call x2, Pallas kernels, pull(): pl.pallas_call(kernel, out_shape=out_shape, grid_spec=pltpu.PrefetchScala...  14.4 us
    pallas_call x2, Pallas kernels, aggregate(): pl.pallas_call(kernel, out_shape=[jax.ShapeDtypeStruct(shape, BF16) for s...  11.7 us
    all_to_all x1, starting transfers between devices, body(): lax.all_to_all(feats.reshape(parts, node_rows // parts, width), 'cols', 0...  6.49 us
    pallas_call x2, Pallas kernels, dense(): pl.pallas_call(kernel, out_shape=[jax.ShapeDtypeStruct((chunk_rows * CHUN...  5.77 us
    unnamed x29, local copies, waits for them, and re-layouts  4.18 us
    pallas_call x1, Pallas kernels, weights(): pl.pallas_call(kernel, out_shape=out_shape, grid_spec=pltpu.PrefetchScala...  3.93 us
  transfers between devices with their start and end apart: 41, of which 13 were waited for; matrix products, arithmetic and copies ran while one was open for 1% of the time, Pallas kernels for 22%

profile of v3, /device:TPU:0, one launch (start us, length us, event | category | flops | bytes accessed | tf_op | source)
XLA Modules:
  0.0 147.6 jit_solution(652685504655555159)
XLA Ops:
  0.7 6.5 %all-to-all-start = ((bf16[4,1024,128]{2,1,0:T(8,128)(2,1)}), bf16[4,1024,128]{2,1,0:T(8,128)(2,1)S(1)}, u32[]{:S(2)}, u32[]{:S(2)}) async-start(bf16[4,1024,128]{2,1,0:T(8,128)(2,1)} %bitcast.24), calls=%async_computation | async-start | bytes 2097152 | tf_op jit(solution)/shard_map/all_to_all | solution.py:510
  7.1 0.8 copy.13
  8.1 1.1 collective-permute-done.refs_1_
  9.2 1.6 %collective-permute-start.1 = (s32[2,128]{1,0:T(2,128)S(1)}, s32[2,128]{1,0:T(2,128)S(1)}, u32[]{:S(2)}, u32[]{:S(2)}) collective-permute-start(s32[2,128]{1,0:T(2,128)S(1)} %pad_add_fusion.1), channel_id=1, source_target_pairs={{0,8},{4,12},{8,0},{12,4},{16,24},{20,28},{24,16},{28,20},{1,9},{5... | collective-permute-start | bytes 3080 | tf_op jit(solution)/shard_map/ppermute | solution.py:482
  10.8 2.1 %collective-permute-done.1.refs_2_ = s32[2,128]{1,0:T(2,128)S(1)} collective-permute-done((s32[2,128]{1,0:T(2,128)S(1)}, s32[2,128]{1,0:T(2,128)S(1)}, u32[]{:S(2)}, u32[]{:S(2)}) %collective-permute-start.1) | collective-permute-done | bytes 1056 | tf_op jit(solution)/shard_map/ppermute | solution.py:482
  12.9 1.6 %collective-permute-start.2 = (s32[4,128]{1,0:T(4,128)S(1)}, s32[4,128]{1,0:T(4,128)S(1)}, u32[]{:S(2)}, u32[]{:S(2)}) collective-permute-start(s32[4,128]{1,0:T(4,128)S(1)} %pad_add_fusion), channel_id=1, source_target_pairs={{0,16},{4,20},{8,24},{12,28},{16,0},{20,4},{24,8},{28,12},{1,17},{... | collective-permute-start | bytes 6152 | tf_op jit(solution)/shard_map/ppermute | solution.py:482
  14.5 2.1 %collective-permute-done.2.refs_3_ = s32[4,128]{1,0:T(4,128)S(1)} collective-permute-done((s32[4,128]{1,0:T(4,128)S(1)}, s32[4,128]{1,0:T(4,128)S(1)}, u32[]{:S(2)}, u32[]{:S(2)}) %collective-permute-start.2) | collective-permute-done | bytes 2080 | tf_op jit(solution)/shard_map/ppermute | solution.py:482
  16.5 1.8 %select_tiles.1 = (bf16[256,128]{1,0:T(8,128)(2,1)S(1)}, bf16[256,128]{1,0:T(8,128)(2,1)S(1)}, bf16[256,128]{1,0:T(8,128)(2,1)S(1)}, bf16[256,128]{1,0:T(8,128)(...) custom-call(s32[1]{0:T(128)} %bitcast.3.row_ref, ...), custom_call_target="tpu_custom_call" | custom-call | tf_op jit(solution)/shard_map/select_tiles/pallas_call | solution.py:77
  18.4 1.5 %collective-permute-start.4 = (bf16[256,128]{1,0:T(8,128)(2,1)S(1)}, bf16[256,128]{1,0:T(8,128)(2,1)S(1)}, u32[]{:S(2)}, u32[]{:S(2)}) collective-permute-start(bf16[256,128]{1,0:T(8,128)(2,1)S(1)} %get-tuple-element.47), channel_id=1, source_target_pairs={{0,8},{4,12},{8,0},{12,4},{16,24},{20,28},{24,16},{28,20},{1,9},{5... | collective-permute-start | bytes 196616 | tf_op jit(solution)/shard_map/ppermute | solution.py:482
  20.2 1.4 collective-permute-start.6
  21.9 2.4 %collective-permute-start.8 = (bf16[256,128]{1,0:T(8,128)(2,1)S(1)}, bf16[256,128]{1,0:T(8,128)(2,1)S(1)}, u32[]{:S(2)}, u32[]{:S(2)}) collective-permute-start(bf16[256,128]{1,0:T(8,128)(2,1)S(1)} %get-tuple-element.51), channel_id=1, source_target_pairs={{0,24},{4,28},{8,16},{12,20},{16,8},{20,12},{24,0},{28,4},{1,25},{... | collective-permute-start | bytes 196616 | tf_op jit(solution)/shard_map/ppermute | solution.py:482
  24.7 1.1 collective-permute-done.7.refs_5_
  25.8 1.6 %collective-permute-done.8.refs_6_ = bf16[256,128]{1,0:T(8,128)(2,1)S(1)} collective-permute-done((bf16[256,128]{1,0:T(8,128)(2,1)S(1)}, bf16[256,128]{1,0:T(8,128)(2,1)S(1)}, u32[]{:S(2)}, u32[]{:S(2)}) %collective-permute-start.8) | collective-permute-done | bytes 65568 | tf_op jit(solution)/shard_map/ppermute | solution.py:482
  27.4 1.9 %collective-permute-done.9.refs_7_ = bf16[256,128]{1,0:T(8,128)(2,1)S(1)} collective-permute-done((bf16[256,128]{1,0:T(8,128)(2,1)S(1)}, bf16[256,128]{1,0:T(8,128)(2,1)S(1)}, u32[]{:S(2)}, u32[]{:S(2)}) %collective-permute-start.9) | collective-permute-done | bytes 65568 | tf_op jit(solution)/shard_map/ppermute | solution.py:482
  29.3 5.9 %aggregate.2 = (bf16[512,128]{1,0:T(8,128)(2,1)S(1)}, bf16[512,128]{1,0:T(8,128)(2,1)S(1)}, bf16[512,128]{1,0:T(8,128)(2,1)S(1)}, bf16[512,128]{1,0:T(8,128)(2,1)S(1)}, bf16[6144,128]{1,0:T(8,128)(2,1)S(1)}) custom-call(s32[1]{0:T(128)} %bitcast.col_ref, s32[16,32]{1,0:T(8,128)S(1)} %compare_select_fusion.colref_ref, bf16[4096,128]{1,0:T(8,128)(2,1)S(1)} %copy-done, ...), custom_call_target="tpu_custom_call" | custom-call | tf_op jit(solution)/shard_map/aggregate/pallas_call | solution.py:138
  35.2 2.1 %collective-permute-start.13 = (bf16[512,128]{1,0:T(8,128)(2,1)S(1)}, bf16[512,128]{1,0:T(8,128)(2,1)S(1)}, u32[]{:S(2)}, u32[]{:S(2)}) collective-permute-start(bf16[512,128]{1,0:T(8,128)(2,1)S(1)} %get-tuple-element.59), channel_id=1, source_target_pairs={{0,1},{1,0},{2,3},{3,2},{4,5},{5,4},{6,7},{7,6},{8,9},{9,8},{10,11... | collective-permute-start | bytes 393224 | tf_op jit(solution)/shard_map/ppermute | solution.py:482
  37.3 2.4 %collective-permute-start.14 = (bf16[512,128]{1,0:T(8,128)(2,1)S(1)}, bf16[512,128]{1,0:T(8,128)(2,1)S(1)}, u32[]{:S(2)}, u32[]{:S(2)}) collective-permute-start(bf16[512,128]{1,0:T(8,128)(2,1)S(1)} %get-tuple-element.60), channel_id=1, source_target_pairs={{0,2},{1,3},{2,0},{3,1},{4,6},{5,7},{6,4},{7,5},{8,10},{9,11},{10,... | collective-permute-start | bytes 393224 | tf_op jit(solution)/shard_map/ppermute | solution.py:482
  39.7 5.8 %aggregate.3 = (bf16[512,128]{1,0:T(8,128)(2,1)S(1)}, bf16[512,128]{1,0:T(8,128)(2,1)}, bf16[512,128]{1,0:T(8,128)(2,1)}, bf16[512,128]{1,0:T(8,128)(2,1)}) custom-call(s32[1]{0:T(128)} %bitcast.col_ref, s32[16,32]{1,0:T(8,128)S(1)} %compare_select_fusion.colref_ref, bf16[6144,128]{1,0:T(8,128)(2,1)S(1)} %get-tuple-element.53.refs_0_, ...), custom_call_target="tpu_custom_call" | custom-call | tf_op jit(solution)/shard_map/aggregate/pallas_call | solution.py:138
  46.2 1.1 collective-permute-start.10
  47.3 3.3 %collective-permute-start.11 = (bf16[512,128]{1,0:T(8,128)(2,1)}, bf16[512,128]{1,0:T(8,128)(2,1)}, u32[]{:S(2)}, u32[]{:S(2)}) collective-permute-start(bf16[512,128]{1,0:T(8,128)(2,1)} %get-tuple-element.56), channel_id=1, source_target_pairs={{0,2},{1,3},{2,0},{3,1},{4,6},{5,7},{6,4},{7,5},{8,10},{9,11},{10,... | collective-permute-start | bytes 393224 | tf_op jit(solution)/shard_map/ppermute | solution.py:482
  51.3 0.9 copy-done.5
  52.2 2.4 %dense.2 = (bf16[1024,512]{1,0:T(8,128)(2,1)}, bf16[512,512]{1,0:T(8,128)(2,1)S(1)}, bf16[512,128]{1,0:T(8,128)(2,1)S(1)}, bf16[512,128]{1,0:T(8,128)(2,1)S(1)},...) custom-call(s32[1]{0:T(128)} %bitcast.col_ref, bf16[4,1024,128]{2,1,0:T(8,128)(2,1)S(1)} %all-to-all-done.refs_0_, ...), custom_call_target="tpu_custom_call" | custom-call | tf_op jit(solution)/shard_map/dense/pallas_call | solution.py:209
  54.6 6.9 %collective-permute-done.11.refs_3_.refs_7_ = bf16[512,128]{1,0:T(8,128)(2,1)} collective-permute-done((bf16[512,128]{1,0:T(8,128)(2,1)}, bf16[512,128]{1,0:T(8,128)(2,1)}, u32[]{:S(2)}, u32[]{:S(2)}) %collective-permute-start.11) | collective-permute-done | bytes 131104 | tf_op jit(solution)/shard_map/ppermute | solution.py:482
  61.5 3.4 %dense.3 = (bf16[1024,512]{1,0:T(8,128)(2,1)}, bf16[512,512]{1,0:T(8,128)(2,1)S(1)}, bf16[512,128]{1,0:T(8,128)(2,1)S(1)}, bf16[512,128]{1,0:T(8,128)(2,1)S(1)},...) custom-call(s32[1]{0:T(128)} %bitcast.col_ref, ...), custom_call_target="tpu_custom_call", output_to_operand_aliasing={{0}: (9, {})} | custom-call | tf_op jit(solution)/shard_map/dense/pallas_call | solution.py:209
  64.9 3.9 %weights.1 = (f32[512,512]{1,0:T(8,128)S(1)}, f32[512,512]{1,0:T(8,128)S(1)}, bf16[1024,128]{1,0:T(8,128)(2,1)S(1)}, bf16[1024,128]{1,0:T(8,128)(2,1)}, bf16[102...) custom-call(s32[1]{0:T(128)} %bitcast.col_ref, s32[1]{0:T(128)} %bitcast.3.row_ref, ...), custom_call_target="tpu_custom_call" | custom-call | tf_op jit(solution)/shard_map/weights/pallas_call | solution.py:266
  68.8 2.7 %collective-permute-done.16.received_ref = f32[512,512]{1,0:T(8,128)S(1)} collective-permute-done((f32[512,512]{1,0:T(8,128)S(1)}, f32[512,512]{1,0:T(8,128)S(1)}, u32[]{:S(2)}, u32[]{:S(2)}) %collective-permute-start.16) | collective-permute-done | bytes 1048608 | tf_op jit(solution)/shard_map/ppermute | solution.py:482
  72.4 1.7 %collective-permute-start.18 = (f32[128,512]{1,0:T(8,128)S(1)}, f32[128,512]{1,0:T(8,128)S(1)}, u32[]{:S(2)}, u32[]{:S(2)}) collective-permute-start(f32[128,512]{1,0:T(8,128)S(1)} %get-tuple-element.70), channel_id=1, source_target_pairs={{0,16},{4,20},{8,24},{12,28},{16,0},{20,4},{24,8},{28,12},{1,17},{... | collective-permute-start | bytes 786440 | tf_op jit(solution)/shard_map/ppermute | solution.py:482
  74.1 1.1 collective-permute-start.19
  75.2 2.3 %collective-permute-start.36 = (bf16[512,128]{1,0:T(8,128)(2,1)S(1)}, bf16[512,128]{1,0:T(8,128)(2,1)S(1)}, u32[]{:S(2)}, u32[]{:S(2)}) collective-permute-start(bf16[512,128]{1,0:T(8,128)(2,1)S(1)} %get-tuple-element.83), channel_id=1, source_target_pairs={{0,1},{1,0},{2,3},{3,2},{4,5},{5,4},{6,7},{7,6},{8,9},{9,8},{10,11... | collective-permute-start | bytes 393224 | tf_op jit(solution)/shard_map/ppermute | solution.py:482
  77.5 1.0 collective-permute-start.37
  78.5 3.3 %collective-permute-done.36.refs_1_ = bf16[512,128]{1,0:T(8,128)(2,1)S(1)} collective-permute-done((bf16[512,128]{1,0:T(8,128)(2,1)S(1)}, bf16[512,128]{1,0:T(8,128)(2,1)S(1)}, u32[]{:S(2)}, u32[]{:S(2)}) %collective-permute-start.36) | collective-permute-done | bytes 131104 | tf_op jit(solution)/shard_map/ppermute | solution.py:482
  81.8 2.1 %collective-permute-start.38 = (bf16[512,128]{1,0:T(8,128)(2,1)S(1)}, bf16[512,128]{1,0:T(8,128)(2,1)S(1)}, u32[]{:S(2)}, u32[]{:S(2)}) collective-permute-start(bf16[512,128]{1,0:T(8,128)(2,1)S(1)} %get-tuple-element.85), channel_id=1, source_target_pairs={{0,3},{1,2},{2,1},{3,0},{4,7},{5,6},{6,5},{7,4},{8,11},{9,10},{10,... | collective-permute-start | bytes 393224 | tf_op jit(solution)/shard_map/ppermute | solution.py:482
  83.8 1.6 %collective-permute-start.33 = (bf16[512,128]{1,0:T(8,128)(2,1)S(1)}, bf16[512,128]{1,0:T(8,128)(2,1)S(1)}, u32[]{:S(2)}, u32[]{:S(2)}) collective-permute-start(bf16[512,128]{1,0:T(8,128)(2,1)S(1)} %get-tuple-element.79), channel_id=1, source_target_pairs={{0,1},{1,0},{2,3},{3,2},{4,5},{5,4},{6,7},{7,6},{8,9},{9,8},{10,11... | collective-permute-start | bytes 393224 | tf_op jit(solution)/shard_map/ppermute | solution.py:482
  86.1 3.4 %collective-permute-start.34 = (bf16[512,128]{1,0:T(8,128)(2,1)S(1)}, bf16[512,128]{1,0:T(8,128)(2,1)S(1)}, u32[]{:S(2)}, u32[]{:S(2)}) collective-permute-start(bf16[512,128]{1,0:T(8,128)(2,1)S(1)} %get-tuple-element.80), channel_id=1, source_target_pairs={{0,2},{1,3},{2,0},{3,1},{4,6},{5,7},{6,4},{7,5},{8,10},{9,11},{10,... | collective-permute-start | bytes 393224 | tf_op jit(solution)/shard_map/ppermute | solution.py:482
  89.5 1.4 collective-permute-start.35
  91.0 2.5 %collective-permute-start.22 = (bf16[128,512]{1,0:T(8,128)(2,1)S(1)}, bf16[128,512]{1,0:T(8,128)(2,1)S(1)}, u32[]{:S(2)}, u32[]{:S(2)}) collective-permute-start(bf16[128,512]{1,0:T(8,128)(2,1)S(1)} %add_convert_fusion), channel_id=1, source_target_pairs={{0,3},{1,2},{2,1},{3,0},{4,7},{5,6},{6,5},{7,4},{8,11},{9,10},{10,... | collective-permute-start | bytes 393224 | tf_op jit(solution)/shard_map/ppermute | solution.py:482
  93.5 8.6 %collective-permute-start.21 = (bf16[128,512]{1,0:T(8,128)(2,1)S(1)}, bf16[128,512]{1,0:T(8,128)(2,1)S(1)}, u32[]{:S(2)}, u32[]{:S(2)}) collective-permute-start(bf16[128,512]{1,0:T(8,128)(2,1)S(1)} %add_convert_fusion), channel_id=1, source_target_pairs={{0,2},{1,3},{2,0},{3,1},{4,6},{5,7},{6,4},{7,5},{8,10},{9,11},{10,... | collective-permute-start | bytes 393224 | tf_op jit(solution)/shard_map/ppermute | solution.py:482
  102.6 2.2 %collective-permute-done.34.refs_2_ = bf16[512,128]{1,0:T(8,128)(2,1)S(1)} collective-permute-done((bf16[512,128]{1,0:T(8,128)(2,1)S(1)}, bf16[512,128]{1,0:T(8,128)(2,1)S(1)}, u32[]{:S(2)}, u32[]{:S(2)}) %collective-permute-start.34) | collective-permute-done | bytes 131104 | tf_op jit(solution)/shard_map/ppermute | solution.py:482
  104.9 6.6 %pull.2.refs_5_ = f32[48,128,128]{2,1,0:T(8,128)S(1)} custom-call(s32[1]{0:T(128)} %bitcast.col_ref, s32[1]{0:T(128)} %bitcast.3.row_ref, s32[16,32]{1,0:T(8,128)S(1)} %compare_select_fusion.colref_ref, bf16[512,128]{1,0:T(8,128)(2,1)S(1)} %get-tuple-element.82.refs_0_, bf16[512,128]{1,0:T(8,128)(2,1)S(1)} %collective-permute-done.36.refs_1_, ...), custom_call_target="tpu_custom_call" | custom-call | tf_op jit(solution)/shard_map/pull/pallas_call | solution.py:416
  111.5 3.0 %collective-permute-start.31 = (bf16[1024,128]{1,0:T(8,128)(2,1)}, bf16[1024,128]{1,0:T(8,128)(2,1)S(1)}, u32[]{:S(2)}, u32[]{:S(2)}) collective-permute-start(bf16[1024,128]{1,0:T(8,128)(2,1)} %get-tuple-element.76), channel_id=1, source_target_pairs={{0,2},{1,3},{2,0},{3,1},{4,6},{5,7},{6,4},{7,5},{8,10},{9,11},{10,... | collective-permute-start | bytes 786440 | tf_op jit(solution)/shard_map/ppermute | solution.py:482
  114.5 7.8 %pull.3 = (bf16[4096,128]{1,0:T(8,128)(2,1)S(1)}, bf16[8,256,128]{2,1,0:T(8,128)(2,1)}) custom-call(s32[1]{0:T(128)} %bitcast.col_ref, s32[1]{0:T(128)} %bitcast.3.row_ref, s32[16,32]{1,0:T(8,128)S(1)} %compare_select_fusion.colref_ref, bf16[512,128]{1,0:T(8,128)(2,1)S(1)} %get-tuple-element.78.refs_0_, ...), custom_call_target="tpu_custom_call" | custom-call | tf_op jit(solution)/shard_map/pull/pallas_call | solution.py:416
  122.3 3.5 %all-to-all-start.1 = ((bf16[8,256,128]{2,1,0:T(8,128)(2,1)}), bf16[8,256,128]{2,1,0:T(8,128)(2,1)S(1)}, u32[]{:S(2)}, u32[]{:S(2)}) async-start(bf16[8,256,128]{2,1,0:T(8,128)(2,1)} %get-tuple-element.87), calls=%async_computation.1 | async-start | bytes 1048576 | tf_op jit(solution)/shard_map/all_to_all | solution.py:562
  125.8 1.5 %collective-permute-start.32 = (bf16[1024,128]{1,0:T(8,128)(2,1)}, bf16[1024,128]{1,0:T(8,128)(2,1)S(1)}, u32[]{:S(2)}, u32[]{:S(2)}) collective-permute-start(bf16[1024,128]{1,0:T(8,128)(2,1)} %get-tuple-element.77), channel_id=1, source_target_pairs={{0,3},{1,2},{2,1},{3,0},{4,7},{5,6},{6,5},{7,4},{8,11},{9,10},{10,... | collective-permute-start | bytes 786440 | tf_op jit(solution)/shard_map/ppermute | solution.py:482
  127.4 2.8 %collective-permute-start.25 = (bf16[128,512]{1,0:T(8,128)(2,1)S(1)}, bf16[128,512]{1,0:T(8,128)(2,1)S(1)}, u32[]{:S(2)}, u32[]{:S(2)}) collective-permute-start(bf16[128,512]{1,0:T(8,128)(2,1)S(1)} %multiply_convert_fusion.refs_0_), channel_id=1, source_target_pairs={{0,24},{4,28},{8,16},{12,20},{16,8},{20,12},{24,0},{28,4},{1,25},{... | collective-permute-start | bytes 393224 | tf_op jit(solution)/shard_map/ppermute | solution.py:482
  131.0 7.8 %collective-permute-done.25.refs_3_ = bf16[128,512]{1,0:T(8,128)(2,1)S(1)} collective-permute-done((bf16[128,512]{1,0:T(8,128)(2,1)S(1)}, bf16[128,512]{1,0:T(8,128)(2,1)S(1)}, u32[]{:S(2)}, u32[]{:S(2)}) %collective-permute-start.25) | collective-permute-done | bytes 131104 | tf_op jit(solution)/shard_map/ppermute | solution.py:482
  138.8 1.3 collective-permute-done.24.refs_2_
  141.9 2.5 %finish.1 = f32[4096,128]{1,0:T(8,128)} custom-call(s32[1]{0:T(128)} %bitcast.col_ref, s32[1]{0:T(128)} %bitcast.3.row_ref, s32[1,128]{1,0:T(1,128)S(1)} %copy-done.10, s32[1,128]{1,0:T(1,128)S(1)} %copy-done.12, s32[2,128]{1,0:T(2,128)S(1)} %collective-permute-done.1.refs_2_, s32[4,128]{1,0:T(4,128)S(1)} %collective-permute-done.2.refs_3_, ...), custom_call_target="tpu_custom_call" | custom-call | tf_op jit(solution)/shard_map/finish/pallas_call | solution.py:461
  144.5 3.1 %widen.1 = (f32[512,512]{1,0:T(8,128)}, f32[512,512]{1,0:T(8,128)}) custom-call(s32[1]{0:T(128)} %bitcast.3.row_ref, bf16[128,512]{1,0:T(8,128)(2,1)S(1)} %multiply_convert_fusion.refs_0_, bf16[128,512]{1,0:T(8,128)(2,1)S(1)} %collective-permute-done.23.refs_1_, bf16[128,512]{1,0:T(8,128)(2,1)S(1)} %collective-permute-done.24.refs_2_, ...), custom_call_target="tpu_custom_call" | custom-call | tf_op jit(solution)/shard_map/widen/pallas_call | solution.py:328
  (81 shorter events, 7.3 us)
Async XLA Ops:
  0.6 28.7 %copy-start = (bf16[4096,128]{1,0:T(8,128)(2,1)S(1)}, bf16[4096,128]{1,0:T(8,128)(2,1)}, u32[]{:S(2)}) copy-start(bf16[4096,128]{1,0:T(8,128)(2,1)} %refs_0_.1) | copy-start | bytes 3145732
  0.6 24.0 %copy-start.13 = (s32[32,16]{0,1:T(8,128)S(1)}, s32[32,16]{0,1:T(8,128)}, u32[]{:S(2)}) copy-start(s32[32,16]{0,1:T(8,128)} %param.9) | copy-start | bytes 6148
  0.7 50.6 %all-to-all-start = ((bf16[4,1024,128]{2,1,0:T(8,128)(2,1)}), bf16[4,1024,128]{2,1,0:T(8,128)(2,1)S(1)}, u32[]{:S(2)}, u32[]{:S(2)}) async-start(bf16[4,1024,128]{2,1,0:T(8,128)(2,1)} %bitcast.24), calls=%async_computation | async-start | bytes 2097152 | tf_op jit(solution)/shard_map/all_to_all | solution.py:510
  8.0 13.7 %copy-start.9 = (s32[1,128]{1,0:T(1,128)}, s32[1,128]{1,0:T(1,128)S(1)}, u32[]{:S(2)}) copy-start(s32[1,128]{1,0:T(1,128)S(1)} %pad.4.refs_0_) | copy-start | bytes 1540
  8.0 1.2 collective-permute-start
  9.2 12.5 %copy-start.11 = (s32[1,128]{1,0:T(1,128)}, s32[1,128]{1,0:T(1,128)S(1)}, u32[]{:S(2)}) copy-start(s32[1,128]{1,0:T(1,128)S(1)} %collective-permute-done.refs_1_) | copy-start | bytes 1540
  9.2 3.6 %collective-permute-start.1 = (s32[2,128]{1,0:T(2,128)S(1)}, s32[2,128]{1,0:T(2,128)S(1)}, u32[]{:S(2)}, u32[]{:S(2)}) collective-permute-start(s32[2,128]{1,0:T(2,128)S(1)} %pad_add_fusion.1), channel_id=1, source_target_pairs={{0,8},{4,12},{8,0},{12,4},{16,24},{20,28},{24,16},{28,20},{1,9},{5... | collective-permute-start | bytes 3080 | tf_op jit(solution)/shard_map/ppermute | solution.py:482
  12.9 3.6 %collective-permute-start.2 = (s32[4,128]{1,0:T(4,128)S(1)}, s32[4,128]{1,0:T(4,128)S(1)}, u32[]{:S(2)}, u32[]{:S(2)}) collective-permute-start(s32[4,128]{1,0:T(4,128)S(1)} %pad_add_fusion), channel_id=1, source_target_pairs={{0,16},{4,20},{8,24},{12,28},{16,0},{20,4},{24,8},{28,12},{1,17},{... | collective-permute-start | bytes 6152 | tf_op jit(solution)/shard_map/ppermute | solution.py:482
  18.3 3.6 %collective-permute-start.3 = (bf16[256,128]{1,0:T(8,128)(2,1)S(1)}, bf16[256,128]{1,0:T(8,128)(2,1)S(1)}, u32[]{:S(2)}, u32[]{:S(2)}) collective-permute-start(bf16[256,128]{1,0:T(8,128)(2,1)S(1)} %get-tuple-element.46), channel_id=1, source_target_pairs={{0,4},{4,0},{8,12},{12,8},{16,20},{20,16},{24,28},{28,24},{1,5},{5... | collective-permute-start | bytes 196616 | tf_op jit(solution)/shard_map/ppermute | solution.py:482
  18.4 5.9 %collective-permute-start.4 = (bf16[256,128]{1,0:T(8,128)(2,1)S(1)}, bf16[256,128]{1,0:T(8,128)(2,1)S(1)}, u32[]{:S(2)}, u32[]{:S(2)}) collective-permute-start(bf16[256,128]{1,0:T(8,128)(2,1)S(1)} %get-tuple-element.47), channel_id=1, source_target_pairs={{0,8},{4,12},{8,0},{12,4},{16,24},{20,28},{24,16},{28,20},{1,9},{5... | collective-permute-start | bytes 196616 | tf_op jit(solution)/shard_map/ppermute | solution.py:482
  19.9 4.8 %collective-permute-start.5 = (bf16[256,128]{1,0:T(8,128)(2,1)S(1)}, bf16[256,128]{1,0:T(8,128)(2,1)S(1)}, u32[]{:S(2)}, u32[]{:S(2)}) collective-permute-start(bf16[256,128]{1,0:T(8,128)(2,1)S(1)} %get-tuple-element.48), channel_id=1, source_target_pairs={{0,12},{4,8},{8,4},{12,0},{16,28},{20,24},{24,20},{28,16},{1,13},{... | collective-permute-start | bytes 196616 | tf_op jit(solution)/shard_map/ppermute | solution.py:482
  20.2 4.4 %collective-permute-start.6 = (bf16[256,128]{1,0:T(8,128)(2,1)S(1)}, bf16[256,128]{1,0:T(8,128)(2,1)S(1)}, u32[]{:S(2)}, u32[]{:S(2)}) collective-permute-start(bf16[256,128]{1,0:T(8,128)(2,1)S(1)} %get-tuple-element.49), channel_id=1, source_target_pairs={{0,16},{4,20},{8,24},{12,28},{16,0},{20,4},{24,8},{28,12},{1,17},{... | collective-permute-start | bytes 196616 | tf_op jit(solution)/shard_map/ppermute | solution.py:482
  21.7 4.1 %collective-permute-start.7 = (bf16[256,128]{1,0:T(8,128)(2,1)S(1)}, bf16[256,128]{1,0:T(8,128)(2,1)S(1)}, u32[]{:S(2)}, u32[]{:S(2)}) collective-permute-start(bf16[256,128]{1,0:T(8,128)(2,1)S(1)} %get-tuple-element.50), channel_id=1, source_target_pairs={{0,20},{4,16},{8,28},{12,24},{16,4},{20,0},{24,12},{28,8},{1,21},{... | collective-permute-start | bytes 196616 | tf_op jit(solution)/shard_map/ppermute | solution.py:482
  21.9 5.4 %collective-permute-start.8 = (bf16[256,128]{1,0:T(8,128)(2,1)S(1)}, bf16[256,128]{1,0:T(8,128)(2,1)S(1)}, u32[]{:S(2)}, u32[]{:S(2)}) collective-permute-start(bf16[256,128]{1,0:T(8,128)(2,1)S(1)} %get-tuple-element.51), channel_id=1, source_target_pairs={{0,24},{4,28},{8,16},{12,20},{16,8},{20,12},{24,0},{28,4},{1,25},{... | collective-permute-start | bytes 196616 | tf_op jit(solution)/shard_map/ppermute | solution.py:482
  24.3 5.0 %collective-permute-start.9 = (bf16[256,128]{1,0:T(8,128)(2,1)S(1)}, bf16[256,128]{1,0:T(8,128)(2,1)S(1)}, u32[]{:S(2)}, u32[]{:S(2)}) collective-permute-start(bf16[256,128]{1,0:T(8,128)(2,1)S(1)} %get-tuple-element.52), channel_id=1, source_target_pairs={{0,28},{4,24},{8,20},{12,16},{16,12},{20,8},{24,4},{28,0},{1,29},{... | collective-permute-start | bytes 196616 | tf_op jit(solution)/shard_map/ppermute | solution.py:482
  35.2 15.3 %collective-permute-start.13 = (bf16[512,128]{1,0:T(8,128)(2,1)S(1)}, bf16[512,128]{1,0:T(8,128)(2,1)S(1)}, u32[]{:S(2)}, u32[]{:S(2)}) collective-permute-start(bf16[512,128]{1,0:T(8,128)(2,1)S(1)} %get-tuple-element.59), channel_id=1, source_target_pairs={{0,1},{1,0},{2,3},{3,2},{4,5},{5,4},{6,7},{7,6},{8,9},{9,8},{10,11... | collective-permute-start | bytes 393224 | tf_op jit(solution)/shard_map/ppermute | solution.py:482
  37.3 13.3 %collective-permute-start.14 = (bf16[512,128]{1,0:T(8,128)(2,1)S(1)}, bf16[512,128]{1,0:T(8,128)(2,1)S(1)}, u32[]{:S(2)}, u32[]{:S(2)}) collective-permute-start(bf16[512,128]{1,0:T(8,128)(2,1)S(1)} %get-tuple-element.60), channel_id=1, source_target_pairs={{0,2},{1,3},{2,0},{3,1},{4,6},{5,7},{6,4},{7,5},{8,10},{9,11},{10,... | collective-permute-start | bytes 393224 | tf_op jit(solution)/shard_map/ppermute | solution.py:482
  39.7 11.0 %collective-permute-start.15 = (bf16[512,128]{1,0:T(8,128)(2,1)S(1)}, bf16[512,128]{1,0:T(8,128)(2,1)S(1)}, u32[]{:S(2)}, u32[]{:S(2)}) collective-permute-start(bf16[512,128]{1,0:T(8,128)(2,1)S(1)} %get-tuple-element.61), channel_id=1, source_target_pairs={{0,3},{1,2},{2,1},{3,0},{4,7},{5,6},{6,5},{7,4},{8,11},{9,10},{10,... | collective-permute-start | bytes 393224 | tf_op jit(solution)/shard_map/ppermute | solution.py:482
  39.7 11.6 %copy-start.1 = (bf16[512,512]{1,0:T(8,128)(2,1)S(1)}, bf16[512,512]{1,0:T(8,128)(2,1)}, u32[]{:S(2)}) copy-start(bf16[512,512]{1,0:T(8,128)(2,1)} %refs_11_.1) | copy-start | bytes 1572868
  39.7 11.6 %copy-start.2 = (bf16[1024,512]{1,0:T(8,128)(2,1)S(1)}, bf16[1024,512]{1,0:T(8,128)(2,1)}, u32[]{:S(2)}) copy-start(bf16[1024,512]{1,0:T(8,128)(2,1)} %refs_7_.3) | copy-start | bytes 3145732
  39.7 11.6 %copy-start.3 = (bf16[512,512]{1,0:T(8,128)(2,1)S(1)}, bf16[512,512]{1,0:T(8,128)(2,1)}, u32[]{:S(2)}) copy-start(bf16[512,512]{1,0:T(8,128)(2,1)} %refs_6_.3) | copy-start | bytes 1572868
  46.2 8.4 %collective-permute-start.10 = (bf16[512,128]{1,0:T(8,128)(2,1)}, bf16[512,128]{1,0:T(8,128)(2,1)}, u32[]{:S(2)}, u32[]{:S(2)}) collective-permute-start(bf16[512,128]{1,0:T(8,128)(2,1)} %get-tuple-element.55), channel_id=1, source_target_pairs={{0,1},{1,0},{2,3},{3,2},{4,5},{5,4},{6,7},{7,6},{8,9},{9,8},{10,11... | collective-permute-start | bytes 393224 | tf_op jit(solution)/shard_map/ppermute | solution.py:482
  47.3 14.2 %collective-permute-start.11 = (bf16[512,128]{1,0:T(8,128)(2,1)}, bf16[512,128]{1,0:T(8,128)(2,1)}, u32[]{:S(2)}, u32[]{:S(2)}) collective-permute-start(bf16[512,128]{1,0:T(8,128)(2,1)} %get-tuple-element.56), channel_id=1, source_target_pairs={{0,2},{1,3},{2,0},{3,1},{4,6},{5,7},{6,4},{7,5},{8,10},{9,11},{10,... | collective-permute-start | bytes 393224 | tf_op jit(solution)/shard_map/ppermute | solution.py:482
  50.5 11.0 %collective-permute-start.12 = (bf16[512,128]{1,0:T(8,128)(2,1)}, bf16[512,128]{1,0:T(8,128)(2,1)}, u32[]{:S(2)}, u32[]{:S(2)}) collective-permute-start(bf16[512,128]{1,0:T(8,128)(2,1)} %get-tuple-element.57), channel_id=1, source_target_pairs={{0,3},{1,2},{2,1},{3,0},{4,7},{5,6},{6,5},{7,4},{8,11},{9,10},{10,... | collective-permute-start | bytes 393224 | tf_op jit(solution)/shard_map/ppermute | solution.py:482
  68.8 2.7 %collective-permute-start.16 = (f32[512,512]{1,0:T(8,128)S(1)}, f32[512,512]{1,0:T(8,128)S(1)}, u32[]{:S(2)}, u32[]{:S(2)}) collective-permute-start(f32[512,512]{1,0:T(8,128)S(1)} %get-tuple-element.67), channel_id=1, source_target_pairs={{0,4},{4,0},{8,12},{12,8},{16,20},{20,16},{24,28},{28,24},{1,5},{5... | collective-permute-start | bytes 3145736 | tf_op jit(solution)/shard_map/ppermute | solution.py:482
  71.6 12.2 %collective-permute-start.17 = (f32[128,512]{1,0:T(8,128)S(1)}, f32[128,512]{1,0:T(8,128)S(1)}, u32[]{:S(2)}, u32[]{:S(2)}) collective-permute-start(f32[128,512]{1,0:T(8,128)S(1)} %get-tuple-element.69), channel_id=1, source_target_pairs={{0,8},{4,12},{8,0},{12,4},{16,24},{20,28},{24,16},{28,20},{1,9},{5... | collective-permute-start | bytes 786440 | tf_op jit(solution)/shard_map/ppermute | solution.py:482
  72.4 13.7 %collective-permute-start.18 = (f32[128,512]{1,0:T(8,128)S(1)}, f32[128,512]{1,0:T(8,128)S(1)}, u32[]{:S(2)}, u32[]{:S(2)}) collective-permute-start(f32[128,512]{1,0:T(8,128)S(1)} %get-tuple-element.70), channel_id=1, source_target_pairs={{0,16},{4,20},{8,24},{12,28},{16,0},{20,4},{24,8},{28,12},{1,17},{... | collective-permute-start | bytes 786440 | tf_op jit(solution)/shard_map/ppermute | solution.py:482
  74.1 15.3 %collective-permute-start.19 = (f32[128,512]{1,0:T(8,128)S(1)}, f32[128,512]{1,0:T(8,128)S(1)}, u32[]{:S(2)}, u32[]{:S(2)}) collective-permute-start(f32[128,512]{1,0:T(8,128)S(1)} %get-tuple-element.71), channel_id=1, source_target_pairs={{0,24},{4,28},{8,16},{12,20},{16,8},{20,12},{24,0},{28,4},{1,25},{... | collective-permute-start | bytes 786440 | tf_op jit(solution)/shard_map/ppermute | solution.py:482
  75.2 6.6 %collective-permute-start.36 = (bf16[512,128]{1,0:T(8,128)(2,1)S(1)}, bf16[512,128]{1,0:T(8,128)(2,1)S(1)}, u32[]{:S(2)}, u32[]{:S(2)}) collective-permute-start(bf16[512,128]{1,0:T(8,128)(2,1)S(1)} %get-tuple-element.83), channel_id=1, source_target_pairs={{0,1},{1,0},{2,3},{3,2},{4,5},{5,4},{6,7},{7,6},{8,9},{9,8},{10,11... | collective-permute-start | bytes 393224 | tf_op jit(solution)/shard_map/ppermute | solution.py:482
  77.5 13.4 %collective-permute-start.37 = (bf16[512,128]{1,0:T(8,128)(2,1)S(1)}, bf16[512,128]{1,0:T(8,128)(2,1)S(1)}, u32[]{:S(2)}, u32[]{:S(2)}) collective-permute-start(bf16[512,128]{1,0:T(8,128)(2,1)S(1)} %get-tuple-element.84), channel_id=1, source_target_pairs={{0,2},{1,3},{2,0},{3,1},{4,6},{5,7},{6,4},{7,5},{8,10},{9,11},{10,... | collective-permute-start | bytes 393224 | tf_op jit(solution)/shard_map/ppermute | solution.py:482
  81.8 11.7 %collective-permute-start.38 = (bf16[512,128]{1,0:T(8,128)(2,1)S(1)}, bf16[512,128]{1,0:T(8,128)(2,1)S(1)}, u32[]{:S(2)}, u32[]{:S(2)}) collective-permute-start(bf16[512,128]{1,0:T(8,128)(2,1)S(1)} %get-tuple-element.85), channel_id=1, source_target_pairs={{0,3},{1,2},{2,1},{3,0},{4,7},{5,6},{6,5},{7,4},{8,11},{9,10},{10,... | collective-permute-start | bytes 393224 | tf_op jit(solution)/shard_map/ppermute | solution.py:482
  83.8 18.3 %collective-permute-start.33 = (bf16[512,128]{1,0:T(8,128)(2,1)S(1)}, bf16[512,128]{1,0:T(8,128)(2,1)S(1)}, u32[]{:S(2)}, u32[]{:S(2)}) collective-permute-start(bf16[512,128]{1,0:T(8,128)(2,1)S(1)} %get-tuple-element.79), channel_id=1, source_target_pairs={{0,1},{1,0},{2,3},{3,2},{4,5},{5,4},{6,7},{7,6},{8,9},{9,8},{10,11... | collective-permute-start | bytes 393224 | tf_op jit(solution)/shard_map/ppermute | solution.py:482
  86.1 18.8 %collective-permute-start.34 = (bf16[512,128]{1,0:T(8,128)(2,1)S(1)}, bf16[512,128]{1,0:T(8,128)(2,1)S(1)}, u32[]{:S(2)}, u32[]{:S(2)}) collective-permute-start(bf16[512,128]{1,0:T(8,128)(2,1)S(1)} %get-tuple-element.80), channel_id=1, source_target_pairs={{0,2},{1,3},{2,0},{3,1},{4,6},{5,7},{6,4},{7,5},{8,10},{9,11},{10,... | collective-permute-start | bytes 393224 | tf_op jit(solution)/shard_map/ppermute | solution.py:482
  89.5 22.0 %collective-permute-start.35 = (bf16[512,128]{1,0:T(8,128)(2,1)S(1)}, bf16[512,128]{1,0:T(8,128)(2,1)S(1)}, u32[]{:S(2)}, u32[]{:S(2)}) collective-permute-start(bf16[512,128]{1,0:T(8,128)(2,1)S(1)} %get-tuple-element.81), channel_id=1, source_target_pairs={{0,3},{1,2},{2,1},{3,0},{4,7},{5,6},{6,5},{7,4},{8,11},{9,10},{10,... | collective-permute-start | bytes 393224 | tf_op jit(solution)/shard_map/ppermute | solution.py:482
  91.0 34.9 %collective-permute-start.22 = (bf16[128,512]{1,0:T(8,128)(2,1)S(1)}, bf16[128,512]{1,0:T(8,128)(2,1)S(1)}, u32[]{:S(2)}, u32[]{:S(2)}) collective-permute-start(bf16[128,512]{1,0:T(8,128)(2,1)S(1)} %add_convert_fusion), channel_id=1, source_target_pairs={{0,3},{1,2},{2,1},{3,0},{4,7},{5,6},{6,5},{7,4},{8,11},{9,10},{10,... | collective-permute-start | bytes 393224 | tf_op jit(solution)/shard_map/ppermute | solution.py:482
  93.5 33.8 %collective-permute-start.21 = (bf16[128,512]{1,0:T(8,128)(2,1)S(1)}, bf16[128,512]{1,0:T(8,128)(2,1)S(1)}, u32[]{:S(2)}, u32[]{:S(2)}) collective-permute-start(bf16[128,512]{1,0:T(8,128)(2,1)S(1)} %add_convert_fusion), channel_id=1, source_target_pairs={{0,2},{1,3},{2,0},{3,1},{4,6},{5,7},{6,4},{7,5},{8,10},{9,11},{10,... | collective-permute-start | bytes 393224 | tf_op jit(solution)/shard_map/ppermute | solution.py:482
  102.1 25.2 %collective-permute-start.20 = (bf16[128,512]{1,0:T(8,128)(2,1)S(1)}, bf16[128,512]{1,0:T(8,128)(2,1)S(1)}, u32[]{:S(2)}, u32[]{:S(2)}) collective-permute-start(bf16[128,512]{1,0:T(8,128)(2,1)S(1)} %add_convert_fusion), channel_id=1, source_target_pairs={{0,1},{1,0},{2,3},{3,2},{4,5},{5,4},{6,7},{7,6},{8,9},{9,8},{10,11... | collective-permute-start | bytes 393224 | tf_op jit(solution)/shard_map/ppermute | solution.py:482
  104.9 25.9 %collective-permute-start.30 = (bf16[1024,128]{1,0:T(8,128)(2,1)}, bf16[1024,128]{1,0:T(8,128)(2,1)S(1)}, u32[]{:S(2)}, u32[]{:S(2)}) collective-permute-start(bf16[1024,128]{1,0:T(8,128)(2,1)} %get-tuple-element.75), channel_id=1, source_target_pairs={{0,1},{1,0},{2,3},{3,2},{4,5},{5,4},{6,7},{7,6},{8,9},{9,8},{10,11... | collective-permute-start | bytes 786440 | tf_op jit(solution)/shard_map/ppermute | solution.py:482
  111.5 19.5 %collective-permute-start.31 = (bf16[1024,128]{1,0:T(8,128)(2,1)}, bf16[1024,128]{1,0:T(8,128)(2,1)S(1)}, u32[]{:S(2)}, u32[]{:S(2)}) collective-permute-start(bf16[1024,128]{1,0:T(8,128)(2,1)} %get-tuple-element.76), channel_id=1, source_target_pairs={{0,2},{1,3},{2,0},{3,1},{4,6},{5,7},{6,4},{7,5},{8,10},{9,11},{10,... | collective-permute-start | bytes 786440 | tf_op jit(solution)/shard_map/ppermute | solution.py:482
  122.3 18.4 %all-to-all-start.1 = ((bf16[8,256,128]{2,1,0:T(8,128)(2,1)}), bf16[8,256,128]{2,1,0:T(8,128)(2,1)S(1)}, u32[]{:S(2)}, u32[]{:S(2)}) async-start(bf16[8,256,128]{2,1,0:T(8,128)(2,1)} %get-tuple-element.87), calls=%async_computation.1 | async-start | bytes 1048576 | tf_op jit(solution)/shard_map/all_to_all | solution.py:562
  125.8 14.9 %collective-permute-start.32 = (bf16[1024,128]{1,0:T(8,128)(2,1)}, bf16[1024,128]{1,0:T(8,128)(2,1)S(1)}, u32[]{:S(2)}, u32[]{:S(2)}) collective-permute-start(bf16[1024,128]{1,0:T(8,128)(2,1)} %get-tuple-element.77), channel_id=1, source_target_pairs={{0,3},{1,2},{2,1},{3,0},{4,7},{5,6},{6,5},{7,4},{8,11},{9,10},{10,... | collective-permute-start | bytes 786440 | tf_op jit(solution)/shard_map/ppermute | solution.py:482
  127.4 11.4 %collective-permute-start.25 = (bf16[128,512]{1,0:T(8,128)(2,1)S(1)}, bf16[128,512]{1,0:T(8,128)(2,1)S(1)}, u32[]{:S(2)}, u32[]{:S(2)}) collective-permute-start(bf16[128,512]{1,0:T(8,128)(2,1)S(1)} %multiply_convert_fusion.refs_0_), channel_id=1, source_target_pairs={{0,24},{4,28},{8,16},{12,20},{16,8},{20,12},{24,0},{28,4},{1,25},{... | collective-permute-start | bytes 393224 | tf_op jit(solution)/shard_map/ppermute | solution.py:482
  130.3 9.9 %collective-permute-start.24 = (bf16[128,512]{1,0:T(8,128)(2,1)S(1)}, bf16[128,512]{1,0:T(8,128)(2,1)S(1)}, u32[]{:S(2)}, u32[]{:S(2)}) collective-permute-start(bf16[128,512]{1,0:T(8,128)(2,1)S(1)} %multiply_convert_fusion.refs_0_), channel_id=1, source_target_pairs={{0,16},{4,20},{8,24},{12,28},{16,0},{20,4},{24,8},{28,12},{1,17},{... | collective-permute-start | bytes 393224 | tf_op jit(solution)/shard_map/ppermute | solution.py:482
  130.8 9.4 %collective-permute-start.23 = (bf16[128,512]{1,0:T(8,128)(2,1)S(1)}, bf16[128,512]{1,0:T(8,128)(2,1)S(1)}, u32[]{:S(2)}, u32[]{:S(2)}) collective-permute-start(bf16[128,512]{1,0:T(8,128)(2,1)S(1)} %multiply_convert_fusion.refs_0_), channel_id=1, source_target_pairs={{0,8},{4,12},{8,0},{12,4},{16,24},{20,28},{24,16},{28,20},{1,9},{5... | collective-permute-start | bytes 393224 | tf_op jit(solution)/shard_map/ppermute | solution.py:482
  131.0 13.4 %collective-permute-start.26 = (bf16[128,512]{1,0:T(8,128)(2,1)S(1)}, bf16[128,512]{1,0:T(8,128)(2,1)S(1)}, u32[]{:S(2)}, u32[]{:S(2)}) collective-permute-start(bf16[128,512]{1,0:T(8,128)(2,1)S(1)} %multiply_convert_fusion.refs_0_), channel_id=1, source_target_pairs={{0,4},{4,0},{8,12},{12,8},{16,20},{20,16},{24,28},{28,24},{1,5},{5... | collective-permute-start | bytes 393224 | tf_op jit(solution)/shard_map/ppermute | solution.py:482
  138.8 5.6 %collective-permute-start.29 = (bf16[128,512]{1,0:T(8,128)(2,1)S(1)}, bf16[128,512]{1,0:T(8,128)(2,1)S(1)}, u32[]{:S(2)}, u32[]{:S(2)}) collective-permute-start(bf16[128,512]{1,0:T(8,128)(2,1)S(1)} %collective-permute-done.25.refs_3_), channel_id=1, source_target_pairs={{0,4},{4,0},{8,12},{12,8},{16,20},{20,16},{24,28},{28,24},{1,5},{5... | collective-permute-start | bytes 393224 | tf_op jit(solution)/shard_map/ppermute | solution.py:482
  140.2 4.3 %collective-permute-start.28 = (bf16[128,512]{1,0:T(8,128)(2,1)S(1)}, bf16[128,512]{1,0:T(8,128)(2,1)S(1)}, u32[]{:S(2)}, u32[]{:S(2)}) collective-permute-start(bf16[128,512]{1,0:T(8,128)(2,1)S(1)} %collective-permute-done.24.refs_2_), channel_id=1, source_target_pairs={{0,4},{4,0},{8,12},{12,8},{16,20},{20,16},{24,28},{28,24},{1,5},{5... | collective-permute-start | bytes 393224 | tf_op jit(solution)/shard_map/ppermute | solution.py:482
  140.2 4.3 %collective-permute-start.27 = (bf16[128,512]{1,0:T(8,128)(2,1)S(1)}, bf16[128,512]{1,0:T(8,128)(2,1)}, u32[]{:S(2)}, u32[]{:S(2)}) collective-permute-start(bf16[128,512]{1,0:T(8,128)(2,1)S(1)} %collective-permute-done.23.refs_1_), channel_id=1, source_target_pairs={{0,4},{4,0},{8,12},{12,8},{16,20},{20,16},{24,28},{28,24},{1,5},{5... | collective-permute-start | bytes 393224 | tf_op jit(solution)/shard_map/ppermute | solution.py:482
  (7 other events, 23.0 us)

commit v4 on v3

--- a/solution.py
+++ b/solution.py
@@ -97,9 +97,9 @@
     shapes = [(chunk_rows, width)] * parts + [(pool_rows, width)] * fresh
 
     def kernel(col_ref, colref_ref, *refs):
-        source_refs, adj_ref, outs = refs[:count], refs[count], refs[count + 1 : -3]
-        held, sems, adj_sems = refs[-3:]
-        pool = outs[parts] if fresh else source_refs[0]
+        source_refs, adj_ref, outs = refs[:count], refs[count], refs[count + 1 :]
+        held, sems, adj_sems = refs[-3 - fresh : len(refs) - fresh]
+        pool = refs[-1] if fresh else source_refs[0]
 
         def first(k):
             return (k ^ col_ref[0]) * per_part + chunk * per_chunk
@@ -121,6 +121,7 @@
                 fetch(t, k).start()
         for copy in copies:
             copy.wait()
+        passed = begin([pool], [outs[parts]], sems) if fresh else []
 
         @pl.loop(0, per_chunk)
         def _(t):
@@ -135,6 +136,9 @@
                 result = jnp.dot(left, right, preferred_element_type=F32)
                 outs[k][rows_at(t, tile), :] = result.astype(BF16)
 
+        for copy in passed:
+            copy.wait()
+
     return pl.pallas_call(
         kernel,
         out_shape=[jax.ShapeDtypeStruct(shape, BF16) for shape in shapes],
@@ -142,12 +146,13 @@
             num_scalar_prefetch=2,
             grid=(1,),
             in_specs=([ANY] * count if fresh else [full(sources[0].shape)]) + [ANY],
-            out_specs=[full(shape) for shape in shapes],
+            out_specs=[full((chunk_rows, width))] * parts + [ANY] * fresh,
             scratch_shapes=[
                 pltpu.VMEM((per_chunk, parts, per_block, tile, tile), BF16),
                 pltpu.SemaphoreType.DMA((count,)),
                 pltpu.SemaphoreType.DMA((per_chunk, parts)),
-            ],
+            ]
+            + [pltpu.VMEM((pool_rows, width), BF16)] * fresh,
         ),
         compiler_params=params(),
         name="aggregate",
@@ -236,30 +241,43 @@
     def kernel(col_ref, row_ref, *refs):
         f_ref, refs = refs[0], refs[1:]
         a_refs, refs = refs[: parts * CHUNKS], refs[parts * CHUNKS :]
-        g_refs, ws_ref = refs[:CHUNKS], refs[CHUNKS]
-        keep_ref, send_ref, *s_refs = refs[CHUNKS + 1 :]
+        g_refs, ws_ref, refs = refs[:CHUNKS], refs[CHUNKS], refs[CHUNKS + 1 :]
+        keep_ref, send_ref, s_refs = refs[0], refs[1], refs[2 : 2 + parts]
+        agg, spread, sems, out_sems = refs[2 + parts :]
+        targets = [
+            agg.at[k, h * chunk_rows : (h + 1) * chunk_rows]
+            for h in range(CHUNKS)
+            for k in range(parts)
+        ]
+        copies = begin(a_refs, targets, sems)
         g = jnp.concatenate([r[...] for r in g_refs], axis=0)
         ws = permuted(ws_ref, col_ref, parts, width)
         s = lax.dot_general(g, ws, NT, preferred_element_type=F32).astype(BF16)
-        for k, out in enumerate(s_refs):
-            out[...] = s[:, k * width : (k + 1) * width]
+        for k in range(parts):
+            spread[k] = s[:, k * width : (k + 1) * width]
+        writes = begin([spread.at[k] for k in range(parts)], s_refs, out_sems)
 
         def emit(self_ref, neigh_ref):
-            g = jnp.concatenate([r[...] for r in g_refs], axis=0)
             for k in range(parts):
                 self_ref[k * width : (k + 1) * width, :] = lax.dot_general(
                     f_ref[k], g, TN, preferred_element_type=F32
                 )
-                a = jnp.concatenate([a_refs[h * parts + k][...] for h in range(CHUNKS)], axis=0)
+            for copy in copies:
+                copy.wait()
+            for k in range(parts):
                 neigh_ref[rows_at(k ^ col_ref[0], width), :] = lax.dot_general(
-                    a, g, TN, preferred_element_type=F32
+                    agg[k], g, TN, preferred_element_type=F32
                 )
 
         even = row_ref[0] % 2 == 0
         pl.when(even)(lambda: emit(keep_ref, send_ref))
         pl.when(jnp.logical_not(even))(lambda: emit(send_ref, keep_ref))
-
-    args = [feat_rows, *[a for chunk in agg_chunks for a in chunk], *grads, w_self]
+        for write in writes:
+            write.wait()
+
+    flat = [a for chunk in agg_chunks for a in chunk]
+    chunk_rows = flat[0].shape[0]
+    args = [feat_rows, *flat, *grads, w_self]
     out_shape = [jax.ShapeDtypeStruct((parts * width, hidden), F32)] * 2 + [
         jax.ShapeDtypeStruct((rows, width), BF16)
     ] * parts
@@ -269,8 +287,16 @@
         grid_spec=pltpu.PrefetchScalarGridSpec(
             num_scalar_prefetch=2,
             grid=(1,),
-            in_specs=[full(a.shape) for a in args],
-            out_specs=[full(o.shape) for o in out_shape],
+            in_specs=[full(feat_rows.shape)]
+            + [ANY] * len(flat)
+            + [full(a.shape) for a in (*grads, w_self)],
+            out_specs=[full(o.shape) for o in out_shape[:2]] + [ANY] * parts,
+            scratch_shapes=[
+                pltpu.VMEM((parts, rows, width), BF16),
+                pltpu.VMEM((parts, rows, width), BF16),
+                pltpu.SemaphoreType.DMA((len(flat),)),
+                pltpu.SemaphoreType.DMA((parts,)),
+            ],
         ),
         compiler_params=params(),
         name="weights",

time: 148 us -> 148 us (level)
  no operation moved by 1% of the time
where the time goes in v4:
time: 148 us; the launch traced here: 147 us
  starting transfers between devices  64.1 us (43%)
  Pallas kernels  42.9 us (29%)
  waiting for transfers between devices  34.8 us (24%)
  local copies, waits for them, and re-layouts  4.27 us (3%)
    ppermute x39, starting transfers between devices, swap(): return lax.ppermute(x, axis, [(i, i ^ k) for i in range(n)])  54.1 us
    ppermute x39, waiting for transfers between devices, swap(): return lax.ppermute(x, axis, [(i, i ^ k) for i in range(n)])  34.8 us
    pallas_call x2, Pallas kernels, pull(): pl.pallas_call(kernel, out_shape=out_shape, grid_spec=pltpu.PrefetchScala...  14.4 us
    pallas_call x2, Pallas kernels, aggregate(): pl.pallas_call(kernel, out_shape=[jax.ShapeDtypeStruct(shape, BF16) for s...  11.7 us
    all_to_all x1, starting transfers between devices, body(): lax.all_to_all(feats.reshape(parts, node_rows // parts, width), 'cols', 0...  6.49 us
    pallas_call x2, Pallas kernels, dense(): pl.pallas_call(kernel, out_shape=[jax.ShapeDtypeStruct((chunk_rows * CHUN...  5.77 us
    unnamed x29, local copies, waits for them, and re-layouts  4.18 us
    all_to_all x1, starting transfers between devices, body(): returned = lax.all_to_all(remote[0], 'rows', 0, 0, tiled=True)  3.51 us
  transfers between devices with their start and end apart: 41, of which 13 were waited for; matrix products, arithmetic and copies ran while one was open for 1% of the time, Pallas kernels for 22%

profile of v4, /device:TPU:0, one launch (start us, length us, event | category | flops | bytes accessed | tf_op | source)
XLA Modules:
  0.0 147.2 jit_solution(1875915674764226203)
XLA Ops:
  0.7 6.5 %all-to-all-start = ((bf16[4,1024,128]{2,1,0:T(8,128)(2,1)}), bf16[4,1024,128]{2,1,0:T(8,128)(2,1)S(1)}, u32[]{:S(2)}, u32[]{:S(2)}) async-start(bf16[4,1024,128]{2,1,0:T(8,128)(2,1)} %bitcast.24), calls=%async_computation | async-start | bytes 2097152 | tf_op jit(solution)/shard_map/all_to_all | solution.py:536
  8.1 1.1 collective-permute-done.refs_1_
  9.2 1.6 %collective-permute-start.1 = (s32[2,128]{1,0:T(2,128)S(1)}, s32[2,128]{1,0:T(2,128)S(1)}, u32[]{:S(2)}, u32[]{:S(2)}) collective-permute-start(s32[2,128]{1,0:T(2,128)S(1)} %pad_add_fusion.1), channel_id=1, source_target_pairs={{0,8},{4,12},{8,0},{12,4},{16,24},{20,28},{24,16},{28,20},{1,9},{5... | collective-permute-start | bytes 3080 | tf_op jit(solution)/shard_map/ppermute | solution.py:508
  10.8 2.1 %collective-permute-done.1.refs_2_ = s32[2,128]{1,0:T(2,128)S(1)} collective-permute-done((s32[2,128]{1,0:T(2,128)S(1)}, s32[2,128]{1,0:T(2,128)S(1)}, u32[]{:S(2)}, u32[]{:S(2)}) %collective-permute-start.1) | collective-permute-done | bytes 1056 | tf_op jit(solution)/shard_map/ppermute | solution.py:508
  12.9 1.6 %collective-permute-start.2 = (s32[4,128]{1,0:T(4,128)S(1)}, s32[4,128]{1,0:T(4,128)S(1)}, u32[]{:S(2)}, u32[]{:S(2)}) collective-permute-start(s32[4,128]{1,0:T(4,128)S(1)} %pad_add_fusion), channel_id=1, source_target_pairs={{0,16},{4,20},{8,24},{12,28},{16,0},{20,4},{24,8},{28,12},{1,17},{... | collective-permute-start | bytes 6152 | tf_op jit(solution)/shard_map/ppermute | solution.py:508
  14.5 2.1 %collective-permute-done.2.refs_3_ = s32[4,128]{1,0:T(4,128)S(1)} collective-permute-done((s32[4,128]{1,0:T(4,128)S(1)}, s32[4,128]{1,0:T(4,128)S(1)}, u32[]{:S(2)}, u32[]{:S(2)}) %collective-permute-start.2) | collective-permute-done | bytes 2080 | tf_op jit(solution)/shard_map/ppermute | solution.py:508
  16.5 1.8 %select_tiles.1 = (bf16[256,128]{1,0:T(8,128)(2,1)S(1)}, bf16[256,128]{1,0:T(8,128)(2,1)S(1)}, bf16[256,128]{1,0:T(8,128)(2,1)S(1)}, bf16[256,128]{1,0:T(8,128)(...) custom-call(s32[1]{0:T(128)} %bitcast.3.row_ref, ...), custom_call_target="tpu_custom_call" | custom-call | tf_op jit(solution)/shard_map/select_tiles/pallas_call | solution.py:77
  18.4 1.5 %collective-permute-start.4 = (bf16[256,128]{1,0:T(8,128)(2,1)S(1)}, bf16[256,128]{1,0:T(8,128)(2,1)S(1)}, u32[]{:S(2)}, u32[]{:S(2)}) collective-permute-start(bf16[256,128]{1,0:T(8,128)(2,1)S(1)} %get-tuple-element.47), channel_id=1, source_target_pairs={{0,8},{4,12},{8,0},{12,4},{16,24},{20,28},{24,16},{28,20},{1,9},{5... | collective-permute-start | bytes 196616 | tf_op jit(solution)/shard_map/ppermute | solution.py:508
  20.2 1.4 collective-permute-start.6
  21.9 2.4 %collective-permute-start.8 = (bf16[256,128]{1,0:T(8,128)(2,1)S(1)}, bf16[256,128]{1,0:T(8,128)(2,1)S(1)}, u32[]{:S(2)}, u32[]{:S(2)}) collective-permute-start(bf16[256,128]{1,0:T(8,128)(2,1)S(1)} %get-tuple-element.51), channel_id=1, source_target_pairs={{0,24},{4,28},{8,16},{12,20},{16,8},{20,12},{24,0},{28,4},{1,25},{... | collective-permute-start | bytes 196616 | tf_op jit(solution)/shard_map/ppermute | solution.py:508
  24.7 1.1 collective-permute-done.7.refs_5_
  25.8 1.6 %collective-permute-done.8.refs_6_ = bf16[256,128]{1,0:T(8,128)(2,1)S(1)} collective-permute-done((bf16[256,128]{1,0:T(8,128)(2,1)S(1)}, bf16[256,128]{1,0:T(8,128)(2,1)S(1)}, u32[]{:S(2)}, u32[]{:S(2)}) %collective-permute-start.8) | collective-permute-done | bytes 65568 | tf_op jit(solution)/shard_map/ppermute | solution.py:508
  27.4 1.9 %collective-permute-done.9.refs_7_ = bf16[256,128]{1,0:T(8,128)(2,1)S(1)} collective-permute-done((bf16[256,128]{1,0:T(8,128)(2,1)S(1)}, bf16[256,128]{1,0:T(8,128)(2,1)S(1)}, u32[]{:S(2)}, u32[]{:S(2)}) %collective-permute-start.9) | collective-permute-done | bytes 65568 | tf_op jit(solution)/shard_map/ppermute | solution.py:508
  29.3 5.9 %aggregate.2 = (bf16[512,128]{1,0:T(8,128)(2,1)S(1)}, bf16[512,128]{1,0:T(8,128)(2,1)S(1)}, bf16[512,128]{1,0:T(8,128)(2,1)S(1)}, bf16[512,128]{1,0:T(8,128)(2,1)S(1)}, bf16[6144,128]{1,0:T(8,128)(2,1)S(1)}) custom-call(s32[1]{0:T(128)} %bitcast.col_ref, s32[16,32]{1,0:T(8,128)S(1)} %compare_select_fusion.colref_ref, bf16[4096,128]{1,0:T(8,128)(2,1)S(1)} %copy-done, ...), custom_call_target="tpu_custom_call" | custom-call | tf_op jit(solution)/shard_map/aggregate/pallas_call | solution.py:142
  35.2 2.1 %collective-permute-start.13 = (bf16[512,128]{1,0:T(8,128)(2,1)S(1)}, bf16[512,128]{1,0:T(8,128)(2,1)S(1)}, u32[]{:S(2)}, u32[]{:S(2)}) collective-permute-start(bf16[512,128]{1,0:T(8,128)(2,1)S(1)} %get-tuple-element.59), channel_id=1, source_target_pairs={{0,1},{1,0},{2,3},{3,2},{4,5},{5,4},{6,7},{7,6},{8,9},{9,8},{10,11... | collective-permute-start | bytes 393224 | tf_op jit(solution)/shard_map/ppermute | solution.py:508
  37.3 2.4 %collective-permute-start.14 = (bf16[512,128]{1,0:T(8,128)(2,1)S(1)}, bf16[512,128]{1,0:T(8,128)(2,1)S(1)}, u32[]{:S(2)}, u32[]{:S(2)}) collective-permute-start(bf16[512,128]{1,0:T(8,128)(2,1)S(1)} %get-tuple-element.60), channel_id=1, source_target_pairs={{0,2},{1,3},{2,0},{3,1},{4,6},{5,7},{6,4},{7,5},{8,10},{9,11},{10,... | collective-permute-start | bytes 393224 | tf_op jit(solution)/shard_map/ppermute | solution.py:508
  39.7 5.8 %aggregate.3 = (bf16[512,128]{1,0:T(8,128)(2,1)S(1)}, bf16[512,128]{1,0:T(8,128)(2,1)}, bf16[512,128]{1,0:T(8,128)(2,1)}, bf16[512,128]{1,0:T(8,128)(2,1)}) custom-call(s32[1]{0:T(128)} %bitcast.col_ref, s32[16,32]{1,0:T(8,128)S(1)} %compare_select_fusion.colref_ref, bf16[6144,128]{1,0:T(8,128)(2,1)S(1)} %get-tuple-element.53.refs_0_, ...), custom_call_target="tpu_custom_call" | custom-call | tf_op jit(solution)/shard_map/aggregate/pallas_call | solution.py:142
  46.2 1.1 collective-permute-start.10
  47.3 3.3 %collective-permute-start.11 = (bf16[512,128]{1,0:T(8,128)(2,1)}, bf16[512,128]{1,0:T(8,128)(2,1)}, u32[]{:S(2)}, u32[]{:S(2)}) collective-permute-start(bf16[512,128]{1,0:T(8,128)(2,1)} %get-tuple-element.56), channel_id=1, source_target_pairs={{0,2},{1,3},{2,0},{3,1},{4,6},{5,7},{6,4},{7,5},{8,10},{9,11},{10,... | collective-permute-start | bytes 393224 | tf_op jit(solution)/shard_map/ppermute | solution.py:508
  51.3 0.9 copy-done.5
  52.2 2.4 %dense.2 = (bf16[1024,512]{1,0:T(8,128)(2,1)}, bf16[512,512]{1,0:T(8,128)(2,1)S(1)}, bf16[512,128]{1,0:T(8,128)(2,1)S(1)}, bf16[512,128]{1,0:T(8,128)(2,1)S(1)},...) custom-call(s32[1]{0:T(128)} %bitcast.col_ref, bf16[4,1024,128]{2,1,0:T(8,128)(2,1)S(1)} %all-to-all-done.refs_0_, ...), custom_call_target="tpu_custom_call" | custom-call | tf_op jit(solution)/shard_map/dense/pallas_call | solution.py:214
  54.6 6.9 %collective-permute-done.11.refs_3_.refs_7_ = bf16[512,128]{1,0:T(8,128)(2,1)} collective-permute-done((bf16[512,128]{1,0:T(8,128)(2,1)}, bf16[512,128]{1,0:T(8,128)(2,1)}, u32[]{:S(2)}, u32[]{:S(2)}) %collective-permute-start.11) | collective-permute-done | bytes 131104 | tf_op jit(solution)/shard_map/ppermute | solution.py:508
  61.5 3.4 %dense.3 = (bf16[1024,512]{1,0:T(8,128)(2,1)}, bf16[512,512]{1,0:T(8,128)(2,1)S(1)}, bf16[512,128]{1,0:T(8,128)(2,1)S(1)}, bf16[512,128]{1,0:T(8,128)(2,1)S(1)},...) custom-call(s32[1]{0:T(128)} %bitcast.col_ref, ...), custom_call_target="tpu_custom_call", output_to_operand_aliasing={{0}: (9, {})} | custom-call | tf_op jit(solution)/shard_map/dense/pallas_call | solution.py:214
  64.9 3.5 %weights.1 = (f32[512,512]{1,0:T(8,128)S(1)}, f32[512,512]{1,0:T(8,128)S(1)}, bf16[1024,128]{1,0:T(8,128)(2,1)S(1)}, bf16[1024,128]{1,0:T(8,128)(2,1)}, bf16[102...) custom-call(s32[1]{0:T(128)} %bitcast.col_ref, s32[1]{0:T(128)} %bitcast.3.row_ref, ...), custom_call_target="tpu_custom_call" | custom-call | tf_op jit(solution)/shard_map/weights/pallas_call | solution.py:284
  68.4 2.6 %collective-permute-done.16.received_ref = f32[512,512]{1,0:T(8,128)S(1)} collective-permute-done((f32[512,512]{1,0:T(8,128)S(1)}, f32[512,512]{1,0:T(8,128)S(1)}, u32[]{:S(2)}, u32[]{:S(2)}) %collective-permute-start.16) | collective-permute-done | bytes 1048608 | tf_op jit(solution)/shard_map/ppermute | solution.py:508
  71.2 0.8 collective-permute-start.17
  72.0 1.7 %collective-permute-start.18 = (f32[128,512]{1,0:T(8,128)S(1)}, f32[128,512]{1,0:T(8,128)S(1)}, u32[]{:S(2)}, u32[]{:S(2)}) collective-permute-start(f32[128,512]{1,0:T(8,128)S(1)} %get-tuple-element.70), channel_id=1, source_target_pairs={{0,16},{4,20},{8,24},{12,28},{16,0},{20,4},{24,8},{28,12},{1,17},{... | collective-permute-start | bytes 786440 | tf_op jit(solution)/shard_map/ppermute | solution.py:508
  73.7 1.1 collective-permute-start.19
  74.8 2.3 %collective-permute-start.36 = (bf16[512,128]{1,0:T(8,128)(2,1)S(1)}, bf16[512,128]{1,0:T(8,128)(2,1)S(1)}, u32[]{:S(2)}, u32[]{:S(2)}) collective-permute-start(bf16[512,128]{1,0:T(8,128)(2,1)S(1)} %get-tuple-element.83), channel_id=1, source_target_pairs={{0,1},{1,0},{2,3},{3,2},{4,5},{5,4},{6,7},{7,6},{8,9},{9,8},{10,11... | collective-permute-start | bytes 393224 | tf_op jit(solution)/shard_map/ppermute | solution.py:508
  77.1 1.0 collective-permute-start.37
  78.1 3.3 %collective-permute-done.36.refs_1_ = bf16[512,128]{1,0:T(8,128)(2,1)S(1)} collective-permute-done((bf16[512,128]{1,0:T(8,128)(2,1)S(1)}, bf16[512,128]{1,0:T(8,128)(2,1)S(1)}, u32[]{:S(2)}, u32[]{:S(2)}) %collective-permute-start.36) | collective-permute-done | bytes 131104 | tf_op jit(solution)/shard_map/ppermute | solution.py:508
  81.4 2.1 %collective-permute-start.38 = (bf16[512,128]{1,0:T(8,128)(2,1)S(1)}, bf16[512,128]{1,0:T(8,128)(2,1)S(1)}, u32[]{:S(2)}, u32[]{:S(2)}) collective-permute-start(bf16[512,128]{1,0:T(8,128)(2,1)S(1)} %get-tuple-element.85), channel_id=1, source_target_pairs={{0,3},{1,2},{2,1},{3,0},{4,7},{5,6},{6,5},{7,4},{8,11},{9,10},{10,... | collective-permute-start | bytes 393224 | tf_op jit(solution)/shard_map/ppermute | solution.py:508
  83.4 1.6 %collective-permute-start.33 = (bf16[512,128]{1,0:T(8,128)(2,1)S(1)}, bf16[512,128]{1,0:T(8,128)(2,1)S(1)}, u32[]{:S(2)}, u32[]{:S(2)}) collective-permute-start(bf16[512,128]{1,0:T(8,128)(2,1)S(1)} %get-tuple-element.79), channel_id=1, source_target_pairs={{0,1},{1,0},{2,3},{3,2},{4,5},{5,4},{6,7},{7,6},{8,9},{9,8},{10,11... | collective-permute-start | bytes 393224 | tf_op jit(solution)/shard_map/ppermute | solution.py:508
  85.7 3.4 %collective-permute-start.34 = (bf16[512,128]{1,0:T(8,128)(2,1)S(1)}, bf16[512,128]{1,0:T(8,128)(2,1)S(1)}, u32[]{:S(2)}, u32[]{:S(2)}) collective-permute-start(bf16[512,128]{1,0:T(8,128)(2,1)S(1)} %get-tuple-element.80), channel_id=1, source_target_pairs={{0,2},{1,3},{2,0},{3,1},{4,6},{5,7},{6,4},{7,5},{8,10},{9,11},{10,... | collective-permute-start | bytes 393224 | tf_op jit(solution)/shard_map/ppermute | solution.py:508
  89.1 1.4 collective-permute-start.35
  90.6 2.5 %collective-permute-start.22 = (bf16[128,512]{1,0:T(8,128)(2,1)S(1)}, bf16[128,512]{1,0:T(8,128)(2,1)S(1)}, u32[]{:S(2)}, u32[]{:S(2)}) collective-permute-start(bf16[128,512]{1,0:T(8,128)(2,1)S(1)} %add_convert_fusion), channel_id=1, source_target_pairs={{0,3},{1,2},{2,1},{3,0},{4,7},{5,6},{6,5},{7,4},{8,11},{9,10},{10,... | collective-permute-start | bytes 393224 | tf_op jit(solution)/shard_map/ppermute | solution.py:508
  93.1 8.6 %collective-permute-start.21 = (bf16[128,512]{1,0:T(8,128)(2,1)S(1)}, bf16[128,512]{1,0:T(8,128)(2,1)S(1)}, u32[]{:S(2)}, u32[]{:S(2)}) collective-permute-start(bf16[128,512]{1,0:T(8,128)(2,1)S(1)} %add_convert_fusion), channel_id=1, source_target_pairs={{0,2},{1,3},{2,0},{3,1},{4,6},{5,7},{6,4},{7,5},{8,10},{9,11},{10,... | collective-permute-start | bytes 393224 | tf_op jit(solution)/shard_map/ppermute | solution.py:508
  102.2 2.2 %collective-permute-done.34.refs_2_ = bf16[512,128]{1,0:T(8,128)(2,1)S(1)} collective-permute-done((bf16[512,128]{1,0:T(8,128)(2,1)S(1)}, bf16[512,128]{1,0:T(8,128)(2,1)S(1)}, u32[]{:S(2)}, u32[]{:S(2)}) %collective-permute-start.34) | collective-permute-done | bytes 131104 | tf_op jit(solution)/shard_map/ppermute | solution.py:508
  104.5 6.6 %pull.2.refs_5_ = f32[48,128,128]{2,1,0:T(8,128)S(1)} custom-call(s32[1]{0:T(128)} %bitcast.col_ref, s32[1]{0:T(128)} %bitcast.3.row_ref, s32[16,32]{1,0:T(8,128)S(1)} %compare_select_fusion.colref_ref, bf16[512,128]{1,0:T(8,128)(2,1)S(1)} %get-tuple-element.82.refs_0_, bf16[512,128]{1,0:T(8,128)(2,1)S(1)} %collective-permute-done.36.refs_1_, ...), custom_call_target="tpu_custom_call" | custom-call | tf_op jit(solution)/shard_map/pull/pallas_call | solution.py:442
  111.1 3.0 %collective-permute-start.31 = (bf16[1024,128]{1,0:T(8,128)(2,1)}, bf16[1024,128]{1,0:T(8,128)(2,1)S(1)}, u32[]{:S(2)}, u32[]{:S(2)}) collective-permute-start(bf16[1024,128]{1,0:T(8,128)(2,1)} %get-tuple-element.76), channel_id=1, source_target_pairs={{0,2},{1,3},{2,0},{3,1},{4,6},{5,7},{6,4},{7,5},{8,10},{9,11},{10,... | collective-permute-start | bytes 786440 | tf_op jit(solution)/shard_map/ppermute | solution.py:508
  114.1 7.8 %pull.3 = (bf16[4096,128]{1,0:T(8,128)(2,1)S(1)}, bf16[8,256,128]{2,1,0:T(8,128)(2,1)}) custom-call(s32[1]{0:T(128)} %bitcast.col_ref, s32[1]{0:T(128)} %bitcast.3.row_ref, s32[16,32]{1,0:T(8,128)S(1)} %compare_select_fusion.colref_ref, bf16[512,128]{1,0:T(8,128)(2,1)S(1)} %get-tuple-element.78.refs_0_, ...), custom_call_target="tpu_custom_call" | custom-call | tf_op jit(solution)/shard_map/pull/pallas_call | solution.py:442
  121.9 3.5 %all-to-all-start.1 = ((bf16[8,256,128]{2,1,0:T(8,128)(2,1)}), bf16[8,256,128]{2,1,0:T(8,128)(2,1)S(1)}, u32[]{:S(2)}, u32[]{:S(2)}) async-start(bf16[8,256,128]{2,1,0:T(8,128)(2,1)} %get-tuple-element.87), calls=%async_computation.1 | async-start | bytes 1048576 | tf_op jit(solution)/shard_map/all_to_all | solution.py:588
  125.4 1.5 %collective-permute-start.32 = (bf16[1024,128]{1,0:T(8,128)(2,1)}, bf16[1024,128]{1,0:T(8,128)(2,1)S(1)}, u32[]{:S(2)}, u32[]{:S(2)}) collective-permute-start(bf16[1024,128]{1,0:T(8,128)(2,1)} %get-tuple-element.77), channel_id=1, source_target_pairs={{0,3},{1,2},{2,1},{3,0},{4,7},{5,6},{6,5},{7,4},{8,11},{9,10},{10,... | collective-permute-start | bytes 786440 | tf_op jit(solution)/shard_map/ppermute | solution.py:508
  127.0 2.8 %collective-permute-start.25 = (bf16[128,512]{1,0:T(8,128)(2,1)S(1)}, bf16[128,512]{1,0:T(8,128)(2,1)S(1)}, u32[]{:S(2)}, u32[]{:S(2)}) collective-permute-start(bf16[128,512]{1,0:T(8,128)(2,1)S(1)} %multiply_convert_fusion.refs_0_), channel_id=1, source_target_pairs={{0,24},{4,28},{8,16},{12,20},{16,8},{20,12},{24,0},{28,4},{1,25},{... | collective-permute-start | bytes 393224 | tf_op jit(solution)/shard_map/ppermute | solution.py:508
  130.6 7.9 %collective-permute-done.25.refs_3_ = bf16[128,512]{1,0:T(8,128)(2,1)S(1)} collective-permute-done((bf16[128,512]{1,0:T(8,128)(2,1)S(1)}, bf16[128,512]{1,0:T(8,128)(2,1)S(1)}, u32[]{:S(2)}, u32[]{:S(2)}) %collective-permute-start.25) | collective-permute-done | bytes 131104 | tf_op jit(solution)/shard_map/ppermute | solution.py:508
  138.4 1.3 collective-permute-done.24.refs_2_
  141.5 2.5 %finish.1 = f32[4096,128]{1,0:T(8,128)} custom-call(s32[1]{0:T(128)} %bitcast.col_ref, s32[1]{0:T(128)} %bitcast.3.row_ref, s32[1,128]{1,0:T(1,128)S(1)} %copy-done.10, s32[1,128]{1,0:T(1,128)S(1)} %copy-done.12, s32[2,128]{1,0:T(2,128)S(1)} %collective-permute-done.1.refs_2_, s32[4,128]{1,0:T(4,128)S(1)} %collective-permute-done.2.refs_3_, ...), custom_call_target="tpu_custom_call" | custom-call | tf_op jit(solution)/shard_map/finish/pallas_call | solution.py:487
  144.1 3.1 %widen.1 = (f32[512,512]{1,0:T(8,128)}, f32[512,512]{1,0:T(8,128)}) custom-call(s32[1]{0:T(128)} %bitcast.3.row_ref, bf16[128,512]{1,0:T(8,128)(2,1)S(1)} %multiply_convert_fusion.refs_0_, bf16[128,512]{1,0:T(8,128)(2,1)S(1)} %collective-permute-done.23.refs_1_, bf16[128,512]{1,0:T(8,128)(2,1)S(1)} %collective-permute-done.24.refs_2_, ...), custom_call_target="tpu_custom_call" | custom-call | tf_op jit(solution)/shard_map/widen/pallas_call | solution.py:354
  (81 shorter events, 7.4 us)
Async XLA Ops:
  0.6 28.7 %copy-start = (bf16[4096,128]{1,0:T(8,128)(2,1)S(1)}, bf16[4096,128]{1,0:T(8,128)(2,1)}, u32[]{:S(2)}) copy-start(bf16[4096,128]{1,0:T(8,128)(2,1)} %refs_0_.1) | copy-start | bytes 3145732
  0.6 24.0 %copy-start.13 = (s32[32,16]{0,1:T(8,128)S(1)}, s32[32,16]{0,1:T(8,128)}, u32[]{:S(2)}) copy-start(s32[32,16]{0,1:T(8,128)} %param.9) | copy-start | bytes 6148
  0.7 50.6 %all-to-all-start = ((bf16[4,1024,128]{2,1,0:T(8,128)(2,1)}), bf16[4,1024,128]{2,1,0:T(8,128)(2,1)S(1)}, u32[]{:S(2)}, u32[]{:S(2)}) async-start(bf16[4,1024,128]{2,1,0:T(8,128)(2,1)} %bitcast.24), calls=%async_computation | async-start | bytes 2097152 | tf_op jit(solution)/shard_map/all_to_all | solution.py:536
  8.0 13.7 %copy-start.9 = (s32[1,128]{1,0:T(1,128)}, s32[1,128]{1,0:T(1,128)S(1)}, u32[]{:S(2)}) copy-start(s32[1,128]{1,0:T(1,128)S(1)} %pad.4.refs_0_) | copy-start | bytes 1540
  8.0 1.2 collective-permute-start
  9.2 12.5 %copy-start.11 = (s32[1,128]{1,0:T(1,128)}, s32[1,128]{1,0:T(1,128)S(1)}, u32[]{:S(2)}) copy-start(s32[1,128]{1,0:T(1,128)S(1)} %collective-permute-done.refs_1_) | copy-start | bytes 1540
  9.2 3.6 %collective-permute-start.1 = (s32[2,128]{1,0:T(2,128)S(1)}, s32[2,128]{1,0:T(2,128)S(1)}, u32[]{:S(2)}, u32[]{:S(2)}) collective-permute-start(s32[2,128]{1,0:T(2,128)S(1)} %pad_add_fusion.1), channel_id=1, source_target_pairs={{0,8},{4,12},{8,0},{12,4},{16,24},{20,28},{24,16},{28,20},{1,9},{5... | collective-permute-start | bytes 3080 | tf_op jit(solution)/shard_map/ppermute | solution.py:508
  12.9 3.6 %collective-permute-start.2 = (s32[4,128]{1,0:T(4,128)S(1)}, s32[4,128]{1,0:T(4,128)S(1)}, u32[]{:S(2)}, u32[]{:S(2)}) collective-permute-start(s32[4,128]{1,0:T(4,128)S(1)} %pad_add_fusion), channel_id=1, source_target_pairs={{0,16},{4,20},{8,24},{12,28},{16,0},{20,4},{24,8},{28,12},{1,17},{... | collective-permute-start | bytes 6152 | tf_op jit(solution)/shard_map/ppermute | solution.py:508
  18.3 3.6 %collective-permute-start.3 = (bf16[256,128]{1,0:T(8,128)(2,1)S(1)}, bf16[256,128]{1,0:T(8,128)(2,1)S(1)}, u32[]{:S(2)}, u32[]{:S(2)}) collective-permute-start(bf16[256,128]{1,0:T(8,128)(2,1)S(1)} %get-tuple-element.46), channel_id=1, source_target_pairs={{0,4},{4,0},{8,12},{12,8},{16,20},{20,16},{24,28},{28,24},{1,5},{5... | collective-permute-start | bytes 196616 | tf_op jit(solution)/shard_map/ppermute | solution.py:508
  18.4 5.9 %collective-permute-start.4 = (bf16[256,128]{1,0:T(8,128)(2,1)S(1)}, bf16[256,128]{1,0:T(8,128)(2,1)S(1)}, u32[]{:S(2)}, u32[]{:S(2)}) collective-permute-start(bf16[256,128]{1,0:T(8,128)(2,1)S(1)} %get-tuple-element.47), channel_id=1, source_target_pairs={{0,8},{4,12},{8,0},{12,4},{16,24},{20,28},{24,16},{28,20},{1,9},{5... | collective-permute-start | bytes 196616 | tf_op jit(solution)/shard_map/ppermute | solution.py:508
  19.9 4.8 %collective-permute-start.5 = (bf16[256,128]{1,0:T(8,128)(2,1)S(1)}, bf16[256,128]{1,0:T(8,128)(2,1)S(1)}, u32[]{:S(2)}, u32[]{:S(2)}) collective-permute-start(bf16[256,128]{1,0:T(8,128)(2,1)S(1)} %get-tuple-element.48), channel_id=1, source_target_pairs={{0,12},{4,8},{8,4},{12,0},{16,28},{20,24},{24,20},{28,16},{1,13},{... | collective-permute-start | bytes 196616 | tf_op jit(solution)/shard_map/ppermute | solution.py:508
  20.2 4.4 %collective-permute-start.6 = (bf16[256,128]{1,0:T(8,128)(2,1)S(1)}, bf16[256,128]{1,0:T(8,128)(2,1)S(1)}, u32[]{:S(2)}, u32[]{:S(2)}) collective-permute-start(bf16[256,128]{1,0:T(8,128)(2,1)S(1)} %get-tuple-element.49), channel_id=1, source_target_pairs={{0,16},{4,20},{8,24},{12,28},{16,0},{20,4},{24,8},{28,12},{1,17},{... | collective-permute-start | bytes 196616 | tf_op jit(solution)/shard_map/ppermute | solution.py:508
  21.7 4.1 %collective-permute-start.7 = (bf16[256,128]{1,0:T(8,128)(2,1)S(1)}, bf16[256,128]{1,0:T(8,128)(2,1)S(1)}, u32[]{:S(2)}, u32[]{:S(2)}) collective-permute-start(bf16[256,128]{1,0:T(8,128)(2,1)S(1)} %get-tuple-element.50), channel_id=1, source_target_pairs={{0,20},{4,16},{8,28},{12,24},{16,4},{20,0},{24,12},{28,8},{1,21},{... | collective-permute-start | bytes 196616 | tf_op jit(solution)/shard_map/ppermute | solution.py:508
  21.9 5.4 %collective-permute-start.8 = (bf16[256,128]{1,0:T(8,128)(2,1)S(1)}, bf16[256,128]{1,0:T(8,128)(2,1)S(1)}, u32[]{:S(2)}, u32[]{:S(2)}) collective-permute-start(bf16[256,128]{1,0:T(8,128)(2,1)S(1)} %get-tuple-element.51), channel_id=1, source_target_pairs={{0,24},{4,28},{8,16},{12,20},{16,8},{20,12},{24,0},{28,4},{1,25},{... | collective-permute-start | bytes 196616 | tf_op jit(solution)/shard_map/ppermute | solution.py:508
  24.3 5.0 %collective-permute-start.9 = (bf16[256,128]{1,0:T(8,128)(2,1)S(1)}, bf16[256,128]{1,0:T(8,128)(2,1)S(1)}, u32[]{:S(2)}, u32[]{:S(2)}) collective-permute-start(bf16[256,128]{1,0:T(8,128)(2,1)S(1)} %get-tuple-element.52), channel_id=1, source_target_pairs={{0,28},{4,24},{8,20},{12,16},{16,12},{20,8},{24,4},{28,0},{1,29},{... | collective-permute-start | bytes 196616 | tf_op jit(solution)/shard_map/ppermute | solution.py:508
  35.2 15.3 %collective-permute-start.13 = (bf16[512,128]{1,0:T(8,128)(2,1)S(1)}, bf16[512,128]{1,0:T(8,128)(2,1)S(1)}, u32[]{:S(2)}, u32[]{:S(2)}) collective-permute-start(bf16[512,128]{1,0:T(8,128)(2,1)S(1)} %get-tuple-element.59), channel_id=1, source_target_pairs={{0,1},{1,0},{2,3},{3,2},{4,5},{5,4},{6,7},{7,6},{8,9},{9,8},{10,11... | collective-permute-start | bytes 393224 | tf_op jit(solution)/shard_map/ppermute | solution.py:508
  37.3 13.3 %collective-permute-start.14 = (bf16[512,128]{1,0:T(8,128)(2,1)S(1)}, bf16[512,128]{1,0:T(8,128)(2,1)S(1)}, u32[]{:S(2)}, u32[]{:S(2)}) collective-permute-start(bf16[512,128]{1,0:T(8,128)(2,1)S(1)} %get-tuple-element.60), channel_id=1, source_target_pairs={{0,2},{1,3},{2,0},{3,1},{4,6},{5,7},{6,4},{7,5},{8,10},{9,11},{10,... | collective-permute-start | bytes 393224 | tf_op jit(solution)/shard_map/ppermute | solution.py:508
  39.6 11.0 %collective-permute-start.15 = (bf16[512,128]{1,0:T(8,128)(2,1)S(1)}, bf16[512,128]{1,0:T(8,128)(2,1)S(1)}, u32[]{:S(2)}, u32[]{:S(2)}) collective-permute-start(bf16[512,128]{1,0:T(8,128)(2,1)S(1)} %get-tuple-element.61), channel_id=1, source_target_pairs={{0,3},{1,2},{2,1},{3,0},{4,7},{5,6},{6,5},{7,4},{8,11},{9,10},{10,... | collective-permute-start | bytes 393224 | tf_op jit(solution)/shard_map/ppermute | solution.py:508
  39.7 11.6 %copy-start.1 = (bf16[512,512]{1,0:T(8,128)(2,1)S(1)}, bf16[512,512]{1,0:T(8,128)(2,1)}, u32[]{:S(2)}) copy-start(bf16[512,512]{1,0:T(8,128)(2,1)} %refs_11_.1) | copy-start | bytes 1572868
  39.7 11.6 %copy-start.2 = (bf16[1024,512]{1,0:T(8,128)(2,1)S(1)}, bf16[1024,512]{1,0:T(8,128)(2,1)}, u32[]{:S(2)}) copy-start(bf16[1024,512]{1,0:T(8,128)(2,1)} %refs_7_.3) | copy-start | bytes 3145732
  39.7 11.6 %copy-start.3 = (bf16[512,512]{1,0:T(8,128)(2,1)S(1)}, bf16[512,512]{1,0:T(8,128)(2,1)}, u32[]{:S(2)}) copy-start(bf16[512,512]{1,0:T(8,128)(2,1)} %refs_6_.3) | copy-start | bytes 1572868
  46.2 8.4 %collective-permute-start.10 = (bf16[512,128]{1,0:T(8,128)(2,1)}, bf16[512,128]{1,0:T(8,128)(2,1)}, u32[]{:S(2)}, u32[]{:S(2)}) collective-permute-start(bf16[512,128]{1,0:T(8,128)(2,1)} %get-tuple-element.55), channel_id=1, source_target_pairs={{0,1},{1,0},{2,3},{3,2},{4,5},{5,4},{6,7},{7,6},{8,9},{9,8},{10,11... | collective-permute-start | bytes 393224 | tf_op jit(solution)/shard_map/ppermute | solution.py:508
  47.3 14.2 %collective-permute-start.11 = (bf16[512,128]{1,0:T(8,128)(2,1)}, bf16[512,128]{1,0:T(8,128)(2,1)}, u32[]{:S(2)}, u32[]{:S(2)}) collective-permute-start(bf16[512,128]{1,0:T(8,128)(2,1)} %get-tuple-element.56), channel_id=1, source_target_pairs={{0,2},{1,3},{2,0},{3,1},{4,6},{5,7},{6,4},{7,5},{8,10},{9,11},{10,... | collective-permute-start | bytes 393224 | tf_op jit(solution)/shard_map/ppermute | solution.py:508
  50.5 11.0 %collective-permute-start.12 = (bf16[512,128]{1,0:T(8,128)(2,1)}, bf16[512,128]{1,0:T(8,128)(2,1)}, u32[]{:S(2)}, u32[]{:S(2)}) collective-permute-start(bf16[512,128]{1,0:T(8,128)(2,1)} %get-tuple-element.57), channel_id=1, source_target_pairs={{0,3},{1,2},{2,1},{3,0},{4,7},{5,6},{6,5},{7,4},{8,11},{9,10},{10,... | collective-permute-start | bytes 393224 | tf_op jit(solution)/shard_map/ppermute | solution.py:508
  68.3 2.7 %collective-permute-start.16 = (f32[512,512]{1,0:T(8,128)S(1)}, f32[512,512]{1,0:T(8,128)S(1)}, u32[]{:S(2)}, u32[]{:S(2)}) collective-permute-start(f32[512,512]{1,0:T(8,128)S(1)} %get-tuple-element.67), channel_id=1, source_target_pairs={{0,4},{4,0},{8,12},{12,8},{16,20},{20,16},{24,28},{28,24},{1,5},{5... | collective-permute-start | bytes 3145736 | tf_op jit(solution)/shard_map/ppermute | solution.py:508
  71.2 12.2 %collective-permute-start.17 = (f32[128,512]{1,0:T(8,128)S(1)}, f32[128,512]{1,0:T(8,128)S(1)}, u32[]{:S(2)}, u32[]{:S(2)}) collective-permute-start(f32[128,512]{1,0:T(8,128)S(1)} %get-tuple-element.69), channel_id=1, source_target_pairs={{0,8},{4,12},{8,0},{12,4},{16,24},{20,28},{24,16},{28,20},{1,9},{5... | collective-permute-start | bytes 786440 | tf_op jit(solution)/shard_map/ppermute | solution.py:508
  72.0 13.7 %collective-permute-start.18 = (f32[128,512]{1,0:T(8,128)S(1)}, f32[128,512]{1,0:T(8,128)S(1)}, u32[]{:S(2)}, u32[]{:S(2)}) collective-permute-start(f32[128,512]{1,0:T(8,128)S(1)} %get-tuple-element.70), channel_id=1, source_target_pairs={{0,16},{4,20},{8,24},{12,28},{16,0},{20,4},{24,8},{28,12},{1,17},{... | collective-permute-start | bytes 786440 | tf_op jit(solution)/shard_map/ppermute | solution.py:508
  73.7 15.4 %collective-permute-start.19 = (f32[128,512]{1,0:T(8,128)S(1)}, f32[128,512]{1,0:T(8,128)S(1)}, u32[]{:S(2)}, u32[]{:S(2)}) collective-permute-start(f32[128,512]{1,0:T(8,128)S(1)} %get-tuple-element.71), channel_id=1, source_target_pairs={{0,24},{4,28},{8,16},{12,20},{16,8},{20,12},{24,0},{28,4},{1,25},{... | collective-permute-start | bytes 786440 | tf_op jit(solution)/shard_map/ppermute | solution.py:508
  74.8 6.6 %collective-permute-start.36 = (bf16[512,128]{1,0:T(8,128)(2,1)S(1)}, bf16[512,128]{1,0:T(8,128)(2,1)S(1)}, u32[]{:S(2)}, u32[]{:S(2)}) collective-permute-start(bf16[512,128]{1,0:T(8,128)(2,1)S(1)} %get-tuple-element.83), channel_id=1, source_target_pairs={{0,1},{1,0},{2,3},{3,2},{4,5},{5,4},{6,7},{7,6},{8,9},{9,8},{10,11... | collective-permute-start | bytes 393224 | tf_op jit(solution)/shard_map/ppermute | solution.py:508
  77.1 13.4 %collective-permute-start.37 = (bf16[512,128]{1,0:T(8,128)(2,1)S(1)}, bf16[512,128]{1,0:T(8,128)(2,1)S(1)}, u32[]{:S(2)}, u32[]{:S(2)}) collective-permute-start(bf16[512,128]{1,0:T(8,128)(2,1)S(1)} %get-tuple-element.84), channel_id=1, source_target_pairs={{0,2},{1,3},{2,0},{3,1},{4,6},{5,7},{6,4},{7,5},{8,10},{9,11},{10,... | collective-permute-start | bytes 393224 | tf_op jit(solution)/shard_map/ppermute | solution.py:508
  81.4 11.7 %collective-permute-start.38 = (bf16[512,128]{1,0:T(8,128)(2,1)S(1)}, bf16[512,128]{1,0:T(8,128)(2,1)S(1)}, u32[]{:S(2)}, u32[]{:S(2)}) collective-permute-start(bf16[512,128]{1,0:T(8,128)(2,1)S(1)} %get-tuple-element.85), channel_id=1, source_target_pairs={{0,3},{1,2},{2,1},{3,0},{4,7},{5,6},{6,5},{7,4},{8,11},{9,10},{10,... | collective-permute-start | bytes 393224 | tf_op jit(solution)/shard_map/ppermute | solution.py:508
  83.4 18.3 %collective-permute-start.33 = (bf16[512,128]{1,0:T(8,128)(2,1)S(1)}, bf16[512,128]{1,0:T(8,128)(2,1)S(1)}, u32[]{:S(2)}, u32[]{:S(2)}) collective-permute-start(bf16[512,128]{1,0:T(8,128)(2,1)S(1)} %get-tuple-element.79), channel_id=1, source_target_pairs={{0,1},{1,0},{2,3},{3,2},{4,5},{5,4},{6,7},{7,6},{8,9},{9,8},{10,11... | collective-permute-start | bytes 393224 | tf_op jit(solution)/shard_map/ppermute | solution.py:508
  85.7 18.8 %collective-permute-start.34 = (bf16[512,128]{1,0:T(8,128)(2,1)S(1)}, bf16[512,128]{1,0:T(8,128)(2,1)S(1)}, u32[]{:S(2)}, u32[]{:S(2)}) collective-permute-start(bf16[512,128]{1,0:T(8,128)(2,1)S(1)} %get-tuple-element.80), channel_id=1, source_target_pairs={{0,2},{1,3},{2,0},{3,1},{4,6},{5,7},{6,4},{7,5},{8,10},{9,11},{10,... | collective-permute-start | bytes 393224 | tf_op jit(solution)/shard_map/ppermute | solution.py:508
  89.1 22.0 %collective-permute-start.35 = (bf16[512,128]{1,0:T(8,128)(2,1)S(1)}, bf16[512,128]{1,0:T(8,128)(2,1)S(1)}, u32[]{:S(2)}, u32[]{:S(2)}) collective-permute-start(bf16[512,128]{1,0:T(8,128)(2,1)S(1)} %get-tuple-element.81), channel_id=1, source_target_pairs={{0,3},{1,2},{2,1},{3,0},{4,7},{5,6},{6,5},{7,4},{8,11},{9,10},{10,... | collective-permute-start | bytes 393224 | tf_op jit(solution)/shard_map/ppermute | solution.py:508
  90.6 34.9 %collective-permute-start.22 = (bf16[128,512]{1,0:T(8,128)(2,1)S(1)}, bf16[128,512]{1,0:T(8,128)(2,1)S(1)}, u32[]{:S(2)}, u32[]{:S(2)}) collective-permute-start(bf16[128,512]{1,0:T(8,128)(2,1)S(1)} %add_convert_fusion), channel_id=1, source_target_pairs={{0,3},{1,2},{2,1},{3,0},{4,7},{5,6},{6,5},{7,4},{8,11},{9,10},{10,... | collective-permute-start | bytes 393224 | tf_op jit(solution)/shard_map/ppermute | solution.py:508
  93.1 33.8 %collective-permute-start.21 = (bf16[128,512]{1,0:T(8,128)(2,1)S(1)}, bf16[128,512]{1,0:T(8,128)(2,1)S(1)}, u32[]{:S(2)}, u32[]{:S(2)}) collective-permute-start(bf16[128,512]{1,0:T(8,128)(2,1)S(1)} %add_convert_fusion), channel_id=1, source_target_pairs={{0,2},{1,3},{2,0},{3,1},{4,6},{5,7},{6,4},{7,5},{8,10},{9,11},{10,... | collective-permute-start | bytes 393224 | tf_op jit(solution)/shard_map/ppermute | solution.py:508
  101.7 25.2 %collective-permute-start.20 = (bf16[128,512]{1,0:T(8,128)(2,1)S(1)}, bf16[128,512]{1,0:T(8,128)(2,1)S(1)}, u32[]{:S(2)}, u32[]{:S(2)}) collective-permute-start(bf16[128,512]{1,0:T(8,128)(2,1)S(1)} %add_convert_fusion), channel_id=1, source_target_pairs={{0,1},{1,0},{2,3},{3,2},{4,5},{5,4},{6,7},{7,6},{8,9},{9,8},{10,11... | collective-permute-start | bytes 393224 | tf_op jit(solution)/shard_map/ppermute | solution.py:508
  104.5 25.9 %collective-permute-start.30 = (bf16[1024,128]{1,0:T(8,128)(2,1)}, bf16[1024,128]{1,0:T(8,128)(2,1)S(1)}, u32[]{:S(2)}, u32[]{:S(2)}) collective-permute-start(bf16[1024,128]{1,0:T(8,128)(2,1)} %get-tuple-element.75), channel_id=1, source_target_pairs={{0,1},{1,0},{2,3},{3,2},{4,5},{5,4},{6,7},{7,6},{8,9},{9,8},{10,11... | collective-permute-start | bytes 786440 | tf_op jit(solution)/shard_map/ppermute | solution.py:508
  111.1 19.5 %collective-permute-start.31 = (bf16[1024,128]{1,0:T(8,128)(2,1)}, bf16[1024,128]{1,0:T(8,128)(2,1)S(1)}, u32[]{:S(2)}, u32[]{:S(2)}) collective-permute-start(bf16[1024,128]{1,0:T(8,128)(2,1)} %get-tuple-element.76), channel_id=1, source_target_pairs={{0,2},{1,3},{2,0},{3,1},{4,6},{5,7},{6,4},{7,5},{8,10},{9,11},{10,... | collective-permute-start | bytes 786440 | tf_op jit(solution)/shard_map/ppermute | solution.py:508
  121.9 18.4 %all-to-all-start.1 = ((bf16[8,256,128]{2,1,0:T(8,128)(2,1)}), bf16[8,256,128]{2,1,0:T(8,128)(2,1)S(1)}, u32[]{:S(2)}, u32[]{:S(2)}) async-start(bf16[8,256,128]{2,1,0:T(8,128)(2,1)} %get-tuple-element.87), calls=%async_computation.1 | async-start | bytes 1048576 | tf_op jit(solution)/shard_map/all_to_all | solution.py:588
  125.4 14.9 %collective-permute-start.32 = (bf16[1024,128]{1,0:T(8,128)(2,1)}, bf16[1024,128]{1,0:T(8,128)(2,1)S(1)}, u32[]{:S(2)}, u32[]{:S(2)}) collective-permute-start(bf16[1024,128]{1,0:T(8,128)(2,1)} %get-tuple-element.77), channel_id=1, source_target_pairs={{0,3},{1,2},{2,1},{3,0},{4,7},{5,6},{6,5},{7,4},{8,11},{9,10},{10,... | collective-permute-start | bytes 786440 | tf_op jit(solution)/shard_map/ppermute | solution.py:508
  127.0 11.4 %collective-permute-start.25 = (bf16[128,512]{1,0:T(8,128)(2,1)S(1)}, bf16[128,512]{1,0:T(8,128)(2,1)S(1)}, u32[]{:S(2)}, u32[]{:S(2)}) collective-permute-start(bf16[128,512]{1,0:T(8,128)(2,1)S(1)} %multiply_convert_fusion.refs_0_), channel_id=1, source_target_pairs={{0,24},{4,28},{8,16},{12,20},{16,8},{20,12},{24,0},{28,4},{1,25},{... | collective-permute-start | bytes 393224 | tf_op jit(solution)/shard_map/ppermute | solution.py:508
  129.9 9.9 %collective-permute-start.24 = (bf16[128,512]{1,0:T(8,128)(2,1)S(1)}, bf16[128,512]{1,0:T(8,128)(2,1)S(1)}, u32[]{:S(2)}, u32[]{:S(2)}) collective-permute-start(bf16[128,512]{1,0:T(8,128)(2,1)S(1)} %multiply_convert_fusion.refs_0_), channel_id=1, source_target_pairs={{0,16},{4,20},{8,24},{12,28},{16,0},{20,4},{24,8},{28,12},{1,17},{... | collective-permute-start | bytes 393224 | tf_op jit(solution)/shard_map/ppermute | solution.py:508
  130.4 9.4 %collective-permute-start.23 = (bf16[128,512]{1,0:T(8,128)(2,1)S(1)}, bf16[128,512]{1,0:T(8,128)(2,1)S(1)}, u32[]{:S(2)}, u32[]{:S(2)}) collective-permute-start(bf16[128,512]{1,0:T(8,128)(2,1)S(1)} %multiply_convert_fusion.refs_0_), channel_id=1, source_target_pairs={{0,8},{4,12},{8,0},{12,4},{16,24},{20,28},{24,16},{28,20},{1,9},{5... | collective-permute-start | bytes 393224 | tf_op jit(solution)/shard_map/ppermute | solution.py:508
  130.6 13.5 %collective-permute-start.26 = (bf16[128,512]{1,0:T(8,128)(2,1)S(1)}, bf16[128,512]{1,0:T(8,128)(2,1)S(1)}, u32[]{:S(2)}, u32[]{:S(2)}) collective-permute-start(bf16[128,512]{1,0:T(8,128)(2,1)S(1)} %multiply_convert_fusion.refs_0_), channel_id=1, source_target_pairs={{0,4},{4,0},{8,12},{12,8},{16,20},{20,16},{24,28},{28,24},{1,5},{5... | collective-permute-start | bytes 393224 | tf_op jit(solution)/shard_map/ppermute | solution.py:508
  138.4 5.6 %collective-permute-start.29 = (bf16[128,512]{1,0:T(8,128)(2,1)S(1)}, bf16[128,512]{1,0:T(8,128)(2,1)S(1)}, u32[]{:S(2)}, u32[]{:S(2)}) collective-permute-start(bf16[128,512]{1,0:T(8,128)(2,1)S(1)} %collective-permute-done.25.refs_3_), channel_id=1, source_target_pairs={{0,4},{4,0},{8,12},{12,8},{16,20},{20,16},{24,28},{28,24},{1,5},{5... | collective-permute-start | bytes 393224 | tf_op jit(solution)/shard_map/ppermute | solution.py:508
  139.8 4.3 %collective-permute-start.28 = (bf16[128,512]{1,0:T(8,128)(2,1)S(1)}, bf16[128,512]{1,0:T(8,128)(2,1)S(1)}, u32[]{:S(2)}, u32[]{:S(2)}) collective-permute-start(bf16[128,512]{1,0:T(8,128)(2,1)S(1)} %collective-permute-done.24.refs_2_), channel_id=1, source_target_pairs={{0,4},{4,0},{8,12},{12,8},{16,20},{20,16},{24,28},{28,24},{1,5},{5... | collective-permute-start | bytes 393224 | tf_op jit(solution)/shard_map/ppermute | solution.py:508
  139.8 4.3 %collective-permute-start.27 = (bf16[128,512]{1,0:T(8,128)(2,1)S(1)}, bf16[128,512]{1,0:T(8,128)(2,1)}, u32[]{:S(2)}, u32[]{:S(2)}) collective-permute-start(bf16[128,512]{1,0:T(8,128)(2,1)S(1)} %collective-permute-done.23.refs_1_), channel_id=1, source_target_pairs={{0,4},{4,0},{8,12},{12,8},{16,20},{20,16},{24,28},{28,24},{1,5},{5... | collective-permute-start | bytes 393224 | tf_op jit(solution)/shard_map/ppermute | solution.py:508
  (7 other events, 23.0 us)
